TPU v7x, 32 devices: a whole 2x2x4 slice. The times are simulated.
32 devices in a mesh: gx: 16 (over z, y, core), gy: 2 (over x).
Axes of the slice: x: 2, y: 2, z: 4, core: 2. Of those that a mesh axis runs over, the one named last changes fastest.
Arguments:
- loads: float32 [8, 2, 16384], P(None, 'gy', 'gx'), may hold values from -6 to 6
- dual_op: bfloat16 [2, 16384, 1024], P('gy', 'gx')
- iface: int32 [2, 16, 1024], P('gy', 'gx'), may hold values from 0 to 1023, each once within a row
- precond: float32 [2, 16384], P('gy', 'gx'), may hold values from 0.3 to 3
- corner_map: float32 [2, 128, 16384], P('gy', None, 'gx'), may hold values from -0.25 to 0.25
- coarse_inv: float32 [128, 128], replicated
- elem_stiff: float32 [8, 8], replicated
- elem_dofs: int32 [8, 1024, 256], P(None, 'gx', 'gy'), may hold values from 0 to 1023
- density: float32 [1024, 256], P('gx', 'gy'), may hold values from 0.1 to 1
- passive: int32 [1024, 256], P('gx', 'gy'), may hold values 0 or 1
Outputs:
- adjoint: float32 [8, 2, 16384], P(None, 'gy', 'gx')
- sens: float32 [1024, 256], P('gx', 'gy')
All inputs are finite; a program needn't handle non-finite values. No bound on the sum of `passive` on one device may be relied on, other than what follows from the above.
Results may differ from a plain program's by a relative error of at most 0.00052.
Values sent between devices are 32-bit elements; how exact they have to be, the bound alone decides.
No kernel may reach another device: no remote copies, remote signals or barrier semaphores. Data moves between devices by JAX's collectives and lax.ppermute only.
A program may use at most 128 MiB of HBM per device.

v0:
```python
import jax
import jax.numpy as jnp
from jax import lax
from jax.sharding import PartitionSpec as P

R = 128
ITERS = 2
SWEEPS = 3


coupling = 0.3
radius_sq = 2.0
penalty = 3.0


def padded_2(array, sides, width):
    for axis, dim in sides:
        size, length = (lax.axis_size(axis), array.shape[dim])
        up = [(i, (i + 1) % size) for i in range(size - 1)]
        down = [(j, i) for i, j in up]
        last = lax.slice_in_dim(array, length - width, length, axis=dim)
        leading = lax.slice_in_dim(array, 0, width, axis=dim)
        before = lax.ppermute(last, axis, up)
        after = lax.ppermute(leading, axis, down)
        array = jnp.concatenate([before, array, after], axis=dim)
    return array


def local_part(vec, op_local, left_idx, right_idx):
    local = jnp.einsum(
        "ck,mk->cm", vec.astype(jnp.bfloat16), op_local, preferred_element_type=jnp.float32
    )
    width = left_idx.shape[0]
    outgoing = jnp.concatenate([vec[:, left_idx], vec[:, right_idx]], axis=1)
    extended = padded_2(outgoing, (("gx", 1),), width)
    local = local.at[:, left_idx].add(-coupling * extended[:, :width])
    local = local.at[:, right_idx].add(-coupling * extended[:, 3 * width :])
    return local


def apply_dual(vec, op_local, left_idx, right_idx, corners, coarse_inv):
    hi = lax.Precision.HIGHEST
    local = local_part(vec, op_local, left_idx, right_idx)
    csum = lax.psum(jnp.dot(vec, corners.T, precision=hi), ("gx", "gy"))
    coarse_vals = jnp.dot(csum, coarse_inv.T, precision=hi)
    return local + jnp.dot(coarse_vals, corners, precision=hi)


def inner(first, second):
    return jnp.sum(first * second, axis=1)[:, None]


def residual_products(resid, zvec):
    return lax.psum(inner(resid, zvec), ("gx", "gy"))


def on_device(
    loads, dual_op, iface, precond, corner_map, coarse_inv, elem_stiff, elem_dofs, density, passive
):
    hi = lax.Precision.HIGHEST
    op_local = dual_op[0]
    width = R
    left_idx = iface[0, 0, :width]
    right_idx = iface[0, 0, width : 2 * width]
    corners = corner_map[0]
    scaling = precond[0][None, :]
    resid = loads[:, 0, :]
    adjoint = jnp.zeros_like(resid)
    zvec = scaling * resid
    direction = zvec
    rz_now = residual_products(resid, zvec)
    for step in range(ITERS):
        image = apply_dual(direction, op_local, left_idx, right_idx, corners, coarse_inv)
        alpha = rz_now / lax.psum(inner(direction, image), ("gx", "gy"))
        adjoint = adjoint + alpha * direction
        resid = resid - alpha * image
        if step + 1 < ITERS:
            zvec = scaling * resid
            rz_next = residual_products(resid, zvec)
            direction = zvec + rz_next / rz_now * direction
            rz_now = rz_next
    nodal = adjoint[:, elem_dofs]
    pushed = jnp.einsum("ab,cbxy->caxy", elem_stiff, nodal, precision=hi)
    energy = jnp.sum(nodal * pushed, axis=(0, 1))
    grad = jnp.where(passive == 1, 0.0, -penalty * density * density * energy)
    diag = 1.0 + 4.0 * radius_sq
    smooth = grad / diag
    for sweep in range(SWEEPS - 1):
        padded = padded_2(smooth, (("gx", 0), ("gy", 1)), 1)
        beside = padded[2:, 1:-1] + padded[:-2, 1:-1] + padded[1:-1, 2:] + padded[1:-1, :-2]
        smooth = (grad + radius_sq * beside) / diag
    return (adjoint[:, None, :], smooth)


def solution(mesh):
    placed = (
        P(None, "gy", "gx"),
        P("gy", "gx", None),
        P("gy", "gx", None),
        P("gy", "gx"),
        P("gy", None, "gx"),
        P(),
        P(),
        P(None, "gx", "gy"),
        P("gx", "gy"),
        P("gx", "gy"),
    )
    return jax.shard_map(
        on_device,
        mesh=mesh,
        in_specs=placed,
        out_specs=(P(None, "gy", "gx"), P("gx", "gy")),
        check_vma=False,
    )
```

profile of v0, /device:TPU:1, one launch (start us, length us, event | category | flops | bytes accessed | tf_op | source)
XLA Modules:
  0.0 516.3 jit_solution(12681567802003912632)
XLA Ops:
  2.5 1.7 bitcast_multiply_fusion.2
  4.2 2.3 gather_fusion
  6.5 4.5 collective-permute-start
  11.0 2.3 gather_fusion.1
  13.3 1.9 collective-permute-start.1
  16.5 39.7 %psum.43 = f32[8,128]{1,0:T(8,128)S(1)} all-reduce(f32[8,128]{1,0:T(8,128)S(1)} %fusion.22), channel_id=1, replica_groups=mesh['gx'=16,'gy'=2] {'gx','gy'}, use_global_device_ids=true, to_apply=%region_2.0 | all-reduce | flops 1024 | bytes 8192 | tf_op jit(solution)/shard_map/psum | solution.py:44
  57.8 1.8 scatter_custom_fusion
  59.6 1.8 scatter_custom_fusion.1
  61.6 41.0 %all-reduce = (f32[8,1]{0,1:T(1,128)S(1)}, f32[8,1]{0,1:T(1,128)S(1)}) all-reduce(f32[8,1]{0,1:T(1,128)S(1)} %bitcast.112, f32[8,1]{0,1:T(1,128)S(1)} %bitcast.111), channel_id=1, replica_groups=mesh['gx'=16,'gy'=2] {'gx','gy'}, use_global_device_ids=true, to_apply=%region_1.0 | all-reduce | flops 16 | bytes 128 | tf_op jit(solution)/shard_map/psum | solution.py:54
  102.8 39.1 %psum.45 = f32[8,1]{0,1:T(1,128)S(1)} all-reduce(f32[8,1]{0,1:T(1,128)S(1)} %bitcast.113), channel_id=1, replica_groups=mesh['gx'=16,'gy'=2] {'gx','gy'}, use_global_device_ids=true, to_apply=%region_8.0 | all-reduce | flops 8 | bytes 64 | tf_op jit(solution)/shard_map/psum | solution.py:54
  143.3 2.2 fusion.18
  147.9 41.0 %psum.46 = f32[8,128]{1,0:T(8,128)S(1)} all-reduce(f32[8,128]{1,0:T(8,128)S(1)} %fusion.18), channel_id=1, replica_groups=mesh['gx'=16,'gy'=2] {'gx','gy'}, use_global_device_ids=true, to_apply=%region_9.0 | all-reduce | flops 1024 | bytes 8192 | tf_op jit(solution)/shard_map/psum | solution.py:44
  189.1 1.5 fusion.16
  190.5 5.3 %collective-permute-start.2 = (f32[8,128]{0,1:T(8,128)}, f32[8,128]{0,1:T(8,128)}, u32[]{:S(2)}, u32[]{:S(2)}) collective-permute-start(f32[8,128]{0,1:T(8,128)} %bitcast.116), channel_id=1, source_target_pairs={{0,2},{2,4},{4,6},{6,8},{8,10},{10,12},{12,14},{14,16},{16,18},{18... | collective-permute-start | bytes 12296 | tf_op jit(solution)/shard_map/ppermute | solution.py:23
  195.8 1.9 collective-permute-start.3
  199.4 3.3 scatter_custom_fusion.2
  202.7 3.1 scatter_custom_fusion.3
  207.0 37.8 %psum.47 = f32[8,1]{0,1:T(1,128)S(1)} all-reduce(f32[8,1]{0,1:T(1,128)S(1)} %bitcast.114), channel_id=1, replica_groups=mesh['gx'=16,'gy'=2] {'gx','gy'}, use_global_device_ids=true, to_apply=%region_13.0 | all-reduce | flops 8 | bytes 64 | tf_op jit(solution)/shard_map/psum | solution.py:74
  244.8 1.2 multiply_add_fusion.1
  246.1 215.5 %gather_fusion.4 = f32[65536,8]{1,0:T(8,128)} fusion(f32[8,1024]{0,1:T(8,128)S(1)} %multiply_add_fusion.1, s32[65536]{0:T(1024)S(1)} %broadcast_clamp_fusion), kind=kCustom, calls=%fused_computation.4 | custom fusion | bytes 4456448 | tf_op jit(solution)/shard_map/gather | solution.py:82
  461.6 18.7 %copy.20 = f32[8,64,128,8]{2,0,1,3:T(8,128)} copy(f32[8,64,128,8]{3,2,1,0:T(8,128)} %bitcast.103) | data formatting | bytes 4194304 | tf_op jit(solution)/shard_map/gather | solution.py:82
  480.2 4.2 fusion
  484.5 5.3 %collective-permute-start.5 = (f32[1,128]{1,0:T(1,128)S(1)}, f32[1,128]{1,0:T(1,128)S(1)}, u32[]{:S(2)}, u32[]{:S(2)}) collective-permute-start(f32[1,128]{1,0:T(1,128)S(1)} %get-tuple-element.20), channel_id=1, source_target_pairs={{0,2},{2,4},{4,6},{6,8},{8,10},{10,12},{12,14},{14,16},{16,18},{18... | collective-permute-start | bytes 1544 | tf_op jit(solution)/shard_map/ppermute | solution.py:23
  489.8 1.9 collective-permute-start.4
  491.8 2.9 collective-permute-done.4
  494.8 1.3 collective-permute-start.6
  496.1 4.0 collective-permute-start.7
  501.2 3.1 collective-permute-start.9
  504.3 1.9 collective-permute-start.8
  506.3 2.9 collective-permute-done.8
  509.3 1.3 collective-permute-start.10
  510.6 4.0 collective-permute-start.11
  (72 shorter events, 15.0 us)
Async XLA Ops:
  0.6 56.3 %copy-start = (bf16[1,1024,1024]{2,1,0:T(8,128)(2,1)S(1)}, bf16[1,1024,1024]{2,1,0:T(8,128)(2,1)}, u32[]{:S(2)}) copy-start(bf16[1,1024,1024]{2,1,0:T(8,128)(2,1)} %param.11) | copy-start | bytes 6291460
  0.6 15.4 %copy-start.2 = (f32[1,128,1024]{2,1,0:T(8,128)S(1)}, f32[1,128,1024]{2,1,0:T(8,128)}, u32[]{:S(2)}) copy-start(f32[1,128,1024]{2,1,0:T(8,128)} %param.14) | copy-start | bytes 1572868
  0.7 55.6 %copy-start.4 = (f32[128,128]{1,0:T(8,128)S(1)}, f32[128,128]{1,0:T(8,128)}, u32[]{:S(2)}) copy-start(f32[128,128]{1,0:T(8,128)} %param.15) | copy-start | bytes 196612
  0.7 56.1 %copy-start.5 = (s32[8,64,128]{2,1,0:T(8,128)S(1)}, s32[8,64,128]{2,1,0:T(8,128)}, u32[]{:S(2)}) copy-start(s32[8,64,128]{2,1,0:T(8,128)} %param.17) | copy-start | bytes 786436
  1.5 14.5 %copy-start.11 = (s32[128]{0:T(128)}, s32[128]{0:T(128)S(1)}, u32[]{:S(2)}) copy-start(s32[128]{0:T(128)S(1)} %get-tuple-element.23) | copy-start | bytes 1540
  1.5 58.1 %copy-start.10 = (s32[128]{0:T(128)}, s32[128]{0:T(128)S(1)}, u32[]{:S(2)}) copy-start(s32[128]{0:T(128)S(1)} %get-tuple-element.22) | copy-start | bytes 1540
  6.5 51.3 %collective-permute-start = (f32[8,128]{0,1:T(8,128)}, f32[8,128]{0,1:T(8,128)}, u32[]{:S(2)}, u32[]{:S(2)}) collective-permute-start(f32[8,128]{0,1:T(8,128)} %bitcast.9), channel_id=1, source_target_pairs={{0,2},{2,4},{4,6},{6,8},{8,10},{10,12},{12,14},{14,16},{16,18},{18... | collective-permute-start | bytes 12296 | tf_op jit(solution)/shard_map/ppermute | solution.py:23
  13.3 46.3 %collective-permute-start.1 = (f32[8,128]{0,1:T(8,128)}, f32[8,128]{0,1:T(8,128)}, u32[]{:S(2)}, u32[]{:S(2)}) collective-permute-start(f32[8,128]{0,1:T(8,128)} %bitcast.11), channel_id=1, source_target_pairs={{2,0},{4,2},{6,4},{8,6},{10,8},{12,10},{14,12},{16,14},{18,16},{20... | collective-permute-start | bytes 12296 | tf_op jit(solution)/shard_map/ppermute | solution.py:24
  56.8 4.5 copy-start.6
  61.4 80.6 %copy-start.3 = (f32[8,1024]{0,1:T(8,128)}, f32[8,1024]{0,1:T(8,128)S(1)}, u32[]{:S(2)}) copy-start(f32[8,1024]{0,1:T(8,128)S(1)} %scatter_custom_fusion.1) | copy-start | bytes 98308
  142.0 4.7 copy-start.12
  143.3 62.6 %copy-start.1 = (f32[8,1024]{0,1:T(8,128)}, f32[8,1024]{0,1:T(8,128)S(1)}, u32[]{:S(2)}) copy-start(f32[8,1024]{0,1:T(8,128)S(1)} %multiply_add_fusion) | copy-start | bytes 98308
  190.5 8.9 %collective-permute-start.2 = (f32[8,128]{0,1:T(8,128)}, f32[8,128]{0,1:T(8,128)}, u32[]{:S(2)}, u32[]{:S(2)}) collective-permute-start(f32[8,128]{0,1:T(8,128)} %bitcast.116), channel_id=1, source_target_pairs={{0,2},{2,4},{4,6},{6,8},{8,10},{10,12},{12,14},{14,16},{16,18},{18... | collective-permute-start | bytes 12296 | tf_op jit(solution)/shard_map/ppermute | solution.py:23
  195.8 49.0 %copy-start.13 = (f32[8,1]{0,1:T(1,128)S(1)}, f32[8,1]{0,1:T(1,128)}, u32[]{:S(2)}) copy-start(f32[8,1]{0,1:T(1,128)} %copy-done.12) | copy-start | bytes 100
  195.8 6.9 %collective-permute-start.3 = (f32[8,128]{0,1:T(8,128)}, f32[8,128]{0,1:T(8,128)S(1)}, u32[]{:S(2)}, u32[]{:S(2)}) collective-permute-start(f32[8,128]{0,1:T(8,128)} %bitcast.115), channel_id=1, source_target_pairs={{2,0},{4,2},{6,4},{8,6},{10,8},{12,10},{14,12},{16,14},{18,16},{20... | collective-permute-start | bytes 12296 | tf_op jit(solution)/shard_map/ppermute | solution.py:24
  461.6 18.7 %copy-start.9 = (f32[8,8]{1,0:T(8,128)S(1)}, f32[8,8]{1,0:T(8,128)}, u32[]{:S(2)}) copy-start(f32[8,8]{1,0:T(8,128)} %param.16) | copy-start | bytes 772
  480.2 4.3 copy-start.7
  480.2 4.3 copy-start.8
  484.5 7.2 %collective-permute-start.5 = (f32[1,128]{1,0:T(1,128)S(1)}, f32[1,128]{1,0:T(1,128)S(1)}, u32[]{:S(2)}, u32[]{:S(2)}) collective-permute-start(f32[1,128]{1,0:T(1,128)S(1)} %get-tuple-element.20), channel_id=1, source_target_pairs={{0,2},{2,4},{4,6},{6,8},{8,10},{10,12},{12,14},{14,16},{16,18},{18... | collective-permute-start | bytes 1544 | tf_op jit(solution)/shard_map/ppermute | solution.py:23
  489.8 4.9 collective-permute-start.4
  494.8 5.3 %collective-permute-start.6 = (f32[66,1]{1,0:T(8,128)S(1)}, f32[66,1]{1,0:T(8,128)S(1)}, u32[]{:S(2)}, u32[]{:S(2)}) collective-permute-start(f32[66,1]{1,0:T(8,128)S(1)} %get-tuple-element.16), channel_id=1, source_target_pairs={{1,0},{3,2},{5,4},{7,6},{9,8},{11,10},{13,12},{15,14},{17,16},{19,... | collective-permute-start | bytes 800 | tf_op jit(solution)/shard_map/ppermute | solution.py:24
  496.1 5.0 collective-permute-start.7
  501.2 5.1 collective-permute-start.9
  504.3 4.9 collective-permute-start.8
  509.3 6.1 %collective-permute-start.10 = (f32[66,1]{1,0:T(8,128)S(1)}, f32[66,1]{1,0:T(8,128)S(1)}, u32[]{:S(2)}, u32[]{:S(2)}) collective-permute-start(f32[66,1]{1,0:T(8,128)S(1)} %get-tuple-element.14), channel_id=1, source_target_pairs={{1,0},{3,2},{5,4},{7,6},{9,8},{11,10},{13,12},{15,14},{17,16},{19,... | collective-permute-start | bytes 800 | tf_op jit(solution)/shard_map/ppermute | solution.py:24
  510.6 5.0 collective-permute-start.11
where the time goes:
time: 519 us; the launch traced here: 516 us
  local copies, waits for them, and re-layouts  244 us (47%)
  blocking collectives  199 us (38%)
  starting transfers between devices  36.4 us (7%)
  other arithmetic  18.3 us (4%)
  matrix products  10.4 us (2%)
  waiting for transfers between devices  7.15 us (1%)
    gather x2, local copies, waits for them, and re-layouts, on_device(): nodal = adjoint[:, elem_dofs]  234 us
    psum x2, blocking collectives, apply_dual(): csum = lax.psum(jnp.dot(vec, corners.T, precision=hi), ('gx', 'gy'))  80.7 us
    psum x2, blocking collectives, residual_products(): return lax.psum(inner(resid, zvec), ('gx', 'gy'))  80.2 us
    psum x1, blocking collectives, on_device(): alpha = rz_now / lax.psum(inner(direction, image), ('gx', 'gy'))  37.8 us
    ppermute x6, starting transfers between devices, padded_2(): before = lax.ppermute(last, axis, up)  26.1 us
  transfers between devices with their start and end apart: 12, of which 4 were waited for; matrix products, arithmetic and copies ran while one was open for 2% of the time, Pallas kernels for 0%

commit v1 on v0

v1 whole, which is shorter than its diff:
```python
import jax
import jax.numpy as jnp
from jax import lax
from jax.experimental import pallas as pl
from jax.experimental.pallas import tpu as pltpu
from jax.sharding import PartitionSpec as P

R = 128
LANES = 128
CASES = 8
CORNERS = 4

coupling = 0.3
radius_sq = 2.0
penalty = 3.0
diag = 1.0 + 4.0 * radius_sq

HI = lax.Precision.HIGHEST
F32 = jnp.float32
BF16 = jnp.bfloat16
VMEM = pl.BlockSpec(memory_space=pltpu.VMEM)
SMEM = pl.BlockSpec(memory_space=pltpu.SMEM)

SIDE_P, SIDE_Y, SIDE_M, SIDE_C = 0, 8, 16, 24
RZ, PQ, QMQ, TLT, PE, TE = range(6)


def rows_dot(a, b):
    return lax.dot_general(a, b, (((1,), (1,)), ((), ())), precision=HI, preferred_element_type=F32)


def plain_dot(a, b):
    return lax.dot_general(a, b, (((1,), (0,)), ((), ())), precision=HI, preferred_element_type=F32)


def halves(x):
    high = x.astype(BF16)
    low = (x - high.astype(F32)).astype(BF16)
    return jnp.concatenate([high, low], axis=0)


def lane_sum(x):
    return jnp.sum(x, axis=1, keepdims=True)


def pattern(idx):
    return idx & (LANES - 1), (idx & 128) != 0, (idx & 256) != 0, (idx & 512) != 0


def pick(blocks, where):
    lane, bit0, bit1, bit2 = where
    got = [jnp.take_along_axis(b, lane, axis=1, mode="promise_in_bounds") for b in blocks]
    got = [jnp.where(bit0, got[2 * i + 1], got[2 * i]) for i in range(4)]
    got = [jnp.where(bit1, got[2 * i + 1], got[2 * i]) for i in range(2)]
    return jnp.where(bit2, got[1], got[0])


def blocks_of(row8):
    return [row8[:, LANES * h : LANES * (h + 1)] for h in range(8)]


def first_kernel(loads_ref, pre_ref, corner_ref, send_ref, p_ref):
    p = pre_ref[...] * loads_ref[:, 0, :]
    p_ref[...] = p
    part = rows_dot(p, corner_ref[0])
    for d in range(send_ref.shape[0]):
        send_ref[d] = part


def side_kernel(odd_ref, p_ref, op_ref, iface_ref, pre_ref, corner_ref,
                y_ref, rest_ref, even_ref, oddp_ref, hot_ref):
    p = p_ref[...]
    both = lax.dot_general(halves(p), op_ref[0], (((1,), (1,)), ((), ())), preferred_element_type=F32)
    y = both[:CASES]
    y_ref[...] = y
    rest_ref[...] = both[CASES:]
    pre = jnp.broadcast_to(pre_ref[...], (8, pre_ref.shape[1]))
    left = iface_ref[0, :, :R]
    right = iface_ref[0, :, R : 2 * R]
    odd = jnp.broadcast_to(odd_ref[0] != 0, (1, R))
    for side, (idx, out) in enumerate(((jnp.where(odd, left, right), even_ref),
                                       (jnp.where(odd, right, left), oddp_ref))):
        where = pattern(jnp.broadcast_to(idx, (8, R)))
        scale = pick(blocks_of(pre), where)
        out[SIDE_P : SIDE_P + 8] = pick(blocks_of(p), where)
        out[SIDE_Y : SIDE_Y + 8] = scale * pick(blocks_of(y), where)
        out[SIDE_M : SIDE_M + 8] = scale
        for j in range(corner_ref.shape[1] // 8):
            rows = corner_ref[0, 8 * j : 8 * j + 8]
            out[SIDE_C + 8 * j : SIDE_C + 8 * j + 8] = scale * pick(blocks_of(rows), where)
        column = jnp.transpose(jnp.broadcast_to(idx, (R, R)))
        for h in range(8):
            at = lax.broadcasted_iota(jnp.int32, (R, LANES), 1) + LANES * h
            hot_ref[side, :, LANES * h : LANES * (h + 1)] = jnp.where(column == at, 1.0, 0.0).astype(BF16)


def spread(values, hot):
    high = values.astype(BF16)
    rest = values - high.astype(F32)
    mid = rest.astype(BF16)
    low = (rest - mid.astype(F32)).astype(BF16)
    parts = jnp.concatenate([high, mid, low, jnp.zeros_like(low)], axis=0)
    got = lax.dot_general(parts, hot, (((1,), (0,)), ((), ())), preferred_element_type=F32)
    return got[:8] + got[8:16] + got[16:24]


def second_kernel(got_ref, coarse_ref, loads_ref, p_ref, y_ref, rest_ref, pre_ref, corner_ref, op_ref,
                  mine_e_ref, mine_o_ref, theirs_e_ref, theirs_o_ref, hot_ref,
                  send_ref, t_ref):
    total = got_ref[0]
    for d in range(1, got_ref.shape[0]):
        total = total + got_ref[d]
    w = rows_dot(total, coarse_ref[...])
    p = p_ref[...]
    q = y_ref[...] + plain_dot(w, corner_ref[0])
    tlt = None
    for side, (mine, theirs) in enumerate(((mine_e_ref, theirs_e_ref), (mine_o_ref, theirs_o_ref))):
        p_mine, p_theirs = mine[SIDE_P : SIDE_P + 8], theirs[SIDE_P : SIDE_P + 8]
        q = q + spread(-coupling * p_theirs, hot_ref[side])
        t_mine = mine[SIDE_Y : SIDE_Y + 8] - coupling * mine[SIDE_M : SIDE_M + 8] * p_theirs
        t_mine = t_mine + plain_dot(w, mine[SIDE_C:])
        t_theirs = theirs[SIDE_Y : SIDE_Y + 8] - coupling * theirs[SIDE_M : SIDE_M + 8] * p_mine
        t_theirs = t_theirs + plain_dot(w, theirs[SIDE_C:])
        term = -coupling * lane_sum(t_mine * t_theirs)
        tlt = term if tlt is None else tlt + term
    t = pre_ref[...] * q
    t_ref[...] = t
    both = lax.dot_general(halves(t), op_ref[0], (((1,), (1,)), ((), ())), preferred_element_type=F32)
    tlt = tlt + lane_sum(t * (both[:CASES] + both[CASES:]))
    g = rows_dot(t, corner_ref[0])
    rest = rest_ref[...]
    scalars = (lane_sum(loads_ref[:, 0, :] * p), lane_sum(p * q), lane_sum(q * t), tlt,
               lane_sum(p * rest), lane_sum(t * rest))
    lane = lax.broadcasted_iota(jnp.int32, (CASES, LANES), 1)
    block = jnp.zeros((CASES, LANES), F32)
    for j, s in enumerate(scalars):
        block = jnp.where(lane == j, s, block)
    for d in range(send_ref.shape[0]):
        send_ref[d, :CASES] = g
        send_ref[d, CASES:] = block


def make_table(table_ref, adj):
    for c in range(CASES):
        for h in range(8):
            table_ref[c, h] = jnp.broadcast_to(adj[c : c + 1, LANES * h : LANES * (h + 1)], (8, LANES))


def tile_energy(dofs, stiff_ref, table_ref, u_ref):
    for a in range(8):
        where = pattern(dofs(a))
        for c in range(CASES):
            u_ref[a, c] = pick([table_ref[c, h] for h in range(8)], where)
    total = None
    for c in range(CASES):
        u = [u_ref[a, c] for a in range(8)]
        for a in range(8):
            v = stiff_ref[a, 0] * u[0]
            for b in range(1, 8):
                v = v + stiff_ref[a, b] * u[b]
            total = u[a] * v if total is None else total + u[a] * v
    return total


def adjoint_kernel(stiff_ref, got_ref, coarse_ref, p_ref, t_ref, pack_ref, wpack_ref,
                   out_ref, adj_ref, edge_ref, table_ref, u_ref):
    total = got_ref[0]
    for d in range(1, got_ref.shape[0]):
        total = total + got_ref[d]
    g, s = total[:CASES], total[CASES:]
    rz, pq, qmq, tlt, pe, te = (s[:, j : j + 1] for j in (RZ, PQ, QMQ, TLT, PE, TE))
    tat = tlt + lane_sum(g * rows_dot(g, coarse_ref[...]))
    alpha = rz / pq
    rz_next = rz - 2.0 * alpha * pq + alpha * alpha * qmq
    grow = 1.0 + rz_next / rz
    pap = grow * grow * (pq + pe) - 2.0 * alpha * grow * (qmq + te) + alpha * alpha * tat
    alpha_next = rz_next / pap
    adj = (alpha + alpha_next * grow) * p_ref[...] - (alpha * alpha_next) * t_ref[...]
    out_ref[:, 0, :] = adj
    adj_ref[...] = adj
    make_table(table_ref, adj)
    edge_ref[...] = wpack_ref[...] * tile_energy(lambda a: pack_ref[a], stiff_ref, table_ref, u_ref)


def energy_kernel(stiff_ref, adj_ref, dofs_ref, density_ref, passive_ref, grad_ref, table_ref, u_ref):
    make_table(table_ref, adj_ref[...])

    @pl.loop(0, grad_ref.shape[0] // 8)
    def _(tile):
        rows = pl.ds(pl.multiple_of(8 * tile, 8), 8)
        energy = tile_energy(lambda a: dofs_ref[a, rows, :], stiff_ref, table_ref, u_ref)
        rho = density_ref[rows, :]
        grad_ref[rows, :] = jnp.where(passive_ref[rows, :] == 1, 0.0, -penalty * rho * rho * energy)


def filter_kernel(place_ref, grad_ref, mine_ref, xe_ref, xo_ref, ye_ref, yo_ref,
                  ee_ref, eo_ref, oe_ref, oo_ref, out_ref):
    grad = grad_ref[...]
    ex, ey = grad.shape
    x_odd, y_odd = place_ref[0] != 0, place_ref[1] != 0
    has = [jnp.where(place_ref[2 + i] != 0, 1.0, 0.0) for i in range(4)]

    def choose(flag, a, b):
        return jnp.where(jnp.broadcast_to(flag, a.shape), a, b)

    xe, xo, ye, yo = xe_ref[...], xo_ref[...], ye_ref[...], yo_ref[...]
    below, above = choose(x_odd, xe, xo), choose(x_odd, xo, xe)
    before, after = choose(y_odd, ye, yo), choose(y_odd, yo, ye)
    ee, eo, oe, oo = ee_ref[...], eo_ref[...], oe_ref[...], oo_ref[...]
    diag_ye = (choose(x_odd, ee, oe), choose(x_odd, oe, ee))
    diag_yo = (choose(x_odd, eo, oo), choose(x_odd, oo, eo))
    below_before, below_after = (choose(y_odd, diag_ye[0], diag_yo[0]), choose(y_odd, diag_yo[0], diag_ye[0]))
    above_before, above_after = (choose(y_odd, diag_ye[1], diag_yo[1]), choose(y_odd, diag_yo[1], diag_ye[1]))
    mine = mine_ref[...]
    last = LANES - 1
    corner = [
        below_before[3:4, last:] / diag, below_after[3:4, :1] / diag,
        above_before[0:1, last:] / diag, above_after[0:1, :1] / diag,
    ]
    lane = lax.broadcasted_iota(jnp.int32, (1, LANES), 1)

    def shifted(row, low, high, length):
        left = jnp.where(lane == 0, low, pltpu.roll(row, 1, 1))
        right = jnp.where(lane == length - 1, high, pltpu.roll(row, LANES - 1, 1))
        return left + right

    def half(row, second):
        return pltpu.roll(row, LANES - ex, 1) if second else row

    g_before1, g_before2 = half(before[5:6], True), half(before[5:6], False)
    g_after1, g_after2 = half(after[4:5], False), half(after[4:5], True)
    col_first, col_last = half(mine[4:5], False), half(mine[5:6], True)
    g_below1, g_below2 = below[3:4], below[2:3]
    g_above1, g_above2 = above[0:1], above[1:2]
    s_below1, s_above1 = g_below1 / diag, g_above1 / diag
    s_before1, s_after1 = g_before1 / diag, g_after1 / diag

    def ring(g1, s2, inner, beside, there):
        return there * (g1 + radius_sq * (s2 + inner + beside)) / diag

    def at(row, j):
        return row[:, j : j + 1]

    n_below = ring(g_below1, g_below2 / diag, mine[0:1] / diag,
                   shifted(s_below1, corner[0], corner[1], ey), has[0])
    n_above = ring(g_above1, g_above2 / diag, mine[3:4] / diag,
                   shifted(s_above1, corner[2], corner[3], ey), has[1])
    n_before = ring(g_before1, g_before2 / diag, col_first / diag,
                    shifted(s_before1, corner[0], corner[2], ex), has[2])
    n_after = ring(g_after1, g_after2 / diag, col_last / diag,
                   shifted(s_after1, corner[1], corner[3], ex), has[3])
    stack = jnp.concatenate([s_before1, s_after1, n_before, n_after, jnp.zeros((4, LANES), F32)], axis=0)
    columns = jnp.transpose(stack)[:ex]
    row_no = lax.broadcasted_iota(jnp.int32, (ex, ey), 0)
    col_no = lax.broadcasted_iota(jnp.int32, (ex, ey), 1)

    def sweep(s, below_row, above_row, before_col, after_col):
        down = jnp.where(row_no == 0, below_row, pltpu.roll(s, 1, 0))
        up = jnp.where(row_no == ex - 1, above_row, pltpu.roll(s, ex - 1, 0))
        left = jnp.where(col_no == 0, before_col, pltpu.roll(s, 1, 1))
        right = jnp.where(col_no == ey - 1, after_col, pltpu.roll(s, ey - 1, 1))
        return (grad + radius_sq * (up + down + right + left)) / diag

    s = grad / diag
    s = sweep(s, s_below1, s_above1, columns[:, 0:1], columns[:, 1:2])
    out_ref[...] = sweep(s, n_below, n_above, columns[:, 2:3], columns[:, 3:4])


def swaps(size):
    out = []
    for first in (0, 1):
        pairs = [(i, i + 1) for i in range(first, size - 1, 2)]
        out.append(pairs + [(j, i) for i, j in pairs])
    return out


def swap_over(array, axis, pairs):
    return lax.ppermute(array, axis, pairs) if pairs else jnp.zeros_like(array)


def f32(*shape):
    return jax.ShapeDtypeStruct(shape, F32)


def cost(flops, moved):
    return pl.CostEstimate(flops=flops, bytes_accessed=moved, transcendentals=0)


def params():
    return pltpu.CompilerParams(vmem_limit_bytes=24 * 1024 * 1024)


def edge_pack(array):
    ex, ey = array.shape[-2:]
    rows = jnp.concatenate([array[..., :2, :], array[..., ex - 2 :, :]], axis=-2)
    cols = jnp.concatenate([array[..., :2], array[..., ey - 2 :]], axis=-1)
    cols = jnp.swapaxes(cols, -1, -2).reshape(array.shape[:-2] + (4 * ex // LANES, LANES))
    pad = jnp.zeros(array.shape[:-2] + (8 - rows.shape[-2] - cols.shape[-2], LANES), array.dtype)
    return jnp.concatenate([rows, cols, pad], axis=-2)


def on_device(loads, dual_op, iface, precond, corner_map, coarse_inv, elem_stiff, elem_dofs, density, passive):
    nx, ny = lax.axis_size("gx"), lax.axis_size("gy")
    everyone = nx * ny
    unknowns = dual_op.shape[-1]
    modes = corner_map.shape[1]
    ex, ey = density.shape
    x, y = lax.axis_index("gx"), lax.axis_index("gy")
    place = jnp.stack([x % 2, y % 2, x > 0, x < nx - 1, y > 0, y < ny - 1]).astype(jnp.int32)
    x_even, x_odd = swaps(nx)
    y_even, y_odd = swaps(ny)

    send, p = pl.pallas_call(
        first_kernel, out_shape=(f32(everyone, CASES, modes), f32(CASES, unknowns)),
        in_specs=[VMEM] * 3, out_specs=(VMEM, VMEM), compiler_params=params(), name="first",
    )(loads, precond, corner_map)
    got = lax.all_to_all(send, ("gx", "gy"), 0, 0)

    side = f32(SIDE_C + modes, R)
    yloc, rest, mine_e, mine_o, hot = pl.pallas_call(
        side_kernel,
        out_shape=(f32(CASES, unknowns), f32(CASES, unknowns), side, side,
                   jax.ShapeDtypeStruct((2, R, unknowns), BF16)),
        in_specs=[SMEM] + [VMEM] * 5, out_specs=(VMEM,) * 5, compiler_params=params(), name="sides",
        cost_estimate=cost(40_000_000, 4_000_000),
    )(place, p, dual_op, iface, precond, corner_map)
    theirs_e = swap_over(mine_e, "gx", x_even)
    theirs_o = swap_over(mine_o, "gx", x_odd)

    send, t = pl.pallas_call(
        second_kernel, out_shape=(f32(everyone, 2 * CASES, modes), f32(CASES, unknowns)),
        in_specs=[VMEM] * 14, out_specs=(VMEM, VMEM), compiler_params=params(), name="second",
    )(got, coarse_inv, loads, p, yloc, rest, precond, corner_map, dual_op,
      mine_e, mine_o, theirs_e, theirs_o, hot)
    got = lax.all_to_all(send, ("gx", "gy"), 0, 0)

    weight = jnp.where(passive == 1, 0.0, -penalty * density * density)
    table = pltpu.VMEM((CASES, 8, 8, LANES), F32)
    gathered = pltpu.VMEM((8, CASES, 8, LANES), F32)
    adjoint, adj, edge = pl.pallas_call(
        adjoint_kernel, out_shape=(f32(CASES, 1, unknowns), f32(CASES, unknowns), f32(8, LANES)),
        in_specs=[SMEM] + [VMEM] * 6, out_specs=(VMEM,) * 3, scratch_shapes=[table, gathered],
        compiler_params=params(), name="adjoint",
    )(elem_stiff, got, coarse_inv, p, t, edge_pack(elem_dofs), edge_pack(weight))

    xe, xo = swap_over(edge, "gx", x_even), swap_over(edge, "gx", x_odd)
    ye, yo = swap_over(edge, "gy", y_even), swap_over(edge, "gy", y_odd)
    corners = []
    for px in (x_even, x_odd):
        for py in (y_even, y_odd):
            pairs = [(a * ny + c, b * ny + d) for a, b in px for c, d in py]
            corners.append(swap_over(edge, ("gx", "gy"), pairs))

    grad = pl.pallas_call(
        energy_kernel, out_shape=f32(ex, ey), in_specs=[SMEM] + [VMEM] * 4, out_specs=VMEM,
        scratch_shapes=[table, gathered], compiler_params=params(), name="energy",
        cost_estimate=cost(60_000_000, 20_000_000),
    )(elem_stiff, adj, elem_dofs, density, passive)

    sens = pl.pallas_call(
        filter_kernel, out_shape=f32(ex, ey), in_specs=[SMEM] + [VMEM] * 10, out_specs=VMEM,
        compiler_params=params(), name="smooth",
    )(place, grad, edge, xe, xo, ye, yo, *corners)
    return adjoint, sens


def solution(mesh):
    placed = (
        P(None, "gy", "gx"),
        P("gy", "gx", None),
        P("gy", "gx", None),
        P("gy", "gx"),
        P("gy", None, "gx"),
        P(),
        P(),
        P(None, "gx", "gy"),
        P("gx", "gy"),
        P("gx", "gy"),
    )
    return jax.shard_map(
        on_device,
        mesh=mesh,
        in_specs=placed,
        out_specs=(P(None, "gy", "gx"), P("gx", "gy")),
        check_vma=False,
    )
```

time: 519 us -> 79.9 us (0.15)
  local copies, waits for them, and re-layouts: 244 us -> 26.2 us
  blocking collectives: 199 us -> 0 us
  Pallas kernels: 0 us -> 15.3 us
  other arithmetic: 18.3 us -> 3.02 us
  starting transfers between devices: 36.4 us -> 23.2 us
  matrix products: 10.4 us -> 0 us
    gather x6 -> x0, local copies, waits for them, and re-layouts: 241 us -> none  [the longest x2 234 us: on_device(): nodal = adjoint[:, elem_dofs]]
    psum x5 -> x0, blocking collectives: 199 us -> none  [the longest x2 80.7 us: apply_dual(): csum = lax.psum(jnp.dot(vec, corners.T, precision=hi), ('gx', 'gy'))]
    ppermute x12 -> x7, starting transfers between devices: 36.4 us -> 12.3 us  [swap_over(): return lax.ppermute(array, axis, pairs) if pairs else jnp.zeros_like(array)]
    unnamed x30 -> x58, local copies, waits for them, and re-layouts: 1.85 us -> 20.8 us
    pallas_call x0 -> x6, Pallas kernels: none -> 15.3 us  [the longest x1 6 us: on_device(): pl.pallas_call(energy_kernel, out_shape=f32(ex, ey), in_specs=[SMEM] + [V...]
    all_to_all x0 -> x2, starting transfers between devices: none -> 10.9 us  [on_device(): got = lax.all_to_all(send, ('gx', 'gy'), 0, 0)]
    dot_general x9 -> x0, matrix products: 10.4 us -> none  [the longest x1 4.25 us: on_device(): pushed = jnp.einsum('ab,cbxy->caxy', elem_stiff, nodal, precision=hi)]
    scatter-add x4 -> x0, other arithmetic: 9.97 us -> none  [the longest x2 5.08 us: local_part(): local = local.at[:, left_idx].add(-coupling * extended[:, :width])]
  transfers between devices with their start and end apart: 12 -> 9, of which waited for: 4 -> 1; matrix products, arithmetic and copies ran while one was open for 2% -> 15% of each run, Pallas kernels for 0% -> 8%
where the time goes in v1:
time: 79.9 us; the launch traced here: 78.3 us
  local copies, waits for them, and re-layouts  26.2 us (33%)
  starting transfers between devices  23.2 us (29%)
  Pallas kernels  15.3 us (19%)
  waiting for transfers between devices  9.59 us (12%)
  other arithmetic  3.02 us (4%)
  between operations  0.88 us (1%)
    unnamed x58, local copies, waits for them, and re-layouts  20.8 us
    ppermute x7, starting transfers between devices, swap_over(): return lax.ppermute(array, axis, pairs) if pairs else jnp.zeros_like(array)  12.3 us
    all_to_all x2, starting transfers between devices, on_device(): got = lax.all_to_all(send, ('gx', 'gy'), 0, 0)  10.9 us
    all_to_all x2, waiting for transfers between devices, on_device(): got = lax.all_to_all(send, ('gx', 'gy'), 0, 0)  9.58 us
    pallas_call x1, Pallas kernels, on_device(): pl.pallas_call(energy_kernel, out_shape=f32(ex, ey), in_specs=[SMEM] + [V...  6 us
    slice x4, local copies, waits for them, and re-layouts, edge_pack(): cols = jnp.concatenate([array[..., :2], array[..., ey - 2:]], axis=-1)  3.83 us
    pallas_call x1, Pallas kernels, on_device(): pl.pallas_call(second_kernel, out_shape=(f32(everyone, 2 * CASES, modes),...  3.05 us
    pallas_call x1, Pallas kernels, on_device(): pl.pallas_call(adjoint_kernel, out_shape=(f32(CASES, 1, unknowns), f32(CA...  2.21 us
  transfers between devices with their start and end apart: 9, of which 1 were waited for; matrix products, arithmetic and copies ran while one was open for 15% of the time, Pallas kernels for 8%

profile of v1, /device:TPU:1, one launch (start us, length us, event | category | flops | bytes accessed | tf_op | source)
XLA Modules:
  0.0 78.3 jit_solution(10286014374394872330)
XLA Ops:
  0.7 1.0 %copy-done.2 = f32[1,128,1024]{2,1,0:T(8,128)S(1)} copy-done((f32[1,128,1024]{2,1,0:T(8,128)S(1)}, f32[1,128,1024]{2,1,0:T(8,128)}, u32[]{:S(2)}) %copy-start.2) | copy-done | bytes 524312
  1.7 0.8 copy-done.12
  4.4 1.6 %copy-done = bf16[1,1024,1024]{2,1,0:T(8,128)(2,1)S(1)} copy-done((bf16[1,1024,1024]{2,1,0:T(8,128)(2,1)S(1)}, bf16[1,1024,1024]{2,1,0:T(8,128)(2,1)}, u32[]{:S(2)}) %copy-start) | copy-done | bytes 2097176
  6.0 1.0 %copy-done.3 = f32[1,128,1024]{2,1,0:T(8,128)S(1)} copy-done((f32[1,128,1024]{2,1,0:T(8,128)S(1)}, f32[1,128,1024]{2,1,0:T(8,128)}, u32[]{:S(2)}) %copy-start.3) | copy-done | bytes 524312
  8.4 2.0 %sides.1 = (f32[8,1024]{1,0:T(8,128)S(1)}, f32[8,1024]{1,0:T(8,128)S(1)}, f32[152,128]{1,0:T(8,128)}, f32[152,128]{1,0:T(8,128)}, bf16[2,128,1024]{2,1,0:T(8,128)(2,1)S(1)}) custom-call(s32[6]{0:T(128)S(1)} %stack.43.odd_ref.place_ref, f32[8,1024]{1,0:T(8,128)S(1)} %get-tuple-element.15.p_ref, bf16[1,1024,1024]{2,1,0:T(8,128)(2,1)S(1)} %copy-done, ...), custom_call_target="tpu_custom_call" | custom-call | flops 40000000 | bytes 4000000 | tf_op jit(solution)/shard_map/sides/pallas_call | solution.py:320
  11.7 4.5 %collective-permute-start.1 = (f32[152,128]{1,0:T(8,128)}, f32[152,128]{1,0:T(8,128)}, u32[]{:S(2)}, u32[]{:S(2)}) collective-permute-start(f32[152,128]{1,0:T(8,128)} %get-tuple-element.19.mine_o_ref), channel_id=1, source_target_pairs={{2,4},{6,8},{10,12},{14,16},{18,20},{22,24},{26,28},{4,2},{8,6},{1... | collective-permute-start | bytes 233480 | tf_op jit(solution)/shard_map/ppermute | solution.py:278
  16.2 5.1 %all-to-all-start = ((f32[32,8,128]{2,1,0:T(8,128)}), f32[32,8,128]{2,1,0:T(8,128)S(1)}, u32[]{:S(2)}, u32[]{:S(2)}) async-start(f32[32,8,128]{2,1,0:T(8,128)} %copy-done.16), calls=%async_computation | async-start | bytes 262144 | tf_op jit(solution)/shard_map/all_to_all | solution.py:317
  21.3 0.8 %fusion = f32[64,128]{1,0:T(8,128)S(1)} fusion(f32[64,128]{1,0:T(8,128)} %density_ref.1, s32[64,128]{1,0:T(8,128)} %passive_ref.1), kind=kLoop, calls=%fused_computation.1 | loop fusion | flops 32768 | bytes 98304 | tf_op jit(solution)/shard_map/jit(_where)/select_n | solution.py:337
  23.4 0.8 %copy.17 = f32[64,2]{0,1:T(2,128)S(1)} copy(f32[64,2]{1,0:T(8,128)} %get-tuple-element.32) | data formatting | bytes 1024 | tf_op jit(solution)/shard_map/slice | solution.py:296
  24.2 1.4 %copy.18 = f32[64,2]{0,1:T(2,128)} copy(f32[64,2]{1,0:T(8,128)} %get-tuple-element.33) | data formatting | bytes 1024 | tf_op jit(solution)/shard_map/slice | solution.py:296
  25.6 0.9 %fusion.2 = (s32[8,64,2]{2,1,0:T(8,128)}, s32[8,64,2]{2,1,0:T(8,128)}) fusion(s32[8,64,128]{2,1,0:T(8,128)S(1)} %copy-done.5), kind=kLoop, calls=%fused_computation.7 | loop fusion | bytes 16384 | tf_op jit(solution)/shard_map/slice | solution.py:296
  28.0 0.8 maximum_maximum_fusion.wpack_ref
  28.7 1.7 %copy.19 = s32[8,64,2]{1,0,2:T(8,128)} copy(s32[8,64,2]{2,1,0:T(8,128)} %get-tuple-element.28) | data formatting | bytes 8192
  30.4 1.7 %copy.20 = s32[8,64,2]{1,0,2:T(8,128)} copy(s32[8,64,2]{2,1,0:T(8,128)} %get-tuple-element.29) | data formatting | bytes 8192
  32.1 0.7 copy-done.7
  32.9 0.8 %copy-done.9 = f32[128,128]{1,0:T(8,128)S(1)} copy-done((f32[128,128]{1,0:T(8,128)S(1)}, f32[128,128]{1,0:T(8,128)}, u32[]{:S(2)}) %copy-start.9) | copy-done | bytes 65560
  33.7 0.8 copy-done.13
  34.5 0.8 copy-done.21
  35.2 0.8 copy-done.23
  36.0 3.1 %second.1 = (f32[32,16,128]{2,1,0:T(8,128)S(1)}, f32[8,1024]{1,0:T(8,128)S(1)}) custom-call(f32[32,8,128]{2,1,0:T(8,128)S(1)} %all-to-all-done.got_ref, f32[128,128]{1,0:T(8,128)S(1)} %copy-done.9, f32[8,1,1024]{2,1,0:T(1,128)S(1)} %copy-done.13, f32[8,1024]{1,0:T(8,128)S(1)} %copy-done.7, f32[8,1024]{1,0:T(8,128)S(1)} %copy-done.21, ...), custom_call_target="tpu_custom_call" | custom-call | tf_op jit(solution)/shard_map/second/pallas_call | solution.py:330
  40.4 5.8 %all-to-all-start.1 = ((f32[32,16,128]{2,1,0:T(8,128)}), f32[32,16,128]{2,1,0:T(8,128)S(1)}, u32[]{:S(2)}, u32[]{:S(2)}) async-start(f32[32,16,128]{2,1,0:T(8,128)} %copy-done.11), calls=%async_computation.1 | async-start | bytes 524288 | tf_op jit(solution)/shard_map/all_to_all | solution.py:335
  47.2 9.6 %all-to-all-done.1.got_ref = f32[32,16,128]{2,1,0:T(8,128)S(1)} async-done(((f32[32,16,128]{2,1,0:T(8,128)}), f32[32,16,128]{2,1,0:T(8,128)S(1)}, u32[]{:S(2)}, u32[]{:S(2)}) %all-to-all-start.1) | async-done | bytes 262176 | tf_op jit(solution)/shard_map/all_to_all | solution.py:335
  56.8 0.8 copy-done.8
  57.5 0.8 %copy-done.10 = f32[128,128]{1,0:T(8,128)S(1)} copy-done((f32[128,128]{1,0:T(8,128)S(1)}, f32[128,128]{1,0:T(8,128)}, u32[]{:S(2)}) %copy-start.10) | copy-done | bytes 65560
  58.4 0.8 copy-done.25
  59.1 2.2 %adjoint.1 = (f32[8,1,1024]{2,1,0:T(1,128)}, f32[8,1024]{1,0:T(8,128)S(1)}, f32[8,128]{1,0:T(8,128)S(1)}) custom-call(f32[8,8]{1,0:T(8,128)S(1)} %copy-done.26, f32[32,16,128]{2,1,0:T(8,128)S(1)} %all-to-all-done.1.got_ref, f32[128,128]{1,0:T(8,128)S(1)} %copy-done.10, f32[8,1024]{1,0:T(8,128)S(1)} %copy-done.8, f32[8,1024]{1,0:T(8,128)S(1)} %copy-done.25, ...), custom_call_target="tpu_custom_call" | custom-call | tf_op jit(solution)/shard_map/adjoint/pallas_call | solution.py:340
  61.7 2.3 %collective-permute-start.3 = (f32[8,128]{1,0:T(8,128)S(1)}, f32[8,128]{1,0:T(8,128)S(1)}, u32[]{:S(2)}, u32[]{:S(2)}) collective-permute-start(f32[8,128]{1,0:T(8,128)S(1)} %get-tuple-element.25.mine_ref), channel_id=1, source_target_pairs={{2,4},{6,8},{10,12},{14,16},{18,20},{22,24},{26,28},{4,2},{8,6},{1... | collective-permute-start | bytes 12296 | tf_op jit(solution)/shard_map/ppermute | solution.py:278
  64.7 4.4 %collective-permute-start.6 = (f32[8,128]{1,0:T(8,128)S(1)}, f32[8,128]{1,0:T(8,128)S(1)}, u32[]{:S(2)}, u32[]{:S(2)}) collective-permute-start(f32[8,128]{1,0:T(8,128)S(1)} %get-tuple-element.25.mine_ref), channel_id=1, source_target_pairs={{2,5},{3,4},{6,9},{7,8},{10,13},{11,12},{14,17},{15,16},{18,21},{1... | collective-permute-start | bytes 12296 | tf_op jit(solution)/shard_map/ppermute | solution.py:278
  69.1 0.7 copy-done.14
  69.9 0.8 copy-done.15
  70.6 6.0 %energy.1.grad_ref = f32[64,128]{1,0:T(8,128)S(1)} custom-call(f32[8,8]{1,0:T(8,128)S(1)} %copy-done.26, f32[8,1024]{1,0:T(8,128)S(1)} %get-tuple-element.24.adj_ref, s32[8,64,128]{2,1,0:T(8,128)S(1)} %copy-done.5, f32[64,128]{1,0:T(8,128)S(1)} %copy-done.14, s32[64,128]{1,0:T(8,128)S(1)} %copy-done.15), custom_call_target="tpu_custom_call" | custom-call | flops 60000000 | bytes 20000000 | tf_op jit(solution)/shard_map/energy/pallas_call | solution.py:354
  76.7 1.6 %smooth.1 = f32[64,128]{1,0:T(8,128)} custom-call(s32[6]{0:T(128)S(1)} %stack.43.odd_ref.place_ref, f32[64,128]{1,0:T(8,128)S(1)} %energy.1.grad_ref, f32[8,128]{1,0:T(8,128)S(1)} %get-tuple-element.25.mine_ref, f32[8,128]{1,0:T(8,128)S(1)} %collective-permute-done.2.xe_ref, f32[8,128]{1,0:T(8,128)S(1)} %collective-permute-done.3.xo_ref, ...), custom_call_target="tpu_custom_call" | custom-call | tf_op jit(solution)/shard_map/smooth/pallas_call | solution.py:360
  (70 shorter events, 10.7 us)
Async XLA Ops:
  0.7 1.0 %copy-start.2 = (f32[1,128,1024]{2,1,0:T(8,128)S(1)}, f32[1,128,1024]{2,1,0:T(8,128)}, u32[]{:S(2)}) copy-start(f32[1,128,1024]{2,1,0:T(8,128)} %corner_ref.5) | copy-start | bytes 1572868
  1.7 0.8 copy-start.12
  2.5 0.7 copy-start.17
  3.1 22.5 %copy-start.5 = (s32[8,64,128]{2,1,0:T(8,128)S(1)}, s32[8,64,128]{2,1,0:T(8,128)}, u32[]{:S(2)}) copy-start(s32[8,64,128]{2,1,0:T(8,128)} %dofs_ref.1) | copy-start | bytes 786436
  4.3 11.8 %copy-start.6 = (f32[8,1024]{1,0:T(8,128)}, f32[8,1024]{1,0:T(8,128)S(1)}, u32[]{:S(2)}) copy-start(f32[8,1024]{1,0:T(8,128)S(1)} %get-tuple-element.15.p_ref) | copy-start | bytes 98308
  4.4 1.6 %copy-start = (bf16[1,1024,1024]{2,1,0:T(8,128)(2,1)S(1)}, bf16[1,1024,1024]{2,1,0:T(8,128)(2,1)}, u32[]{:S(2)}) copy-start(bf16[1,1024,1024]{2,1,0:T(8,128)(2,1)} %op_ref.3) | copy-start | bytes 6291460
  6.0 1.0 %copy-start.3 = (f32[1,128,1024]{2,1,0:T(8,128)S(1)}, f32[1,128,1024]{2,1,0:T(8,128)}, u32[]{:S(2)}) copy-start(f32[1,128,1024]{2,1,0:T(8,128)} %corner_ref.5) | copy-start | bytes 1572868
  7.1 0.7 copy-start.18
  8.4 23.6 %copy-start.1 = (bf16[1,1024,1024]{2,1,0:T(8,128)(2,1)S(1)}, bf16[1,1024,1024]{2,1,0:T(8,128)(2,1)}, u32[]{:S(2)}) copy-start(bf16[1,1024,1024]{2,1,0:T(8,128)(2,1)} %op_ref.3) | copy-start | bytes 6291460
  8.4 23.7 %copy-start.4 = (f32[1,128,1024]{2,1,0:T(8,128)S(1)}, f32[1,128,1024]{2,1,0:T(8,128)}, u32[]{:S(2)}) copy-start(f32[1,128,1024]{2,1,0:T(8,128)} %corner_ref.5) | copy-start | bytes 1572868
  8.4 23.7 %copy-start.19 = (f32[1,1024]{1,0:T(1,128)S(1)}, f32[1,1024]{1,0:T(1,128)}, u32[]{:S(2)}) copy-start(f32[1,1024]{1,0:T(1,128)} %pre_ref.5) | copy-start | bytes 12292
  11.6 20.4 %collective-permute-start = (f32[152,128]{1,0:T(8,128)}, f32[152,128]{1,0:T(8,128)}, u32[]{:S(2)}, u32[]{:S(2)}) collective-permute-start(f32[152,128]{1,0:T(8,128)} %get-tuple-element.18.mine_e_ref), channel_id=1, source_target_pairs={{0,2},{4,6},{8,10},{12,14},{16,18},{20,22},{24,26},{28,30},{2,0},{... | collective-permute-start | bytes 233480 | tf_op jit(solution)/shard_map/ppermute | solution.py:278
  11.7 20.4 %collective-permute-start.1 = (f32[152,128]{1,0:T(8,128)}, f32[152,128]{1,0:T(8,128)}, u32[]{:S(2)}, u32[]{:S(2)}) collective-permute-start(f32[152,128]{1,0:T(8,128)} %get-tuple-element.19.mine_o_ref), channel_id=1, source_target_pairs={{2,4},{6,8},{10,12},{14,16},{18,20},{22,24},{26,28},{4,2},{8,6},{1... | collective-permute-start | bytes 233480 | tf_op jit(solution)/shard_map/ppermute | solution.py:278
  16.2 15.9 %all-to-all-start = ((f32[32,8,128]{2,1,0:T(8,128)}), f32[32,8,128]{2,1,0:T(8,128)S(1)}, u32[]{:S(2)}, u32[]{:S(2)}) async-start(f32[32,8,128]{2,1,0:T(8,128)} %copy-done.16), calls=%async_computation | async-start | bytes 262144 | tf_op jit(solution)/shard_map/all_to_all | solution.py:317
  32.1 0.8 copy-start.7
  32.9 0.8 %copy-start.9 = (f32[128,128]{1,0:T(8,128)S(1)}, f32[128,128]{1,0:T(8,128)}, u32[]{:S(2)}) copy-start(f32[128,128]{1,0:T(8,128)} %coarse_ref.3) | copy-start | bytes 196612
  33.7 0.8 copy-start.13
  34.5 0.8 copy-start.21
  35.2 0.8 copy-start.23
  36.0 20.8 %copy-start.26 = (f32[8,8]{1,0:T(8,128)S(1)}, f32[8,8]{1,0:T(8,128)}, u32[]{:S(2)}) copy-start(f32[8,8]{1,0:T(8,128)} %stiff_ref.3) | copy-start | bytes 772
  39.0 0.7 copy-start.11
  40.4 16.4 %all-to-all-start.1 = ((f32[32,16,128]{2,1,0:T(8,128)}), f32[32,16,128]{2,1,0:T(8,128)S(1)}, u32[]{:S(2)}, u32[]{:S(2)}) async-start(f32[32,16,128]{2,1,0:T(8,128)} %copy-done.11), calls=%async_computation.1 | async-start | bytes 524288 | tf_op jit(solution)/shard_map/all_to_all | solution.py:335
  56.8 0.8 copy-start.8
  57.5 0.8 %copy-start.10 = (f32[128,128]{1,0:T(8,128)S(1)}, f32[128,128]{1,0:T(8,128)}, u32[]{:S(2)}) copy-start(f32[128,128]{1,0:T(8,128)} %coarse_ref.3) | copy-start | bytes 196612
  58.4 0.8 copy-start.25
  61.3 15.3 %collective-permute-start.2 = (f32[8,128]{1,0:T(8,128)S(1)}, f32[8,128]{1,0:T(8,128)S(1)}, u32[]{:S(2)}, u32[]{:S(2)}) collective-permute-start(f32[8,128]{1,0:T(8,128)S(1)} %get-tuple-element.25.mine_ref), channel_id=1, source_target_pairs={{0,2},{4,6},{8,10},{12,14},{16,18},{20,22},{24,26},{28,30},{2,0},{... | collective-permute-start | bytes 12296 | tf_op jit(solution)/shard_map/ppermute | solution.py:278
  61.7 14.9 %collective-permute-start.3 = (f32[8,128]{1,0:T(8,128)S(1)}, f32[8,128]{1,0:T(8,128)S(1)}, u32[]{:S(2)}, u32[]{:S(2)}) collective-permute-start(f32[8,128]{1,0:T(8,128)S(1)} %get-tuple-element.25.mine_ref), channel_id=1, source_target_pairs={{2,4},{6,8},{10,12},{14,16},{18,20},{22,24},{26,28},{4,2},{8,6},{1... | collective-permute-start | bytes 12296 | tf_op jit(solution)/shard_map/ppermute | solution.py:278
  64.0 12.6 %collective-permute-start.4 = (f32[8,128]{1,0:T(8,128)S(1)}, f32[8,128]{1,0:T(8,128)S(1)}, u32[]{:S(2)}, u32[]{:S(2)}) collective-permute-start(f32[8,128]{1,0:T(8,128)S(1)} %get-tuple-element.25.mine_ref), channel_id=1, source_target_pairs={{0,1},{1,0},{2,3},{3,2},{4,5},{5,4},{6,7},{7,6},{8,9},{9,8},{10,11... | collective-permute-start | bytes 12296 | tf_op jit(solution)/shard_map/ppermute | solution.py:278
  64.7 12.0 %collective-permute-start.5 = (f32[8,128]{1,0:T(8,128)S(1)}, f32[8,128]{1,0:T(8,128)S(1)}, u32[]{:S(2)}, u32[]{:S(2)}) collective-permute-start(f32[8,128]{1,0:T(8,128)S(1)} %get-tuple-element.25.mine_ref), channel_id=1, source_target_pairs={{0,3},{1,2},{4,7},{5,6},{8,11},{9,10},{12,15},{13,14},{16,19},{17,... | collective-permute-start | bytes 12296 | tf_op jit(solution)/shard_map/ppermute | solution.py:278
  64.7 12.0 %collective-permute-start.6 = (f32[8,128]{1,0:T(8,128)S(1)}, f32[8,128]{1,0:T(8,128)S(1)}, u32[]{:S(2)}, u32[]{:S(2)}) collective-permute-start(f32[8,128]{1,0:T(8,128)S(1)} %get-tuple-element.25.mine_ref), channel_id=1, source_target_pairs={{2,5},{3,4},{6,9},{7,8},{10,13},{11,12},{14,17},{15,16},{18,21},{1... | collective-permute-start | bytes 12296 | tf_op jit(solution)/shard_map/ppermute | solution.py:278
  69.1 0.8 copy-start.14
  69.9 0.8 copy-start.15
  (5 other events, 3.2 us)

commit v2 on v1

v2 whole, which is shorter than its diff:
```python
import jax
import jax.numpy as jnp
from jax import lax
from jax.experimental import pallas as pl
from jax.experimental.pallas import tpu as pltpu
from jax.sharding import PartitionSpec as P

R = 128
LANES = 128
CASES = 8

coupling = 0.3
radius_sq = 2.0
penalty = 3.0
diag = 1.0 + 4.0 * radius_sq

HI = lax.Precision.HIGHEST
F32 = jnp.float32
BF16 = jnp.bfloat16
VMEM = pl.BlockSpec(memory_space=pltpu.VMEM)
HBM = pl.BlockSpec(memory_space=pltpu.HBM)

SIDE_P, SIDE_Y, SIDE_M, SIDE_C = 0, 8, 16, 24
RZ, PE, PQ, QMQ, TLT, TE = range(6)
KEEP_P, KEEP_Y, KEEP_REST, KEEP_S = 0, 8, 16, 24
FIELDS = 3 * CASES


def rows_dot(a, b):
    return lax.dot_general(a, b, (((1,), (1,)), ((), ())), precision=HI, preferred_element_type=F32)


def plain_dot(a, b):
    return lax.dot_general(a, b, (((1,), (0,)), ((), ())), precision=HI, preferred_element_type=F32)


def halves(x):
    high = x.astype(BF16)
    low = (x - high.astype(F32)).astype(BF16)
    return jnp.concatenate([high, low], axis=0)


def lane_sum(x):
    return jnp.sum(x, axis=1, keepdims=True)


def pattern(idx):
    return idx & (LANES - 1), (idx & 128) != 0, (idx & 256) != 0, (idx & 512) != 0


def pick(blocks, where):
    lane, bit0, bit1, bit2 = where
    got = [jnp.take_along_axis(b, lane, axis=1, mode="promise_in_bounds") for b in blocks]
    got = [jnp.where(bit0, got[2 * i + 1], got[2 * i]) for i in range(4)]
    got = [jnp.where(bit1, got[2 * i + 1], got[2 * i]) for i in range(2)]
    return jnp.where(bit2, got[1], got[0])


def blocks_of(row8):
    return [row8[:, LANES * h : LANES * (h + 1)] for h in range(8)]


def is_odd(axis):
    return lax.axis_index(axis) & 1 == 1


def at_lanes(columns, first=0):
    lane = lax.broadcasted_iota(jnp.int32, (CASES, LANES), 1)
    block = jnp.zeros((CASES, LANES), F32)
    for j, column in enumerate(columns):
        block = jnp.where(lane == first + j, column, block)
    return block


def fetch(sems, pairs):
    copies = [pltpu.make_async_copy(a, b, sems.at[i]) for i, (a, b) in enumerate(pairs)]
    for copy in copies:
        copy.start()
    return copies


def first_kernel(loads_hbm, pre_hbm, corner_hbm, send_ref, loads_ref, pre_ref, corner_ref, sems):
    copies = fetch(sems, ((loads_hbm, loads_ref), (pre_hbm, pre_ref), (corner_hbm, corner_ref)))
    for copy in copies:
        copy.wait()
    part = rows_dot(pre_ref[...] * loads_ref[:, 0, :], corner_ref[0])
    for d in range(send_ref.shape[0]):
        send_ref[d] = part


def side_kernel(loads_hbm, op_hbm, iface_hbm, pre_hbm, corner_hbm,
                keep_ref, even_ref, odd_ref, inverse_ref,
                loads_ref, op_ref, iface_ref, pre_ref, corner_ref, sems):
    copies = fetch(sems, ((loads_hbm, loads_ref), (pre_hbm, pre_ref), (iface_hbm, iface_ref),
                          (corner_hbm, corner_ref), (op_hbm, op_ref)))
    for copy in copies[:3]:
        copy.wait()
    loads = loads_ref[:, 0, :]
    p = pre_ref[...] * loads
    keep_ref[KEEP_P : KEEP_P + 8] = p
    pre = jnp.broadcast_to(pre_ref[...], (8, pre_ref.shape[1]))
    left = iface_ref[0, :, :R]
    right = iface_ref[0, :, R : 2 * R]
    x_odd = jnp.broadcast_to(is_odd("gx"), (1, R))
    sides = ((jnp.where(x_odd, left, right), even_ref), (jnp.where(x_odd, right, left), odd_ref))
    copies[3].wait()
    chosen = []
    for side, (idx, out) in enumerate(sides):
        where = pattern(jnp.broadcast_to(idx, (8, R)))
        scale = pick(blocks_of(pre), where)
        chosen.append((where, scale))
        out[SIDE_P : SIDE_P + 8] = pick(blocks_of(p), where)
        out[SIDE_M : SIDE_M + 8] = scale
        for j in range(corner_ref.shape[1] // 8):
            rows = corner_ref[0, 8 * j : 8 * j + 8]
            out[SIDE_C + 8 * j : SIDE_C + 8 * j + 8] = scale * pick(blocks_of(rows), where)
        column = jnp.transpose(jnp.broadcast_to(idx, (R, R)))
        number = lax.broadcasted_iota(jnp.int32, (R, LANES), 0) + 1
        for h in range(8):
            at = lax.broadcasted_iota(jnp.int32, (R, LANES), 1) + LANES * h
            found = jnp.sum(jnp.where(column == at, number, 0), axis=0, keepdims=True)
            inverse_ref[side, :, LANES * h : LANES * (h + 1)] = jnp.broadcast_to(found, (8, LANES))
    copies[4].wait()
    both = lax.dot_general(halves(p), op_ref[0], (((1,), (1,)), ((), ())), preferred_element_type=F32)
    y, rest = both[:CASES], both[CASES:]
    keep_ref[KEEP_Y : KEEP_Y + 8] = y
    keep_ref[KEEP_REST : KEEP_REST + 8] = rest
    keep_ref[KEEP_S : KEEP_S + 8, :LANES] = at_lanes((lane_sum(loads * p), lane_sum(p * rest)))
    for (where, scale), (_, out) in zip(chosen, sides):
        out[SIDE_Y : SIDE_Y + 8] = scale * pick(blocks_of(y), where)


def spread(values, inverse):
    out = []
    for h in range(8):
        at = inverse[:, LANES * h : LANES * (h + 1)]
        got = jnp.take_along_axis(values, jnp.maximum(at - 1, 0), axis=1, mode="promise_in_bounds")
        out.append(jnp.where(at > 0, got, 0.0))
    return jnp.concatenate(out, axis=1)


def second_kernel(got_ref, keep_ref, mine_e_ref, mine_o_ref, theirs_e_ref, theirs_o_ref, inverse_ref,
                  coarse_ref, corner_ref, op_ref, pre_hbm, send_ref, t_ref, pre_ref, sems):
    copies = fetch(sems, ((pre_hbm, pre_ref),))
    total = got_ref[0]
    for d in range(1, got_ref.shape[0]):
        total = total + got_ref[d]
    p = keep_ref[KEEP_P : KEEP_P + 8]
    base = keep_ref[KEEP_Y : KEEP_Y + 8]
    pairs = ((mine_e_ref, theirs_e_ref), (mine_o_ref, theirs_o_ref))
    for side, (_, theirs) in enumerate(pairs):
        base = base + spread(-coupling * theirs[SIDE_P : SIDE_P + 8], inverse_ref[side])
    w = rows_dot(total, coarse_ref[...])
    q = base + plain_dot(w, corner_ref[0])
    copies[0].wait()
    t = pre_ref[...] * q
    t_ref[...] = t
    g = rows_dot(t, corner_ref[0])
    tlt = None
    for mine, theirs in pairs:
        p_mine, p_theirs = mine[SIDE_P : SIDE_P + 8], theirs[SIDE_P : SIDE_P + 8]
        t_mine = mine[SIDE_Y : SIDE_Y + 8] - coupling * mine[SIDE_M : SIDE_M + 8] * p_theirs
        t_mine = t_mine + plain_dot(w, mine[SIDE_C:])
        t_theirs = theirs[SIDE_Y : SIDE_Y + 8] - coupling * theirs[SIDE_M : SIDE_M + 8] * p_mine
        t_theirs = t_theirs + plain_dot(w, theirs[SIDE_C:])
        term = -coupling * lane_sum(t_mine * t_theirs)
        tlt = term if tlt is None else tlt + term
    both = lax.dot_general(halves(t), op_ref[0], (((1,), (1,)), ((), ())), preferred_element_type=F32)
    tlt = tlt + lane_sum(t * (both[:CASES] + both[CASES:]))
    rest = keep_ref[KEEP_REST : KEEP_REST + 8]
    block = keep_ref[KEEP_S : KEEP_S + 8, :LANES]
    block = block + at_lanes((lane_sum(p * q), lane_sum(q * t), tlt, lane_sum(t * rest)), PQ)
    for d in range(send_ref.shape[0]):
        send_ref[d, :CASES] = g
        send_ref[d, CASES:] = block


def make_table(table_ref, vec):
    for c in range(CASES):
        for h in range(8):
            table_ref[c, h] = jnp.broadcast_to(vec[c : c + 1, LANES * h : LANES * (h + 1)], (8, LANES))


def gather_tile(dofs, table_ref, u_ref):
    for a in range(8):
        where = pattern(dofs(a))
        for c in range(CASES):
            u_ref[a, c] = pick([table_ref[c, h] for h in range(8)], where)


def stiff_row(stiff_ref, a, u):
    v = stiff_ref[a, 0] * u[0]
    for b in range(1, 8):
        v = v + stiff_ref[a, b] * u[b]
    return v


def edge_tiles(first, second):
    ex, ey = first.shape
    lane = lax.broadcasted_iota(jnp.int32, (1, LANES), 1)
    turned = jnp.transpose(jnp.concatenate([first, second], axis=0))
    swapped = pltpu.roll(turned, LANES - ex, 1)
    out = []
    for array, low, high in ((first, turned, swapped), (second, swapped, turned)):
        cols = [jnp.where(lane < ex, low[j : j + 1], high[j + 1 : j + 2]) for j in (0, ey - 2)]
        out.append(jnp.concatenate([array[0:2], array[ex - 2 :]] + cols + [array[0:2]], axis=0))
    return out


def p_kernel(keep_ref, dofs_ref, stiff_hbm, density_hbm, passive_hbm,
             kp_ref, pp_ref, pack_ref, weight_ref, table_ref, u_ref, stiff_ref, density_ref, passive_ref, sems):
    copies = fetch(sems, ((stiff_hbm, stiff_ref), (density_hbm, density_ref), (passive_hbm, passive_ref)))
    make_table(table_ref, keep_ref[KEEP_P : KEEP_P + 8])
    for a in range(0, 8, 2):
        first, second = edge_tiles(dofs_ref[a].astype(F32), dofs_ref[a + 1].astype(F32))
        pack_ref[a] = first.astype(jnp.int32)
        pack_ref[a + 1] = second.astype(jnp.int32)
    for copy in copies:
        copy.wait()
    rho = density_ref[...]
    weight = jnp.where(passive_ref[...] == 1, 0.0, -penalty * rho * rho)
    count = weight.shape[0] // 8
    for i in range(count):
        weight_ref[i] = weight[8 * i : 8 * i + 8]
    weight_ref[count] = edge_tiles(weight, weight)[0]

    def work(dofs, tile):
        gather_tile(dofs, table_ref, u_ref)
        scale = weight_ref[tile]
        for c in range(CASES):
            u = [u_ref[a, c] for a in range(8)]
            pp = None
            for a in range(8):
                v = stiff_row(stiff_ref, a, u)
                kp_ref[tile, a, c] = v
                pp = u[a] * v if pp is None else pp + u[a] * v
            pp_ref[tile, c] = scale * pp

    @pl.loop(0, count)
    def _(tile):
        rows = pl.ds(pl.multiple_of(8 * tile, 8), 8)
        work(lambda a: dofs_ref[a, rows, :], tile)

    work(lambda a: pack_ref[a], count)


def t_fields(stiff_ref, kp, scale, u_ref, c):
    u = [u_ref[a, c] for a in range(8)]
    pt = tt = None
    for a in range(8):
        v = stiff_ref[a, a] * u[a]
        for b in range(a + 1, 8):
            v = v + (stiff_ref[a, b] + stiff_ref[b, a]) * u[b]
        one, two = u[a] * kp(a, c), u[a] * v
        pt, tt = (one, two) if pt is None else (pt + one, tt + two)
    return scale * pt, scale * tt


def edge_kernel(t_ref, pack_ref, kp_ref, pp_ref, weight_ref, stiff_hbm,
                row_e_ref, row_o_ref, col_e_ref, col_o_ref, table_ref, u_ref, field_ref, stiff_ref, sems):
    copies = fetch(sems, ((stiff_hbm, stiff_ref),))
    make_table(table_ref, t_ref[...])
    gather_tile(lambda a: pack_ref[a], table_ref, u_ref)
    copies[0].wait()
    tile = kp_ref.shape[0] - 1
    for c in range(CASES):
        pt, tt = t_fields(stiff_ref, lambda a, c: kp_ref[tile, a, c], weight_ref[tile], u_ref, c)
        field_ref[c] = pp_ref[tile, c]
        field_ref[CASES + c] = pt
        field_ref[2 * CASES + c] = tt
    x_odd = jnp.broadcast_to(is_odd("gx"), (FIELDS, LANES))
    y_odd = jnp.broadcast_to(is_odd("gy"), (FIELDS, LANES))
    for i in range(2):
        low, high = field_ref[:, i, :], field_ref[:, 3 - i, :]
        row_e_ref[FIELDS * i : FIELDS * (i + 1)] = jnp.where(x_odd, low, high)
        row_o_ref[FIELDS * i : FIELDS * (i + 1)] = jnp.where(x_odd, high, low)
    low, high = field_ref[:, 4, :], field_ref[:, 5, :]
    col_e_ref[...] = jnp.where(y_odd, low, high)
    col_o_ref[...] = jnp.where(y_odd, high, low)


def t_kernel(t_ref, dofs_ref, kp_ref, weight_ref, stiff_hbm, pt_ref, tt_ref, table_ref, u_ref, stiff_ref, sems):
    copies = fetch(sems, ((stiff_hbm, stiff_ref),))
    make_table(table_ref, t_ref[...])
    copies[0].wait()

    @pl.loop(0, pt_ref.shape[0])
    def _(tile):
        rows = pl.ds(pl.multiple_of(8 * tile, 8), 8)
        gather_tile(lambda a: dofs_ref[a, rows, :], table_ref, u_ref)
        for c in range(CASES):
            pt_ref[tile, c], tt_ref[tile, c] = t_fields(
                stiff_ref, lambda a, c: kp_ref[tile, a, c], weight_ref[tile], u_ref, c)


def last_kernel(got_ref, coarse_ref, keep_ref, t_ref, pp_ref, pt_ref, tt_ref,
                mine_ye_ref, mine_yo_ref, xe_ref, xo_ref, ye_ref, yo_ref, ee_ref, eo_ref, oe_ref, oo_ref,
                adj_ref, out_ref):
    total = got_ref[0]
    for d in range(1, got_ref.shape[0]):
        total = total + got_ref[d]
    g, s = total[:CASES], total[CASES:]
    rz, pq, qmq, tlt, pe, te = (s[:, j : j + 1] for j in (RZ, PQ, QMQ, TLT, PE, TE))
    tat = tlt + lane_sum(g * rows_dot(g, coarse_ref[...]))
    alpha = rz / pq
    rz_next = rz - 2.0 * alpha * pq + alpha * alpha * qmq
    grow = 1.0 + rz_next / rz
    pap = grow * grow * (pq + pe) - 2.0 * alpha * grow * (qmq + te) + alpha * alpha * tat
    alpha_next = rz_next / pap
    of_p, of_t = alpha + alpha_next * grow, -(alpha * alpha_next)
    adj_ref[:, 0, :] = of_p * keep_ref[KEEP_P : KEEP_P + 8] + of_t * t_ref[...]

    factors = [of_p * of_p, 2.0 * of_p * of_t, of_t * of_t]
    wide = [jnp.broadcast_to(f, (CASES, LANES)) for f in factors]
    splat = [[jnp.broadcast_to(f[c : c + 1], (8, LANES)) for c in range(CASES)] for f in wide]
    tiles = []
    for i in range(pt_ref.shape[0]):
        tile = None
        for ref, factor in zip((pp_ref, pt_ref, tt_ref), splat):
            for c in range(CASES):
                term = factor[c] * ref[i, c]
                tile = term if tile is None else tile + term
        tiles.append(tile)
    grad = jnp.concatenate(tiles, axis=0)
    column = jnp.concatenate(wide, axis=0)

    def combine(fields):
        return jnp.sum(column * fields, axis=0, keepdims=True)

    ex, ey = grad.shape
    x_odd, y_odd = is_odd("gx"), is_odd("gy")
    has = []
    for axis in ("gx", "gy"):
        at, size = lax.axis_index(axis), lax.axis_size(axis)
        has += [jnp.where(at > 0, 1.0, 0.0), jnp.where(at < size - 1, 1.0, 0.0)]

    def choose(flag, a, b):
        return jnp.where(jnp.broadcast_to(flag, a.shape), a, b)

    def two(a, b, flag):
        return choose(flag, a, b), choose(flag, b, a)

    rows = [[combine(ref[FIELDS * i : FIELDS * (i + 1)]) for i in range(2)] for ref in (xe_ref, xo_ref)]
    g_below1, g_above1 = two(rows[0][0], rows[1][0], x_odd)
    g_below2, g_above2 = two(rows[0][1], rows[1][1], x_odd)
    before, after = two(combine(ye_ref[...]), combine(yo_ref[...]), y_odd)
    col_low, col_high = two(combine(mine_ye_ref[...]), combine(mine_yo_ref[...]), y_odd)
    ee, eo, oe, oo = (combine(ref[:FIELDS]) for ref in (ee_ref, eo_ref, oe_ref, oo_ref))
    below_e, above_e = two(ee, oe, x_odd)
    below_o, above_o = two(eo, oo, x_odd)
    below_before, below_after = two(below_e, below_o, y_odd)
    above_before, above_after = two(above_e, above_o, y_odd)
    last = LANES - 1
    corner = [below_before[:, last:] / diag, below_after[:, :1] / diag,
              above_before[:, last:] / diag, above_after[:, :1] / diag]
    lane = lax.broadcasted_iota(jnp.int32, (1, LANES), 1)

    def shifted(row, low, high, length):
        left = jnp.where(lane == 0, low, pltpu.roll(row, 1, 1))
        right = jnp.where(lane == length - 1, high, pltpu.roll(row, LANES - 1, 1))
        return left + right

    def upper(row):
        return pltpu.roll(row, LANES - ex, 1)

    g_before1, g_before2 = upper(before), before
    g_after1, g_after2 = after, upper(after)
    col_first, col_last = col_low, upper(col_high)
    s_below1, s_above1 = g_below1 / diag, g_above1 / diag
    s_before1, s_after1 = g_before1 / diag, g_after1 / diag

    def ring(g1, g2, inner, beside, there):
        return there * (g1 + radius_sq * (g2 / diag + inner / diag + beside)) / diag

    n_below = ring(g_below1, g_below2, grad[0:1], shifted(s_below1, corner[0], corner[1], ey), has[0])
    n_above = ring(g_above1, g_above2, grad[ex - 1 :], shifted(s_above1, corner[2], corner[3], ey), has[1])
    n_before = ring(g_before1, g_before2, col_first, shifted(s_before1, corner[0], corner[2], ex), has[2])
    n_after = ring(g_after1, g_after2, col_last, shifted(s_after1, corner[1], corner[3], ex), has[3])
    stack = jnp.concatenate([s_before1, s_after1, n_before, n_after, jnp.zeros((4, LANES), F32)], axis=0)
    columns = jnp.transpose(stack)[:ex]
    row_no = lax.broadcasted_iota(jnp.int32, (ex, ey), 0)
    col_no = lax.broadcasted_iota(jnp.int32, (ex, ey), 1)

    def sweep(s, below_row, above_row, before_col, after_col):
        down = jnp.where(row_no == 0, below_row, pltpu.roll(s, 1, 0))
        up = jnp.where(row_no == ex - 1, above_row, pltpu.roll(s, ex - 1, 0))
        left = jnp.where(col_no == 0, before_col, pltpu.roll(s, 1, 1))
        right = jnp.where(col_no == ey - 1, after_col, pltpu.roll(s, ey - 1, 1))
        return (grad + radius_sq * (up + down + right + left)) / diag

    s = sweep(grad / diag, s_below1, s_above1, columns[:, 0:1], columns[:, 1:2])
    out_ref[...] = sweep(s, n_below, n_above, columns[:, 2:3], columns[:, 3:4])


def swaps(size):
    out = []
    for first in (0, 1):
        pairs = [(i, i + 1) for i in range(first, size - 1, 2)]
        out.append(pairs + [(j, i) for i, j in pairs])
    return out


def swap_over(array, axis, pairs):
    return lax.ppermute(array, axis, pairs) if pairs else jnp.zeros_like(array)


def f32(*shape):
    return jax.ShapeDtypeStruct(shape, F32)


def call(kernel, name, out_shape, in_specs, scratch, moved):
    single = not isinstance(out_shape, tuple)
    return pl.pallas_call(
        kernel, out_shape=out_shape, in_specs=in_specs,
        out_specs=VMEM if single else (VMEM,) * len(out_shape), scratch_shapes=scratch, name=name,
        compiler_params=pltpu.CompilerParams(vmem_limit_bytes=LIMIT),
        cost_estimate=pl.CostEstimate(flops=1_000_000, bytes_accessed=moved, transcendentals=0),
    )


LIMIT = 6 * 1024 * 1024


def on_device(loads, dual_op, iface, precond, corner_map, coarse_inv, elem_stiff, elem_dofs, density, passive):
    nx, ny = lax.axis_size("gx"), lax.axis_size("gy")
    everyone = nx * ny
    unknowns = dual_op.shape[-1]
    modes = corner_map.shape[1]
    ex, ey = density.shape
    tiles = ex // 8
    x_even, x_odd = swaps(nx)
    y_even, y_odd = swaps(ny)

    def held(array):
        return pltpu.VMEM(array.shape, array.dtype)

    def copies(n):
        return pltpu.SemaphoreType.DMA((n,))

    stiff = pltpu.SMEM(elem_stiff.shape, F32)
    table = pltpu.VMEM((CASES, 8, 8, LANES), F32)
    gathered = pltpu.VMEM((8, CASES, 8, LANES), F32)

    send = call(first_kernel, "first", f32(everyone, CASES, modes), [HBM] * 3,
                [held(loads), held(precond), held(corner_map), copies(3)], 4_000_000,
                )(loads, precond, corner_map)
    got = lax.all_to_all(send, ("gx", "gy"), 0, 0)

    side = f32(SIDE_C + modes, R)
    keep, mine_e, mine_o, inverse = call(
        side_kernel, "sides",
        (f32(KEEP_S + 8, unknowns), side, side, jax.ShapeDtypeStruct((2, 8, unknowns), jnp.int32)),
        [HBM] * 5,
        [held(loads), held(dual_op), held(iface), held(precond), held(corner_map), copies(5)], 8_000_000,
    )(loads, dual_op, iface, precond, corner_map)
    theirs_e = swap_over(mine_e, "gx", x_even)
    theirs_o = swap_over(mine_o, "gx", x_odd)

    kp, pp, pack, weight = call(
        p_kernel, "pfields",
        (f32(tiles + 1, 8, CASES, 8, LANES), f32(tiles + 1, CASES, 8, LANES),
         jax.ShapeDtypeStruct((8, 8, LANES), jnp.int32), f32(tiles + 1, 8, LANES)),
        [VMEM] * 2 + [HBM] * 3, [table, gathered, stiff, held(density), held(passive), copies(3)], 24_000_000,
    )(keep, elem_dofs, elem_stiff, density, passive)
    got, pack = lax.optimization_barrier((got, pack))

    send, t = call(
        second_kernel, "second", (f32(everyone, 2 * CASES, modes), f32(CASES, unknowns)),
        [VMEM] * 10 + [HBM], [held(precond), copies(1)], 9_000_000,
    )(got, keep, mine_e, mine_o, theirs_e, theirs_o, inverse, coarse_inv, corner_map, dual_op, precond)
    got = lax.all_to_all(send, ("gx", "gy"), 0, 0)

    row = f32(2 * FIELDS, LANES)
    col = f32(FIELDS, LANES)
    row_e, row_o, col_e, col_o = call(
        edge_kernel, "edges", (row, row, col, col), [VMEM] * 5 + [HBM],
        [table, gathered, pltpu.VMEM((FIELDS, 8, LANES), F32), stiff, copies(1)], 4_000_000,
    )(t, pack, kp, pp, weight, elem_stiff)
    near = [swap_over(row_e, "gx", x_even), swap_over(row_o, "gx", x_odd),
            swap_over(col_e, "gy", y_even), swap_over(col_o, "gy", y_odd)]
    for array, px in ((row_e, x_even), (row_o, x_odd)):
        for py in (y_even, y_odd):
            pairs = [(a * ny + c, b * ny + d) for a, b in px for c, d in py]
            near.append(swap_over(array, ("gx", "gy"), pairs))

    field = f32(tiles, CASES, 8, LANES)
    pt, tt = call(
        t_kernel, "tfields", (field, field), [VMEM] * 4 + [HBM], [table, gathered, stiff, copies(1)], 22_000_000,
    )(t, elem_dofs, kp, weight, elem_stiff)

    adjoint, sens = call(
        last_kernel, "last", (f32(CASES, 1, unknowns), f32(ex, ey)), [VMEM] * 17, [], 4_000_000,
    )(got, coarse_inv, keep, t, pp, pt, tt, col_e, col_o, *near)
    return adjoint, sens


def solution(mesh):
    placed = (
        P(None, "gy", "gx"),
        P("gy", "gx", None),
        P("gy", "gx", None),
        P("gy", "gx"),
        P("gy", None, "gx"),
        P(),
        P(),
        P(None, "gx", "gy"),
        P("gx", "gy"),
        P("gx", "gy"),
    )
    return jax.shard_map(
        on_device,
        mesh=mesh,
        in_specs=placed,
        out_specs=(P(None, "gy", "gx"), P("gx", "gy")),
        check_vma=False,
    )
```

time: 79.9 us -> 70.1 us (0.88)
  waiting for transfers between devices: 9.59 us -> 0.02 us
  Pallas kernels: 15.3 us -> 22.1 us
  local copies, waits for them, and re-layouts: 26.2 us -> 21 us
  other arithmetic: 3.02 us -> 0 us
  starting transfers between devices: 23.2 us -> 25 us
    all_to_all x2, waiting for transfers between devices: 9.58 us -> 0.01 us  [on_device(): got = lax.all_to_all(send, ('gx', 'gy'), 0, 0)]
    pallas_call x6 -> x7, Pallas kernels: 15.3 us -> 22.1 us  [the longest x1 6.82 us: on_device(): call(p_kernel, 'pfields', (f32(tiles + 1, 8, CASES, 8, LANES), f32(tiles...]
    slice x6 -> x0, local copies, waits for them, and re-layouts: 4.44 us -> none  [the longest x4 3.83 us: edge_pack(): cols = jnp.concatenate([array[..., :2], array[..., ey - 2:]], axis=-1)]
    transpose x2 -> x0, other arithmetic: 1.41 us -> none  [edge_pack(): jnp.swapaxes(cols, -1, -2)]
    ppermute x7, starting transfers between devices: 12.3 us -> 13.2 us  [swap_over(): return lax.ppermute(array, axis, pairs) if pairs else jnp.zeros_like(array)]
    all_to_all x2, starting transfers between devices: 10.9 us -> 11.8 us  [on_device(): got = lax.all_to_all(send, ('gx', 'gy'), 0, 0)]
    concatenate x2 -> x0, other arithmetic: 0.83 us -> none  [edge_pack(): return jnp.concatenate([rows, cols, pad], axis=-2)]
    unnamed x58 -> x70, local copies, waits for them, and re-layouts: 20.8 us -> 21 us
  transfers between devices with their start and end apart: 9 -> 9, of which waited for: 1 -> 0; matrix products, arithmetic and copies ran while one was open for 15% -> 0% of each run, Pallas kernels for 8% -> 23%
where the time goes in v2:
time: 70.1 us; the launch traced here: 69 us
  starting transfers between devices  25 us (36%)
  Pallas kernels  22.1 us (32%)
  local copies, waits for them, and re-layouts  21 us (30%)
  between operations  0.92 us (1%)
    unnamed x70, local copies, waits for them, and re-layouts  21 us
    ppermute x7, starting transfers between devices, swap_over(): return lax.ppermute(array, axis, pairs) if pairs else jnp.zeros_like(array)  13.2 us
    all_to_all x2, starting transfers between devices, on_device(): got = lax.all_to_all(send, ('gx', 'gy'), 0, 0)  11.8 us
    pallas_call x1, Pallas kernels, on_device(): call(p_kernel, 'pfields', (f32(tiles + 1, 8, CASES, 8, LANES), f32(tiles...  6.82 us
    pallas_call x1, Pallas kernels, on_device(): call(t_kernel, 'tfields', (field, field), [VMEM] * 4 + [HBM], [table, gat...  5.88 us
    pallas_call x1, Pallas kernels, on_device(): call(second_kernel, 'second', (f32(everyone, 2 * CASES, modes), f32(CASES...  3.11 us
    pallas_call x1, Pallas kernels, on_device(): call(side_kernel, 'sides', (f32(KEEP_S + 8, unknowns), side, side, jax.Sh...  2.2 us
    pallas_call x1, Pallas kernels, on_device(): call(last_kernel, 'last', (f32(CASES, 1, unknowns), f32(ex, ey)), [VMEM]...  1.49 us
  transfers between devices with their start and end apart: 9, of which 0 were waited for; matrix products, arithmetic and copies ran while one was open for 0% of the time, Pallas kernels for 23%

profile of v2, /device:TPU:1, one launch (start us, length us, event | category | flops | bytes accessed | tf_op | source)
XLA Modules:
  0.0 69.0 jit_solution(12196464804953310447)
XLA Ops:
  0.6 1.0 %copy-done.2 = f32[1,128,1024]{2,1,0:T(8,128)S(1)} copy-done((f32[1,128,1024]{2,1,0:T(8,128)S(1)}, f32[1,128,1024]{2,1,0:T(8,128)}, u32[]{:S(2)}) %copy-start.2) | copy-done | bytes 524312
  1.7 0.8 %copy-done.16 = f32[8,1,1024]{2,1,0:T(1,128)S(1)} copy-done((f32[8,1,1024]{2,1,0:T(1,128)S(1)}, f32[8,1,1024]{2,1,0:T(1,128)}, u32[]{:S(2)}) %copy-start.16) | copy-done | bytes 32792
  2.4 0.7 copy-done.20
  3.1 1.3 %first.1 = f32[32,8,128]{2,1,0:T(8,128)} custom-call(f32[8,1,1024]{2,1,0:T(1,128)S(1)} %copy-done.16, f32[1,1024]{1,0:T(1,128)S(1)} %copy-done.20, f32[1,128,1024]{2,1,0:T(8,128)S(1)} %copy-done.2), custom_call_target="tpu_custom_call" | custom-call | flops 1000000 | bytes 4000000 | tf_op jit(solution)/shard_map/first/pallas_call | solution.py:444
  4.4 7.1 %all-to-all-start = ((f32[32,8,128]{2,1,0:T(8,128)}), f32[32,8,128]{2,1,0:T(8,128)S(1)}, u32[]{:S(2)}, u32[]{:S(2)}) async-start(f32[32,8,128]{2,1,0:T(8,128)} %first.1), calls=%async_computation | async-start | bytes 262144 | tf_op jit(solution)/shard_map/all_to_all | solution.py:447
  11.6 1.6 %copy-done = bf16[1,1024,1024]{2,1,0:T(8,128)(2,1)S(1)} copy-done((bf16[1,1024,1024]{2,1,0:T(8,128)(2,1)S(1)}, bf16[1,1024,1024]{2,1,0:T(8,128)(2,1)}, u32[]{:S(2)}) %copy-start) | copy-done | bytes 2097176
  13.1 1.0 %copy-done.3 = f32[1,128,1024]{2,1,0:T(8,128)S(1)} copy-done((f32[1,128,1024]{2,1,0:T(8,128)S(1)}, f32[1,128,1024]{2,1,0:T(8,128)}, u32[]{:S(2)}) %copy-start.3) | copy-done | bytes 524312
  14.2 0.8 %copy-done.17 = f32[8,1,1024]{2,1,0:T(1,128)S(1)} copy-done((f32[8,1,1024]{2,1,0:T(1,128)S(1)}, f32[8,1,1024]{2,1,0:T(1,128)}, u32[]{:S(2)}) %copy-start.17) | copy-done | bytes 32792
  14.9 0.7 copy-done.21
  16.3 2.2 %sides.1 = (f32[32,1024]{1,0:T(8,128)S(1)}, f32[152,128]{1,0:T(8,128)}, f32[152,128]{1,0:T(8,128)}, s32[2,8,1024]{2,1,0:T(8,128)S(1)}) custom-call(f32[8,1,1024]{2,1,0:T(1,128)S(1)} %copy-done.17, bf16[1,1024,1024]{2,1,0:T(8,128)(2,1)S(1)} %copy-done, s32[1,1,1024]{2,1,0:T(1,128)S(1)} %copy-done.34, f32[1,1024]{1,0:T(1,128)S(1)} %copy-done.21, ...), custom_call_target="tpu_custom_call" | custom-call | flops 1000000 | bytes 8000000 | tf_op jit(solution)/shard_map/sides/pallas_call | solution.py:450
  19.4 3.4 %collective-permute-start.1 = (f32[152,128]{1,0:T(8,128)}, f32[152,128]{1,0:T(8,128)}, u32[]{:S(2)}, u32[]{:S(2)}) collective-permute-start(f32[152,128]{1,0:T(8,128)} %get-tuple-element.24.mine_o_ref), channel_id=1, source_target_pairs={{2,4},{6,8},{10,12},{14,16},{18,20},{22,24},{26,28},{4,2},{8,6},{1... | collective-permute-start | bytes 233480 | tf_op jit(solution)/shard_map/ppermute | solution.py:404
  22.9 6.8 %pfields.1 = (f32[9,8,8,8,128]{4,3,2,1,0:T(8,128)S(1)}, f32[9,8,8,128]{3,2,1,0:T(8,128)S(1)}, s32[8,8,128]{2,1,0:T(8,128)S(1)}, f32[9,8,128]{2,1,0:T(8,128)S(1)}) custom-call(f32[32,1024]{1,0:T(8,128)S(1)} %get-tuple-element.20.keep_ref, s32[8,64,128]{2,1,0:T(8,128)S(1)} %copy-done.5, f32[8,8]{1,0:T(8,128)S(1)} %copy-done.23, f32[64,128]{1,0:T(8,128)S(1)} %copy-done.26, ...), custom_call_target="tpu_custom_call" | custom-call | flops 1000000 | bytes 24000000 | tf_op jit(solution)/shard_map/pfields/pallas_call | solution.py:459
  31.0 1.6 %copy-done.1 = bf16[1,1024,1024]{2,1,0:T(8,128)(2,1)S(1)} copy-done((bf16[1,1024,1024]{2,1,0:T(8,128)(2,1)S(1)}, bf16[1,1024,1024]{2,1,0:T(8,128)(2,1)}, u32[]{:S(2)}) %copy-start.1) | copy-done | bytes 2097176
  32.6 0.8 %copy-done.19 = s32[2,8,1024]{2,1,0:T(8,128)S(1)} copy-done((s32[2,8,1024]{2,1,0:T(8,128)S(1)}, s32[2,8,1024]{2,1,0:T(8,128)}, u32[]{:S(2)}) %copy-start.19) | copy-done | bytes 65560
  33.4 3.1 %second.1 = (f32[32,16,128]{2,1,0:T(8,128)S(1)}, f32[8,1024]{1,0:T(8,128)S(1)}) custom-call(f32[32,8,128]{2,1,0:T(8,128)S(1)} %all-to-all-done.got_ref, f32[32,1024]{1,0:T(8,128)S(1)} %get-tuple-element.20.keep_ref, f32[152,128]{1,0:T(8,128)} %get-tuple-element.23.mine_e_ref, f32[152,128]{1,0:T(8,128)} %get-tuple-element.24.mine_o_ref, ...), custom_call_target="tpu_custom_call" | custom-call | flops 1000000 | bytes 9000000 | tf_op jit(solution)/shard_map/second/pallas_call | solution.py:467
  36.5 0.7 %copy-done.8 = f32[32,16,128]{2,1,0:T(8,128)} copy-done((f32[32,16,128]{2,1,0:T(8,128)}, f32[32,16,128]{2,1,0:T(8,128)S(1)}, u32[]{:S(2)}) %copy-start.8) | copy-done | bytes 262168
  37.2 4.7 %all-to-all-start.1 = ((f32[32,16,128]{2,1,0:T(8,128)}), f32[32,16,128]{2,1,0:T(8,128)S(1)}, u32[]{:S(2)}, u32[]{:S(2)}) async-start(f32[32,16,128]{2,1,0:T(8,128)} %copy-done.8), calls=%async_computation.1 | async-start | bytes 524288 | tf_op jit(solution)/shard_map/all_to_all | solution.py:471
  41.9 0.8 %copy-done.14 = f32[9,8,128]{2,1,0:T(8,128)S(1)} copy-done((f32[9,8,128]{2,1,0:T(8,128)S(1)}, f32[9,8,128]{2,1,0:T(8,128)}, u32[]{:S(2)}) %copy-start.14) | copy-done | bytes 36888
  42.7 0.8 %copy-done.25 = s32[8,8,128]{2,1,0:T(8,128)S(1)} copy-done((s32[8,8,128]{2,1,0:T(8,128)S(1)}, s32[8,8,128]{2,1,0:T(8,128)}, u32[]{:S(2)}) %copy-start.25) | copy-done | bytes 32792
  43.4 1.3 %edges.1 = (f32[48,128]{1,0:T(8,128)S(1)}, f32[48,128]{1,0:T(8,128)S(1)}, f32[24,128]{1,0:T(8,128)S(1)}, f32[24,128]{1,0:T(8,128)S(1)}) custom-call(f32[8,1024]{1,0:T(8,128)S(1)} %get-tuple-element.27.t_ref, s32[8,8,128]{2,1,0:T(8,128)S(1)} %copy-done.25, f32[9,8,8,8,128]{4,3,2,1,0:T(8,128)S(1)} %get-tuple-element.29.kp_ref, ...), custom_call_target="tpu_custom_call" | custom-call | flops 1000000 | bytes 4000000 | tf_op jit(solution)/shard_map/edges/pallas_call | solution.py:475
  45.6 3.4 %collective-permute-start.3 = (f32[48,128]{1,0:T(8,128)S(1)}, f32[48,128]{1,0:T(8,128)S(1)}, u32[]{:S(2)}, u32[]{:S(2)}) collective-permute-start(f32[48,128]{1,0:T(8,128)S(1)} %get-tuple-element.37), channel_id=1, source_target_pairs={{2,4},{6,8},{10,12},{14,16},{18,20},{22,24},{26,28},{4,2},{8,6},{1... | collective-permute-start | bytes 73736 | tf_op jit(solution)/shard_map/ppermute | solution.py:404
  49.1 4.5 %collective-permute-start.6 = (f32[48,128]{1,0:T(8,128)S(1)}, f32[48,128]{1,0:T(8,128)S(1)}, u32[]{:S(2)}, u32[]{:S(2)}) collective-permute-start(f32[48,128]{1,0:T(8,128)S(1)} %get-tuple-element.37), channel_id=1, source_target_pairs={{2,5},{3,4},{6,9},{7,8},{10,13},{11,12},{14,17},{15,16},{18,21},{1... | collective-permute-start | bytes 73736 | tf_op jit(solution)/shard_map/ppermute | solution.py:404
  53.6 1.2 %collective-permute-start.4 = (f32[24,128]{1,0:T(8,128)S(1)}, f32[24,128]{1,0:T(8,128)S(1)}, u32[]{:S(2)}, u32[]{:S(2)}) collective-permute-start(f32[24,128]{1,0:T(8,128)S(1)} %get-tuple-element.34.mine_ye_ref), channel_id=1, source_target_pairs={{0,1},{1,0},{2,3},{3,2},{4,5},{5,4},{6,7},{7,6},{8,9},{9,8},{10,11... | collective-permute-start | bytes 36872 | tf_op jit(solution)/shard_map/ppermute | solution.py:404
  54.9 5.9 %tfields.1 = (f32[8,8,8,128]{3,2,1,0:T(8,128)S(1)}, f32[8,8,8,128]{3,2,1,0:T(8,128)S(1)}) custom-call(f32[8,1024]{1,0:T(8,128)S(1)} %get-tuple-element.27.t_ref, s32[8,64,128]{2,1,0:T(8,128)S(1)} %copy-done.6, f32[9,8,8,8,128]{4,3,2,1,0:T(8,128)S(1)} %get-tuple-element.29.kp_ref, f32[9,8,128]{2,1,0:T(8,128)S(1)} %copy-done.15, f32[8,8]{1,0:T(8,128)S(1)} %copy-done.23), custom_call_target="tpu_custom_call" | custom-call | flops 1000000 | bytes 22000000 | tf_op jit(solution)/shard_map/tfields/pallas_call | solution.py:487
  60.8 0.7 %copy-done.9 = f32[8,8,8,128]{3,2,1,0:T(8,128)} copy-done((f32[8,8,8,128]{3,2,1,0:T(8,128)}, f32[8,8,8,128]{3,2,1,0:T(8,128)S(1)}, u32[]{:S(2)}) %copy-start.9) | copy-done | bytes 262168
  61.5 0.7 %copy-done.11 = f32[8,8,8,128]{3,2,1,0:T(8,128)} copy-done((f32[8,8,8,128]{3,2,1,0:T(8,128)}, f32[8,8,8,128]{3,2,1,0:T(8,128)S(1)}, u32[]{:S(2)}) %copy-start.11) | copy-done | bytes 262168
  63.5 0.9 %copy-done.10 = f32[8,8,8,128]{3,2,1,0:T(8,128)S(1)} copy-done((f32[8,8,8,128]{3,2,1,0:T(8,128)S(1)}, f32[8,8,8,128]{3,2,1,0:T(8,128)}, u32[]{:S(2)}) %copy-start.10) | copy-done | bytes 262168
  64.4 0.9 %copy-done.12 = f32[8,8,8,128]{3,2,1,0:T(8,128)S(1)} copy-done((f32[8,8,8,128]{3,2,1,0:T(8,128)S(1)}, f32[8,8,8,128]{3,2,1,0:T(8,128)}, u32[]{:S(2)}) %copy-start.12) | copy-done | bytes 262168
  65.3 0.7 %copy-done.29 = f32[48,128]{1,0:T(8,128)S(1)} copy-done((f32[48,128]{1,0:T(8,128)S(1)}, f32[48,128]{1,0:T(8,128)}, u32[]{:S(2)}) %copy-start.29) | copy-done | bytes 24600
  66.1 0.7 %copy-done.31 = f32[24,128]{1,0:T(8,128)S(1)} copy-done((f32[24,128]{1,0:T(8,128)S(1)}, f32[24,128]{1,0:T(8,128)}, u32[]{:S(2)}) %copy-start.31) | copy-done | bytes 12312
  66.8 0.7 %copy-done.33 = f32[24,128]{1,0:T(8,128)S(1)} copy-done((f32[24,128]{1,0:T(8,128)S(1)}, f32[24,128]{1,0:T(8,128)}, u32[]{:S(2)}) %copy-start.33) | copy-done | bytes 12312
  67.5 1.5 %last.1 = (f32[8,1,1024]{2,1,0:T(1,128)}, f32[64,128]{1,0:T(8,128)}) custom-call(f32[32,16,128]{2,1,0:T(8,128)S(1)} %all-to-all-done.1.got_ref, f32[128,128]{1,0:T(8,128)S(1)} %copy-done.7, f32[32,1024]{1,0:T(8,128)S(1)} %get-tuple-element.20.keep_ref, f32[8,1024]{1,0:T(8,128)S(1)} %get-tuple-element.27.t_ref, ...), custom_call_target="tpu_custom_call" | custom-call | flops 1000000 | bytes 4000000 | tf_op jit(solution)/shard_map/last/pallas_call | solution.py:491
  (65 shorter events, 5.0 us)
Async XLA Ops:
  0.6 1.0 %copy-start.2 = (f32[1,128,1024]{2,1,0:T(8,128)S(1)}, f32[1,128,1024]{2,1,0:T(8,128)}, u32[]{:S(2)}) copy-start(f32[1,128,1024]{2,1,0:T(8,128)} %corner_ref.1) | copy-start | bytes 1572868
  1.7 0.8 %copy-start.16 = (f32[8,1,1024]{2,1,0:T(1,128)S(1)}, f32[8,1,1024]{2,1,0:T(1,128)}, u32[]{:S(2)}) copy-start(f32[8,1,1024]{2,1,0:T(1,128)} %loads_hbm.3) | copy-start | bytes 98308
  3.1 19.7 %copy-start.23 = (f32[8,8]{1,0:T(8,128)S(1)}, f32[8,8]{1,0:T(8,128)}, u32[]{:S(2)}) copy-start(f32[8,8]{1,0:T(8,128)} %stiff_hbm.5) | copy-start | bytes 772
  3.1 27.8 %copy-start.4 = (f32[1,128,1024]{2,1,0:T(8,128)S(1)}, f32[1,128,1024]{2,1,0:T(8,128)}, u32[]{:S(2)}) copy-start(f32[1,128,1024]{2,1,0:T(8,128)} %corner_ref.1) | copy-start | bytes 1572868
  3.1 27.8 %copy-start.7 = (f32[128,128]{1,0:T(8,128)S(1)}, f32[128,128]{1,0:T(8,128)}, u32[]{:S(2)}) copy-start(f32[128,128]{1,0:T(8,128)} %coarse_ref.3) | copy-start | bytes 196612
  3.1 27.8 %copy-start.22 = (f32[1,1024]{1,0:T(1,128)S(1)}, f32[1,1024]{1,0:T(1,128)}, u32[]{:S(2)}) copy-start(f32[1,1024]{1,0:T(1,128)} %pre_hbm.5) | copy-start | bytes 12292
  4.4 26.5 %all-to-all-start = ((f32[32,8,128]{2,1,0:T(8,128)}), f32[32,8,128]{2,1,0:T(8,128)S(1)}, u32[]{:S(2)}, u32[]{:S(2)}) async-start(f32[32,8,128]{2,1,0:T(8,128)} %first.1), calls=%async_computation | async-start | bytes 262144 | tf_op jit(solution)/shard_map/all_to_all | solution.py:447
  11.5 1.6 %copy-start = (bf16[1,1024,1024]{2,1,0:T(8,128)(2,1)S(1)}, bf16[1,1024,1024]{2,1,0:T(8,128)(2,1)}, u32[]{:S(2)}) copy-start(bf16[1,1024,1024]{2,1,0:T(8,128)(2,1)} %op_ref.1) | copy-start | bytes 6291460
  13.1 1.0 %copy-start.3 = (f32[1,128,1024]{2,1,0:T(8,128)S(1)}, f32[1,128,1024]{2,1,0:T(8,128)}, u32[]{:S(2)}) copy-start(f32[1,128,1024]{2,1,0:T(8,128)} %corner_ref.1) | copy-start | bytes 1572868
  14.2 0.8 %copy-start.17 = (f32[8,1,1024]{2,1,0:T(1,128)S(1)}, f32[8,1,1024]{2,1,0:T(1,128)}, u32[]{:S(2)}) copy-start(f32[8,1,1024]{2,1,0:T(1,128)} %loads_hbm.3) | copy-start | bytes 98308
  16.3 6.5 %copy-start.5 = (s32[8,64,128]{2,1,0:T(8,128)S(1)}, s32[8,64,128]{2,1,0:T(8,128)}, u32[]{:S(2)}) copy-start(s32[8,64,128]{2,1,0:T(8,128)} %dofs_ref.3) | copy-start | bytes 786436
  16.3 6.5 %copy-start.26 = (f32[64,128]{1,0:T(8,128)S(1)}, f32[64,128]{1,0:T(8,128)}, u32[]{:S(2)}) copy-start(f32[64,128]{1,0:T(8,128)} %density_hbm.1) | copy-start | bytes 98308
  16.3 6.5 %copy-start.27 = (s32[64,128]{1,0:T(8,128)S(1)}, s32[64,128]{1,0:T(8,128)}, u32[]{:S(2)}) copy-start(s32[64,128]{1,0:T(8,128)} %passive_hbm.1) | copy-start | bytes 98308
  19.1 11.8 %collective-permute-start = (f32[152,128]{1,0:T(8,128)}, f32[152,128]{1,0:T(8,128)}, u32[]{:S(2)}, u32[]{:S(2)}) collective-permute-start(f32[152,128]{1,0:T(8,128)} %get-tuple-element.23.mine_e_ref), channel_id=1, source_target_pairs={{0,2},{4,6},{8,10},{12,14},{16,18},{20,22},{24,26},{28,30},{2,0},{... | collective-permute-start | bytes 233480 | tf_op jit(solution)/shard_map/ppermute | solution.py:404
  19.4 11.5 %collective-permute-start.1 = (f32[152,128]{1,0:T(8,128)}, f32[152,128]{1,0:T(8,128)}, u32[]{:S(2)}, u32[]{:S(2)}) collective-permute-start(f32[152,128]{1,0:T(8,128)} %get-tuple-element.24.mine_o_ref), channel_id=1, source_target_pairs={{2,4},{6,8},{10,12},{14,16},{18,20},{22,24},{26,28},{4,2},{8,6},{1... | collective-permute-start | bytes 233480 | tf_op jit(solution)/shard_map/ppermute | solution.py:404
  31.0 1.6 %copy-start.1 = (bf16[1,1024,1024]{2,1,0:T(8,128)(2,1)S(1)}, bf16[1,1024,1024]{2,1,0:T(8,128)(2,1)}, u32[]{:S(2)}) copy-start(bf16[1,1024,1024]{2,1,0:T(8,128)(2,1)} %op_ref.1) | copy-start | bytes 6291460
  32.5 0.8 %copy-start.19 = (s32[2,8,1024]{2,1,0:T(8,128)S(1)}, s32[2,8,1024]{2,1,0:T(8,128)}, u32[]{:S(2)}) copy-start(s32[2,8,1024]{2,1,0:T(8,128)} %copy-done.18) | copy-start | bytes 196612
  37.2 17.7 %copy-start.6 = (s32[8,64,128]{2,1,0:T(8,128)S(1)}, s32[8,64,128]{2,1,0:T(8,128)}, u32[]{:S(2)}) copy-start(s32[8,64,128]{2,1,0:T(8,128)} %dofs_ref.3) | copy-start | bytes 786436
  37.2 17.7 %copy-start.15 = (f32[9,8,128]{2,1,0:T(8,128)S(1)}, f32[9,8,128]{2,1,0:T(8,128)}, u32[]{:S(2)}) copy-start(f32[9,8,128]{2,1,0:T(8,128)} %copy-done.13) | copy-start | bytes 110596
  37.2 26.2 %all-to-all-start.1 = ((f32[32,16,128]{2,1,0:T(8,128)}), f32[32,16,128]{2,1,0:T(8,128)S(1)}, u32[]{:S(2)}, u32[]{:S(2)}) async-start(f32[32,16,128]{2,1,0:T(8,128)} %copy-done.8), calls=%async_computation.1 | async-start | bytes 524288 | tf_op jit(solution)/shard_map/all_to_all | solution.py:471
  41.9 0.8 %copy-start.14 = (f32[9,8,128]{2,1,0:T(8,128)S(1)}, f32[9,8,128]{2,1,0:T(8,128)}, u32[]{:S(2)}) copy-start(f32[9,8,128]{2,1,0:T(8,128)} %copy-done.13) | copy-start | bytes 110596
  42.7 0.8 %copy-start.25 = (s32[8,8,128]{2,1,0:T(8,128)S(1)}, s32[8,8,128]{2,1,0:T(8,128)}, u32[]{:S(2)}) copy-start(s32[8,8,128]{2,1,0:T(8,128)} %copy-done.24) | copy-start | bytes 98308
  45.3 17.5 %collective-permute-start.2 = (f32[48,128]{1,0:T(8,128)S(1)}, f32[48,128]{1,0:T(8,128)S(1)}, u32[]{:S(2)}, u32[]{:S(2)}) collective-permute-start(f32[48,128]{1,0:T(8,128)S(1)} %get-tuple-element.36), channel_id=1, source_target_pairs={{0,2},{4,6},{8,10},{12,14},{16,18},{20,22},{24,26},{28,30},{2,0},{... | collective-permute-start | bytes 73736 | tf_op jit(solution)/shard_map/ppermute | solution.py:404
  45.6 17.2 %collective-permute-start.3 = (f32[48,128]{1,0:T(8,128)S(1)}, f32[48,128]{1,0:T(8,128)S(1)}, u32[]{:S(2)}, u32[]{:S(2)}) collective-permute-start(f32[48,128]{1,0:T(8,128)S(1)} %get-tuple-element.37), channel_id=1, source_target_pairs={{2,4},{6,8},{10,12},{14,16},{18,20},{22,24},{26,28},{4,2},{8,6},{1... | collective-permute-start | bytes 73736 | tf_op jit(solution)/shard_map/ppermute | solution.py:404
  49.0 13.8 %collective-permute-start.5 = (f32[48,128]{1,0:T(8,128)S(1)}, f32[48,128]{1,0:T(8,128)S(1)}, u32[]{:S(2)}, u32[]{:S(2)}) collective-permute-start(f32[48,128]{1,0:T(8,128)S(1)} %get-tuple-element.36), channel_id=1, source_target_pairs={{0,3},{1,2},{4,7},{5,6},{8,11},{9,10},{12,15},{13,14},{16,19},{17,... | collective-permute-start | bytes 73736 | tf_op jit(solution)/shard_map/ppermute | solution.py:404
  49.1 13.7 %collective-permute-start.6 = (f32[48,128]{1,0:T(8,128)S(1)}, f32[48,128]{1,0:T(8,128)S(1)}, u32[]{:S(2)}, u32[]{:S(2)}) collective-permute-start(f32[48,128]{1,0:T(8,128)S(1)} %get-tuple-element.37), channel_id=1, source_target_pairs={{2,5},{3,4},{6,9},{7,8},{10,13},{11,12},{14,17},{15,16},{18,21},{1... | collective-permute-start | bytes 73736 | tf_op jit(solution)/shard_map/ppermute | solution.py:404
  53.6 8.6 %collective-permute-start.4 = (f32[24,128]{1,0:T(8,128)S(1)}, f32[24,128]{1,0:T(8,128)S(1)}, u32[]{:S(2)}, u32[]{:S(2)}) collective-permute-start(f32[24,128]{1,0:T(8,128)S(1)} %get-tuple-element.34.mine_ye_ref), channel_id=1, source_target_pairs={{0,1},{1,0},{2,3},{3,2},{4,5},{5,4},{6,7},{7,6},{8,9},{9,8},{10,11... | collective-permute-start | bytes 36872 | tf_op jit(solution)/shard_map/ppermute | solution.py:404
  61.5 0.7 %copy-start.11 = (f32[8,8,8,128]{3,2,1,0:T(8,128)}, f32[8,8,8,128]{3,2,1,0:T(8,128)S(1)}, u32[]{:S(2)}) copy-start(f32[8,8,8,128]{3,2,1,0:T(8,128)S(1)} %get-tuple-element.32.tt_ref) | copy-start | bytes 786436
  63.4 1.0 %copy-start.10 = (f32[8,8,8,128]{3,2,1,0:T(8,128)S(1)}, f32[8,8,8,128]{3,2,1,0:T(8,128)}, u32[]{:S(2)}) copy-start(f32[8,8,8,128]{3,2,1,0:T(8,128)} %copy-done.9) | copy-start | bytes 786436
  64.4 0.9 %copy-start.12 = (f32[8,8,8,128]{3,2,1,0:T(8,128)S(1)}, f32[8,8,8,128]{3,2,1,0:T(8,128)}, u32[]{:S(2)}) copy-start(f32[8,8,8,128]{3,2,1,0:T(8,128)} %copy-done.11) | copy-start | bytes 786436
  65.3 0.7 %copy-start.29 = (f32[48,128]{1,0:T(8,128)S(1)}, f32[48,128]{1,0:T(8,128)}, u32[]{:S(2)}) copy-start(f32[48,128]{1,0:T(8,128)} %copy-done.28) | copy-start | bytes 73732
  66.8 0.7 %copy-start.33 = (f32[24,128]{1,0:T(8,128)S(1)}, f32[24,128]{1,0:T(8,128)}, u32[]{:S(2)}) copy-start(f32[24,128]{1,0:T(8,128)} %copy-done.32) | copy-start | bytes 36868
  (12 other events, 7.8 us)

commit v3 on v2

--- a/solution.py
+++ b/solution.py
@@ -140,8 +140,8 @@
 
 
 def second_kernel(got_ref, keep_ref, mine_e_ref, mine_o_ref, theirs_e_ref, theirs_o_ref, inverse_ref,
-                  coarse_ref, corner_ref, op_ref, pre_hbm, send_ref, t_ref, pre_ref, sems):
-    copies = fetch(sems, ((pre_hbm, pre_ref),))
+                  coarse_ref, corner_ref, pre_hbm, op_hbm, send_ref, t_ref, pre_ref, op_ref, sems):
+    copies = fetch(sems, ((pre_hbm, pre_ref), (op_hbm, op_ref)))
     total = got_ref[0]
     for d in range(1, got_ref.shape[0]):
         total = total + got_ref[d]
@@ -165,6 +165,7 @@
         t_theirs = t_theirs + plain_dot(w, theirs[SIDE_C:])
         term = -coupling * lane_sum(t_mine * t_theirs)
         tlt = term if tlt is None else tlt + term
+    copies[1].wait()
     both = lax.dot_general(halves(t), op_ref[0], (((1,), (1,)), ((), ())), preferred_element_type=F32)
     tlt = tlt + lane_sum(t * (both[:CASES] + both[CASES:]))
     rest = keep_ref[KEEP_REST : KEEP_REST + 8]
@@ -208,7 +209,8 @@
 
 
 def p_kernel(keep_ref, dofs_ref, stiff_hbm, density_hbm, passive_hbm,
-             kp_ref, pp_ref, pack_ref, weight_ref, table_ref, u_ref, stiff_ref, density_ref, passive_ref, sems):
+             kp_hbm, pp_ref, pack_ref, weight_ref,
+             table_ref, u_ref, kp_ref, stiff_ref, density_ref, passive_ref, sems, kp_sems):
     copies = fetch(sems, ((stiff_hbm, stiff_ref), (density_hbm, density_ref), (passive_hbm, passive_ref)))
     make_table(table_ref, keep_ref[KEEP_P : KEEP_P + 8])
     for a in range(0, 8, 2):
@@ -235,6 +237,7 @@
                 kp_ref[tile, a, c] = v
                 pp = u[a] * v if pp is None else pp + u[a] * v
             pp_ref[tile, c] = scale * pp
+        pltpu.make_async_copy(kp_ref.at[tile], kp_hbm.at[tile], kp_sems.at[tile]).start()
 
     @pl.loop(0, count)
     def _(tile):
@@ -242,6 +245,8 @@
         work(lambda a: dofs_ref[a, rows, :], tile)
 
     work(lambda a: pack_ref[a], count)
+    for i in range(count + 1):
+        pltpu.make_async_copy(kp_ref.at[i], kp_hbm.at[i], kp_sems.at[i]).wait()
 
 
 def t_fields(stiff_ref, kp, scale, u_ref, c):
@@ -256,15 +261,16 @@
     return scale * pt, scale * tt
 
 
-def edge_kernel(t_ref, pack_ref, kp_ref, pp_ref, weight_ref, stiff_hbm,
-                row_e_ref, row_o_ref, col_e_ref, col_o_ref, table_ref, u_ref, field_ref, stiff_ref, sems):
-    copies = fetch(sems, ((stiff_hbm, stiff_ref),))
+def edge_kernel(t_ref, pack_ref, pp_ref, weight_ref, kp_hbm, stiff_hbm,
+                row_e_ref, row_o_ref, col_e_ref, col_o_ref, table_ref, u_ref, kp_ref, field_ref, stiff_ref, sems):
+    tile = kp_hbm.shape[0] - 1
+    copies = fetch(sems, ((stiff_hbm, stiff_ref), (kp_hbm.at[tile], kp_ref)))
     make_table(table_ref, t_ref[...])
     gather_tile(lambda a: pack_ref[a], table_ref, u_ref)
-    copies[0].wait()
-    tile = kp_ref.shape[0] - 1
+    for copy in copies:
+        copy.wait()
     for c in range(CASES):
-        pt, tt = t_fields(stiff_ref, lambda a, c: kp_ref[tile, a, c], weight_ref[tile], u_ref, c)
+        pt, tt = t_fields(stiff_ref, lambda a, c: kp_ref[a, c], weight_ref[tile], u_ref, c)
         field_ref[c] = pp_ref[tile, c]
         field_ref[CASES + c] = pt
         field_ref[2 * CASES + c] = tt
@@ -279,15 +285,19 @@
     col_o_ref[...] = jnp.where(y_odd, high, low)
 
 
-def t_kernel(t_ref, dofs_ref, kp_ref, weight_ref, stiff_hbm, pt_ref, tt_ref, table_ref, u_ref, stiff_ref, sems):
+def t_kernel(t_ref, dofs_ref, weight_ref, kp_hbm, stiff_hbm, pt_ref, tt_ref,
+             table_ref, u_ref, kp_ref, stiff_ref, sems, kp_sems):
+    count = pt_ref.shape[0]
     copies = fetch(sems, ((stiff_hbm, stiff_ref),))
+    fetch(kp_sems, [(kp_hbm.at[i], kp_ref.at[i]) for i in range(count)])
     make_table(table_ref, t_ref[...])
     copies[0].wait()
 
-    @pl.loop(0, pt_ref.shape[0])
+    @pl.loop(0, count)
     def _(tile):
         rows = pl.ds(pl.multiple_of(8 * tile, 8), 8)
         gather_tile(lambda a: dofs_ref[a, rows, :], table_ref, u_ref)
+        pltpu.make_async_copy(kp_hbm.at[tile], kp_ref.at[tile], kp_sems.at[tile]).wait()
         for c in range(CASES):
             pt_ref[tile, c], tt_ref[tile, c] = t_fields(
                 stiff_ref, lambda a, c: kp_ref[tile, a, c], weight_ref[tile], u_ref, c)
@@ -408,11 +418,11 @@
     return jax.ShapeDtypeStruct(shape, F32)
 
 
-def call(kernel, name, out_shape, in_specs, scratch, moved):
+def call(kernel, name, out_shape, in_specs, scratch, moved, first_in_hbm=False):
     single = not isinstance(out_shape, tuple)
     return pl.pallas_call(
         kernel, out_shape=out_shape, in_specs=in_specs,
-        out_specs=VMEM if single else (VMEM,) * len(out_shape), scratch_shapes=scratch, name=name,
+        out_specs=VMEM if single else (HBM if first_in_hbm else VMEM,) + (VMEM,) * (len(out_shape) - 1), scratch_shapes=scratch, name=name,
         compiler_params=pltpu.CompilerParams(vmem_limit_bytes=LIMIT),
         cost_estimate=pl.CostEstimate(flops=1_000_000, bytes_accessed=moved, transcendentals=0),
     )
@@ -434,6 +444,9 @@
     def held(array):
         return pltpu.VMEM(array.shape, array.dtype)
 
+    def in_hbm(array):
+        return pltpu.with_memory_space_constraint(array, pltpu.HBM)
+
     def copies(n):
         return pltpu.SemaphoreType.DMA((n,))
 
@@ -443,7 +456,7 @@
 
     send = call(first_kernel, "first", f32(everyone, CASES, modes), [HBM] * 3,
                 [held(loads), held(precond), held(corner_map), copies(3)], 4_000_000,
-                )(loads, precond, corner_map)
+                )(in_hbm(loads), in_hbm(precond), in_hbm(corner_map))
     got = lax.all_to_all(send, ("gx", "gy"), 0, 0)
 
     side = f32(SIDE_C + modes, R)
@@ -452,30 +465,32 @@
         (f32(KEEP_S + 8, unknowns), side, side, jax.ShapeDtypeStruct((2, 8, unknowns), jnp.int32)),
         [HBM] * 5,
         [held(loads), held(dual_op), held(iface), held(precond), held(corner_map), copies(5)], 8_000_000,
-    )(loads, dual_op, iface, precond, corner_map)
+    )(*(in_hbm(a) for a in (loads, dual_op, iface, precond, corner_map)))
     theirs_e = swap_over(mine_e, "gx", x_even)
     theirs_o = swap_over(mine_o, "gx", x_odd)
 
     kp, pp, pack, weight = call(
         p_kernel, "pfields",
-        (f32(tiles + 1, 8, CASES, 8, LANES), f32(tiles + 1, CASES, 8, LANES),
+        (pltpu.HBM((tiles + 1, 8, CASES, 8, LANES), F32), f32(tiles + 1, CASES, 8, LANES),
          jax.ShapeDtypeStruct((8, 8, LANES), jnp.int32), f32(tiles + 1, 8, LANES)),
-        [VMEM] * 2 + [HBM] * 3, [table, gathered, stiff, held(density), held(passive), copies(3)], 24_000_000,
-    )(keep, elem_dofs, elem_stiff, density, passive)
+        [VMEM] * 2 + [HBM] * 3,
+        [table, gathered, pltpu.VMEM((tiles + 1, 8, CASES, 8, LANES), F32), stiff, held(density), held(passive),
+         copies(3), copies(tiles + 1)], 24_000_000, first_in_hbm=True,
+    )(keep, elem_dofs, in_hbm(elem_stiff), in_hbm(density), in_hbm(passive))
     got, pack = lax.optimization_barrier((got, pack))
 
     send, t = call(
         second_kernel, "second", (f32(everyone, 2 * CASES, modes), f32(CASES, unknowns)),
-        [VMEM] * 10 + [HBM], [held(precond), copies(1)], 9_000_000,
-    )(got, keep, mine_e, mine_o, theirs_e, theirs_o, inverse, coarse_inv, corner_map, dual_op, precond)
+        [VMEM] * 9 + [HBM] * 2, [held(precond), held(dual_op), copies(2)], 9_000_000,
+    )(got, keep, mine_e, mine_o, theirs_e, theirs_o, inverse, coarse_inv, corner_map, in_hbm(precond), in_hbm(dual_op))
     got = lax.all_to_all(send, ("gx", "gy"), 0, 0)
 
     row = f32(2 * FIELDS, LANES)
     col = f32(FIELDS, LANES)
     row_e, row_o, col_e, col_o = call(
-        edge_kernel, "edges", (row, row, col, col), [VMEM] * 5 + [HBM],
-        [table, gathered, pltpu.VMEM((FIELDS, 8, LANES), F32), stiff, copies(1)], 4_000_000,
-    )(t, pack, kp, pp, weight, elem_stiff)
+        edge_kernel, "edges", (row, row, col, col), [VMEM] * 4 + [HBM] * 2,
+        [table, gathered, gathered, pltpu.VMEM((FIELDS, 8, LANES), F32), stiff, copies(2)], 4_000_000,
+    )(t, pack, pp, weight, in_hbm(kp), in_hbm(elem_stiff))
     near = [swap_over(row_e, "gx", x_even), swap_over(row_o, "gx", x_odd),
             swap_over(col_e, "gy", y_even), swap_over(col_o, "gy", y_odd)]
     for array, px in ((row_e, x_even), (row_o, x_odd)):
@@ -485,8 +500,9 @@
 
     field = f32(tiles, CASES, 8, LANES)
     pt, tt = call(
-        t_kernel, "tfields", (field, field), [VMEM] * 4 + [HBM], [table, gathered, stiff, copies(1)], 22_000_000,
-    )(t, elem_dofs, kp, weight, elem_stiff)
+        t_kernel, "tfields", (field, field), [VMEM] * 3 + [HBM] * 2,
+        [table, gathered, pltpu.VMEM((tiles, 8, CASES, 8, LANES), F32), stiff, copies(1), copies(tiles)], 22_000_000,
+    )(t, elem_dofs, weight, in_hbm(kp), in_hbm(elem_stiff))
 
     adjoint, sens = call(
         last_kernel, "last", (f32(CASES, 1, unknowns), f32(ex, ey)), [VMEM] * 17, [], 4_000_000,

time: 70.1 us -> 52.9 us (0.75)
  local copies, waits for them, and re-layouts: 21 us -> 0.02 us
  Pallas kernels: 22.1 us -> 26.4 us
    unnamed x70 -> x6, local copies, waits for them, and re-layouts: 21 us -> 0.01 us
    pallas_call x3, Pallas kernels: 14 us -> 16.6 us  [the longest x1 7.79 us: on_device(): call(p_kernel, 'pfields', (pltpu.HBM((tiles + 1, 8, CASES, 8, LANES), F32...]
    pallas_call x1, Pallas kernels: 1.29 us -> 2.36 us  [on_device(): call(first_kernel, 'first', f32(everyone, CASES, modes), [HBM] * 3, [held...]
  transfers between devices with their start and end apart: 9 -> 9, of which waited for: 0 -> 0; matrix products, arithmetic and copies ran while one was open for 0% -> 0% of each run, Pallas kernels for 23% -> 37%
where the time goes in v3:
time: 52.9 us; the launch traced here: 52.5 us
  Pallas kernels  26.4 us (50%)
  starting transfers between devices  25.1 us (47%)
  between operations  0.86 us (2%)
    ppermute x7, starting transfers between devices, swap_over(): return lax.ppermute(array, axis, pairs) if pairs else jnp.zeros_like(array)  13.3 us
    all_to_all x2, starting transfers between devices, on_device(): got = lax.all_to_all(send, ('gx', 'gy'), 0, 0)  11.8 us
    pallas_call x1, Pallas kernels, on_device(): call(p_kernel, 'pfields', (pltpu.HBM((tiles + 1, 8, CASES, 8, LANES), F32...  7.79 us
    pallas_call x1, Pallas kernels, on_device(): call(t_kernel, 'tfields', (field, field), [VMEM] * 3 + [HBM] * 2, [table,...  7.15 us
    pallas_call x1, Pallas kernels, on_device(): call(second_kernel, 'second', (f32(everyone, 2 * CASES, modes), f32(CASES...  3.35 us
    pallas_call x1, Pallas kernels, on_device(): call(side_kernel, 'sides', (f32(KEEP_S + 8, unknowns), side, side, jax.Sh...  2.6 us
    pallas_call x1, Pallas kernels, on_device(): call(first_kernel, 'first', f32(everyone, CASES, modes), [HBM] * 3, [held...  2.36 us
    pallas_call x1, Pallas kernels, on_device(): call(edge_kernel, 'edges', (row, row, col, col), [VMEM] * 4 + [HBM] * 2,...  1.66 us
  transfers between devices with their start and end apart: 9, of which 0 were waited for; matrix products, arithmetic and copies ran while one was open for 0% of the time, Pallas kernels for 37%

profile of v3, /device:TPU:1, one launch (start us, length us, event | category | flops | bytes accessed | tf_op | source)
XLA Modules:
  0.0 52.5 jit_solution(15300477722074091862)
XLA Ops:
  0.6 0.0 copy-start
  0.6 0.0 copy-start.1
  0.7 0.0 copy-start.2
  0.7 2.4 %first.1 = f32[32,8,128]{2,1,0:T(8,128)} custom-call(f32[8,1,1024]{2,1,0:T(1,128)} %loads_hbm.3, f32[1,1024]{1,0:T(1,128)} %pre_hbm.5, f32[1,128,1024]{2,1,0:T(8,128)} %corner_ref.1), custom_call_target="tpu_custom_call" | custom-call | flops 1000000 | bytes 4000000 | tf_op jit(solution)/shard_map/first/pallas_call | solution.py:457
  3.0 7.1 %all-to-all-start = ((f32[32,8,128]{2,1,0:T(8,128)}), f32[32,8,128]{2,1,0:T(8,128)S(1)}, u32[]{:S(2)}, u32[]{:S(2)}) async-start(f32[32,8,128]{2,1,0:T(8,128)} %first.1), calls=%async_computation | async-start | bytes 262144 | tf_op jit(solution)/shard_map/all_to_all | solution.py:460
  10.1 2.6 %sides.1 = (f32[32,1024]{1,0:T(8,128)S(1)}, f32[152,128]{1,0:T(8,128)S(1)}, f32[152,128]{1,0:T(8,128)S(1)}, s32[2,8,1024]{2,1,0:T(8,128)S(1)}) custom-call(f32[8,1,1024]{2,1,0:T(1,128)} %loads_hbm.3, bf16[1,1024,1024]{2,1,0:T(8,128)(2,1)} %op_hbm.3, s32[1,1,1024]{2,1,0:T(1,128)} %iface_hbm.1, f32[1,1024]{1,0:T(1,128)} %pre_hbm.5, f32[1,128,1024]{2,1,0:T(8,128)} %corner_ref.1), custom_call_target="tpu_custom_call" | custom-call | flops 1000000 | bytes 8000000 | tf_op jit(solution)/shard_map/sides/pallas_call | solution.py:463
  12.8 0.3 collective-permute-start
  13.1 3.4 %collective-permute-start.1 = (f32[152,128]{1,0:T(8,128)S(1)}, f32[152,128]{1,0:T(8,128)S(1)}, u32[]{:S(2)}, u32[]{:S(2)}) collective-permute-start(f32[152,128]{1,0:T(8,128)S(1)} %get-tuple-element.24.mine_o_ref), channel_id=1, source_target_pairs={{2,4},{6,8},{10,12},{14,16},{18,20},{22,24},{26,28},{4,2},{8,6},{1... | collective-permute-start | bytes 233480 | tf_op jit(solution)/shard_map/ppermute | solution.py:414
  16.5 0.0 copy-done.1
  16.5 7.8 %pfields.1 = (f32[9,8,8,8,128]{4,3,2,1,0:T(8,128)}, f32[9,8,8,128]{3,2,1,0:T(8,128)S(1)}, s32[8,8,128]{2,1,0:T(8,128)S(1)}, f32[9,8,128]{2,1,0:T(8,128)S(1)}) custom-call(f32[32,1024]{1,0:T(8,128)S(1)} %get-tuple-element.20.keep_ref, s32[8,64,128]{2,1,0:T(8,128)S(1)} %copy-done.1, f32[8,8]{1,0:T(8,128)} %stiff_hbm.5, f32[64,128]{1,0:T(8,128)} %density_hbm.1, ...), custom_call_target="tpu_custom_call" | custom-call | flops 1000000 | bytes 24000000 | tf_op jit(solution)/shard_map/pfields/pallas_call | solution.py:472
  24.3 0.0 all-to-all-done.got_ref
  24.3 0.0 collective-permute-done.theirs_e_ref
  24.3 0.0 collective-permute-done.1.theirs_o_ref
  24.3 0.0 copy-done
  24.4 0.0 copy-done.2
  24.4 3.3 %second.1 = (f32[32,16,128]{2,1,0:T(8,128)}, f32[8,1024]{1,0:T(8,128)S(1)}) custom-call(f32[32,8,128]{2,1,0:T(8,128)S(1)} %all-to-all-done.got_ref, f32[32,1024]{1,0:T(8,128)S(1)} %get-tuple-element.20.keep_ref, f32[152,128]{1,0:T(8,128)S(1)} %get-tuple-element.23.mine_e_ref, f32[152,128]{1,0:T(8,128)S(1)} %get-tuple-element.24.mine_o_ref, ...), custom_call_target="tpu_custom_call" | custom-call | flops 1000000 | bytes 9000000 | tf_op jit(solution)/shard_map/second/pallas_call | solution.py:482
  27.7 4.7 %all-to-all-start.1 = ((f32[32,16,128]{2,1,0:T(8,128)}), f32[32,16,128]{2,1,0:T(8,128)S(1)}, u32[]{:S(2)}, u32[]{:S(2)}) async-start(f32[32,16,128]{2,1,0:T(8,128)} %get-tuple-element.26), calls=%async_computation.1 | async-start | bytes 524288 | tf_op jit(solution)/shard_map/all_to_all | solution.py:486
  32.4 1.7 %edges.1 = (f32[48,128]{1,0:T(8,128)S(1)}, f32[48,128]{1,0:T(8,128)S(1)}, f32[24,128]{1,0:T(8,128)S(1)}, f32[24,128]{1,0:T(8,128)S(1)}) custom-call(f32[8,1024]{1,0:T(8,128)S(1)} %get-tuple-element.27.t_ref, s32[8,8,128]{2,1,0:T(8,128)S(1)} %get-tuple-element.33.pack_ref, f32[9,8,8,128]{3,2,1,0:T(8,128)S(1)} %get-tuple-element.28.pp_ref, ...), custom_call_target="tpu_custom_call" | custom-call | flops 1000000 | bytes 4000000 | tf_op jit(solution)/shard_map/edges/pallas_call | solution.py:490
  34.1 0.3 collective-permute-start.2
  34.4 3.4 %collective-permute-start.3 = (f32[48,128]{1,0:T(8,128)S(1)}, f32[48,128]{1,0:T(8,128)S(1)}, u32[]{:S(2)}, u32[]{:S(2)}) collective-permute-start(f32[48,128]{1,0:T(8,128)S(1)} %get-tuple-element.37), channel_id=1, source_target_pairs={{2,4},{6,8},{10,12},{14,16},{18,20},{22,24},{26,28},{4,2},{8,6},{1... | collective-permute-start | bytes 73736 | tf_op jit(solution)/shard_map/ppermute | solution.py:414
  37.8 0.1 collective-permute-start.5
  37.9 4.5 %collective-permute-start.6 = (f32[48,128]{1,0:T(8,128)S(1)}, f32[48,128]{1,0:T(8,128)S(1)}, u32[]{:S(2)}, u32[]{:S(2)}) collective-permute-start(f32[48,128]{1,0:T(8,128)S(1)} %get-tuple-element.37), channel_id=1, source_target_pairs={{2,5},{3,4},{6,9},{7,8},{10,13},{11,12},{14,17},{15,16},{18,21},{1... | collective-permute-start | bytes 73736 | tf_op jit(solution)/shard_map/ppermute | solution.py:414
  42.5 1.2 %collective-permute-start.4 = (f32[24,128]{1,0:T(8,128)S(1)}, f32[24,128]{1,0:T(8,128)S(1)}, u32[]{:S(2)}, u32[]{:S(2)}) collective-permute-start(f32[24,128]{1,0:T(8,128)S(1)} %get-tuple-element.34.mine_ye_ref), channel_id=1, source_target_pairs={{0,1},{1,0},{2,3},{3,2},{4,5},{5,4},{6,7},{7,6},{8,9},{9,8},{10,11... | collective-permute-start | bytes 36872 | tf_op jit(solution)/shard_map/ppermute | solution.py:414
  43.7 7.2 %tfields.1 = (f32[8,8,8,128]{3,2,1,0:T(8,128)S(1)}, f32[8,8,8,128]{3,2,1,0:T(8,128)S(1)}) custom-call(f32[8,1024]{1,0:T(8,128)S(1)} %get-tuple-element.27.t_ref, s32[8,64,128]{2,1,0:T(8,128)S(1)} %copy-done.1, f32[9,8,128]{2,1,0:T(8,128)S(1)} %get-tuple-element.29.weight_ref, f32[9,8,8,8,128]{4,3,2,1,0:T(8,128)} %get-tuple-element.30.kp_hbm, f32[8,8]{1,0:T(8,128)} %stiff_hbm.5), custom_call_target="tpu_custom_call" | custom-call | flops 1000000 | bytes 22000000 | tf_op jit(solution)/shard_map/tfields/pallas_call | solution.py:502
  50.9 0.0 collective-permute-done.4.ye_ref
  50.9 0.0 collective-permute-done.2.xe_ref
  50.9 0.0 collective-permute-done.3.xo_ref
  50.9 0.0 collective-permute-done.5.ee_ref
  50.9 0.0 collective-permute-done.6.oe_ref
  50.9 0.0 all-to-all-done.1.got_ref
  51.0 1.5 %last.1 = (f32[8,1,1024]{2,1,0:T(1,128)}, f32[64,128]{1,0:T(8,128)}) custom-call(f32[32,16,128]{2,1,0:T(8,128)S(1)} %all-to-all-done.1.got_ref, f32[128,128]{1,0:T(8,128)S(1)} %copy-done.2, f32[32,1024]{1,0:T(8,128)S(1)} %get-tuple-element.20.keep_ref, f32[8,1024]{1,0:T(8,128)S(1)} %get-tuple-element.27.t_ref, ...), custom_call_target="tpu_custom_call" | custom-call | flops 1000000 | bytes 4000000 | tf_op jit(solution)/shard_map/last/pallas_call | solution.py:507
  (2 shorter events, 0.0 us)
Async XLA Ops:
  0.6 23.7 %copy-start = (f32[1,128,1024]{2,1,0:T(8,128)S(1)}, f32[1,128,1024]{2,1,0:T(8,128)}, u32[]{:S(2)}) copy-start(f32[1,128,1024]{2,1,0:T(8,128)} %corner_ref.1) | copy-start | bytes 1572868
  0.6 15.9 %copy-start.1 = (s32[8,64,128]{2,1,0:T(8,128)S(1)}, s32[8,64,128]{2,1,0:T(8,128)}, u32[]{:S(2)}) copy-start(s32[8,64,128]{2,1,0:T(8,128)} %dofs_ref.3) | copy-start | bytes 786436
  0.7 23.7 %copy-start.2 = (f32[128,128]{1,0:T(8,128)S(1)}, f32[128,128]{1,0:T(8,128)}, u32[]{:S(2)}) copy-start(f32[128,128]{1,0:T(8,128)} %coarse_ref.3) | copy-start | bytes 196612
  3.0 21.3 %all-to-all-start = ((f32[32,8,128]{2,1,0:T(8,128)}), f32[32,8,128]{2,1,0:T(8,128)S(1)}, u32[]{:S(2)}, u32[]{:S(2)}) async-start(f32[32,8,128]{2,1,0:T(8,128)} %first.1), calls=%async_computation | async-start | bytes 262144 | tf_op jit(solution)/shard_map/all_to_all | solution.py:460
  12.8 11.6 %collective-permute-start = (f32[152,128]{1,0:T(8,128)S(1)}, f32[152,128]{1,0:T(8,128)S(1)}, u32[]{:S(2)}, u32[]{:S(2)}) collective-permute-start(f32[152,128]{1,0:T(8,128)S(1)} %get-tuple-element.23.mine_e_ref), channel_id=1, source_target_pairs={{0,2},{4,6},{8,10},{12,14},{16,18},{20,22},{24,26},{28,30},{2,0},{... | collective-permute-start | bytes 233480 | tf_op jit(solution)/shard_map/ppermute | solution.py:414
  13.1 11.3 %collective-permute-start.1 = (f32[152,128]{1,0:T(8,128)S(1)}, f32[152,128]{1,0:T(8,128)S(1)}, u32[]{:S(2)}, u32[]{:S(2)}) collective-permute-start(f32[152,128]{1,0:T(8,128)S(1)} %get-tuple-element.24.mine_o_ref), channel_id=1, source_target_pairs={{2,4},{6,8},{10,12},{14,16},{18,20},{22,24},{26,28},{4,2},{8,6},{1... | collective-permute-start | bytes 233480 | tf_op jit(solution)/shard_map/ppermute | solution.py:414
  27.7 23.2 %all-to-all-start.1 = ((f32[32,16,128]{2,1,0:T(8,128)}), f32[32,16,128]{2,1,0:T(8,128)S(1)}, u32[]{:S(2)}, u32[]{:S(2)}) async-start(f32[32,16,128]{2,1,0:T(8,128)} %get-tuple-element.26), calls=%async_computation.1 | async-start | bytes 524288 | tf_op jit(solution)/shard_map/all_to_all | solution.py:486
  34.1 16.8 %collective-permute-start.2 = (f32[48,128]{1,0:T(8,128)S(1)}, f32[48,128]{1,0:T(8,128)S(1)}, u32[]{:S(2)}, u32[]{:S(2)}) collective-permute-start(f32[48,128]{1,0:T(8,128)S(1)} %get-tuple-element.36), channel_id=1, source_target_pairs={{0,2},{4,6},{8,10},{12,14},{16,18},{20,22},{24,26},{28,30},{2,0},{... | collective-permute-start | bytes 73736 | tf_op jit(solution)/shard_map/ppermute | solution.py:414
  34.4 16.5 %collective-permute-start.3 = (f32[48,128]{1,0:T(8,128)S(1)}, f32[48,128]{1,0:T(8,128)S(1)}, u32[]{:S(2)}, u32[]{:S(2)}) collective-permute-start(f32[48,128]{1,0:T(8,128)S(1)} %get-tuple-element.37), channel_id=1, source_target_pairs={{2,4},{6,8},{10,12},{14,16},{18,20},{22,24},{26,28},{4,2},{8,6},{1... | collective-permute-start | bytes 73736 | tf_op jit(solution)/shard_map/ppermute | solution.py:414
  37.8 13.1 %collective-permute-start.5 = (f32[48,128]{1,0:T(8,128)S(1)}, f32[48,128]{1,0:T(8,128)S(1)}, u32[]{:S(2)}, u32[]{:S(2)}) collective-permute-start(f32[48,128]{1,0:T(8,128)S(1)} %get-tuple-element.36), channel_id=1, source_target_pairs={{0,3},{1,2},{4,7},{5,6},{8,11},{9,10},{12,15},{13,14},{16,19},{17,... | collective-permute-start | bytes 73736 | tf_op jit(solution)/shard_map/ppermute | solution.py:414
  37.9 13.0 %collective-permute-start.6 = (f32[48,128]{1,0:T(8,128)S(1)}, f32[48,128]{1,0:T(8,128)S(1)}, u32[]{:S(2)}, u32[]{:S(2)}) collective-permute-start(f32[48,128]{1,0:T(8,128)S(1)} %get-tuple-element.37), channel_id=1, source_target_pairs={{2,5},{3,4},{6,9},{7,8},{10,13},{11,12},{14,17},{15,16},{18,21},{1... | collective-permute-start | bytes 73736 | tf_op jit(solution)/shard_map/ppermute | solution.py:414
  42.5 8.4 %collective-permute-start.4 = (f32[24,128]{1,0:T(8,128)S(1)}, f32[24,128]{1,0:T(8,128)S(1)}, u32[]{:S(2)}, u32[]{:S(2)}) collective-permute-start(f32[24,128]{1,0:T(8,128)S(1)} %get-tuple-element.34.mine_ye_ref), channel_id=1, source_target_pairs={{0,1},{1,0},{2,3},{3,2},{4,5},{5,4},{6,7},{7,6},{8,9},{9,8},{10,11... | collective-permute-start | bytes 36872 | tf_op jit(solution)/shard_map/ppermute | solution.py:414

commit v4 on v2

--- a/solution.py
+++ b/solution.py
@@ -24,6 +24,7 @@
 RZ, PE, PQ, QMQ, TLT, TE = range(6)
 KEEP_P, KEEP_Y, KEEP_REST, KEEP_S = 0, 8, 16, 24
 FIELDS = 3 * CASES
+CORNER_PP, CORNER_PT, CORNER_TT = 8, 12, 16
 
 
 def rows_dot(a, b):
@@ -88,11 +89,42 @@
         send_ref[d] = part
 
 
-def side_kernel(loads_hbm, op_hbm, iface_hbm, pre_hbm, corner_hbm,
-                keep_ref, even_ref, odd_ref, inverse_ref,
-                loads_ref, op_ref, iface_ref, pre_ref, corner_ref, sems):
+def edge_tiles(first, second):
+    ex, ey = first.shape
+    lane = lax.broadcasted_iota(jnp.int32, (1, LANES), 1)
+    turned = jnp.transpose(jnp.concatenate([first, second], axis=0))
+    swapped = pltpu.roll(turned, LANES - ex, 1)
+    out = []
+    for array, low, high in ((first, turned, swapped), (second, swapped, turned)):
+        cols = [jnp.where(lane < ex, low[j : j + 1], high[j + 1 : j + 2]) for j in (0, ey - 2)]
+        out.append(jnp.concatenate([array[0:2], array[ex - 2 :]] + cols + [array[0:2]], axis=0))
+    return out
+
+
+def corner_lanes(low, high):
+    lane = lax.broadcasted_iota(jnp.int32, low.shape, 1)
+    out = jnp.where(lane == 0, low, jnp.where(lane == 1, pltpu.roll(low, 2, 1), 0))
+    return jnp.where(lane == 2, pltpu.roll(high, 2, 1), jnp.where(lane == 3, pltpu.roll(high, 4, 1), out))
+
+
+def corner_values(vec, where):
+    return [pick(blocks_of(vec), pattern(jnp.broadcast_to(where[a : a + 1], (8, LANES)))) for a in range(8)]
+
+
+def stiff_row(stiff_ref, a, u):
+    v = stiff_ref[a, 0] * u[0]
+    for b in range(1, 8):
+        v = v + stiff_ref[a, b] * u[b]
+    return v
+
+
+def side_kernel(loads_hbm, op_hbm, iface_hbm, pre_hbm, corner_hbm, stiff_hbm, dofs_hbm, density_hbm, passive_hbm,
+                keep_ref, even_ref, odd_ref, inverse_ref, pack_ref, weight_ref, spot_ref, spot_kp_ref,
+                loads_ref, op_ref, iface_ref, pre_ref, corner_ref, stiff_ref, dofs_ref, density_ref, passive_ref,
+                sems):
     copies = fetch(sems, ((loads_hbm, loads_ref), (pre_hbm, pre_ref), (iface_hbm, iface_ref),
-                          (corner_hbm, corner_ref), (op_hbm, op_ref)))
+                          (corner_hbm, corner_ref), (op_hbm, op_ref), (stiff_hbm, stiff_ref),
+                          (dofs_hbm, dofs_ref), (density_hbm, density_ref), (passive_hbm, passive_ref)))
     for copy in copies[:3]:
         copy.wait()
     loads = loads_ref[:, 0, :]
@@ -104,30 +136,53 @@
     x_odd = jnp.broadcast_to(is_odd("gx"), (1, R))
     sides = ((jnp.where(x_odd, left, right), even_ref), (jnp.where(x_odd, right, left), odd_ref))
     copies[3].wait()
-    chosen = []
-    for side, (idx, out) in enumerate(sides):
+    copies[4].wait()
+    both = lax.dot_general(halves(p), op_ref[0], (((1,), (1,)), ((), ())), preferred_element_type=F32)
+    y, rest = both[:CASES], both[CASES:]
+    keep_ref[KEEP_Y : KEEP_Y + 8] = y
+    keep_ref[KEEP_REST : KEEP_REST + 8] = rest
+    for idx, out in sides:
         where = pattern(jnp.broadcast_to(idx, (8, R)))
         scale = pick(blocks_of(pre), where)
-        chosen.append((where, scale))
         out[SIDE_P : SIDE_P + 8] = pick(blocks_of(p), where)
         out[SIDE_M : SIDE_M + 8] = scale
         for j in range(corner_ref.shape[1] // 8):
             rows = corner_ref[0, 8 * j : 8 * j + 8]
             out[SIDE_C + 8 * j : SIDE_C + 8 * j + 8] = scale * pick(blocks_of(rows), where)
+        out[SIDE_Y : SIDE_Y + 8] = scale * pick(blocks_of(y), where)
+    for side, (idx, _) in enumerate(sides):
         column = jnp.transpose(jnp.broadcast_to(idx, (R, R)))
         number = lax.broadcasted_iota(jnp.int32, (R, LANES), 0) + 1
         for h in range(8):
             at = lax.broadcasted_iota(jnp.int32, (R, LANES), 1) + LANES * h
             found = jnp.sum(jnp.where(column == at, number, 0), axis=0, keepdims=True)
             inverse_ref[side, :, LANES * h : LANES * (h + 1)] = jnp.broadcast_to(found, (8, LANES))
-    copies[4].wait()
-    both = lax.dot_general(halves(p), op_ref[0], (((1,), (1,)), ((), ())), preferred_element_type=F32)
-    y, rest = both[:CASES], both[CASES:]
-    keep_ref[KEEP_Y : KEEP_Y + 8] = y
-    keep_ref[KEEP_REST : KEEP_REST + 8] = rest
-    keep_ref[KEEP_S : KEEP_S + 8, :LANES] = at_lanes((lane_sum(loads * p), lane_sum(p * rest)))
-    for (where, scale), (_, out) in zip(chosen, sides):
-        out[SIDE_Y : SIDE_Y + 8] = scale * pick(blocks_of(y), where)
+    for copy in copies[5:]:
+        copy.wait()
+    for a in range(0, 8, 2):
+        first, second = edge_tiles(dofs_ref[a].astype(F32), dofs_ref[a + 1].astype(F32))
+        pack_ref[a] = first.astype(jnp.int32)
+        pack_ref[a + 1] = second.astype(jnp.int32)
+    rho = density_ref[...]
+    weight = jnp.where(passive_ref[...] == 1, 0.0, -penalty * rho * rho)
+    ex = weight.shape[0]
+    for i in range(ex // 8):
+        weight_ref[i] = weight[8 * i : 8 * i + 8]
+    weight_ref[ex // 8] = edge_tiles(weight, weight)[0]
+    spot = corner_lanes(dofs_ref[:, 0, :], dofs_ref[:, ex - 1, :])
+    spot_ref[...] = spot
+    spot_weight = jnp.broadcast_to(corner_lanes(weight[0:1], weight[ex - 1 :]), (8, LANES))
+    u = corner_values(p, spot)
+    pp = None
+    for a in range(8):
+        v = stiff_row(stiff_ref, a, u)
+        spot_kp_ref[a] = spot_weight * v
+        pp = u[a] * v if pp is None else pp + u[a] * v
+    spot_kp_ref[8] = spot_weight
+    block = at_lanes((lane_sum(loads * p), lane_sum(p * rest)))
+    lane = lax.broadcasted_iota(jnp.int32, (CASES, LANES), 1)
+    pp = jnp.where(lane < 4, spot_weight * pp, 0.0)
+    keep_ref[KEEP_S : KEEP_S + 8, :LANES] = block + pltpu.roll(pp, CORNER_PP, 1)
 
 
 def spread(values, inverse):
@@ -140,8 +195,9 @@
 
 
 def second_kernel(got_ref, keep_ref, mine_e_ref, mine_o_ref, theirs_e_ref, theirs_o_ref, inverse_ref,
-                  coarse_ref, corner_ref, op_ref, pre_hbm, send_ref, t_ref, pre_ref, sems):
-    copies = fetch(sems, ((pre_hbm, pre_ref),))
+                  spot_ref, spot_kp_ref, coarse_ref, corner_ref, pre_hbm, op_hbm, stiff_hbm,
+                  send_ref, t_ref, pre_ref, op_ref, stiff_ref, sems):
+    copies = fetch(sems, ((pre_hbm, pre_ref), (op_hbm, op_ref), (stiff_hbm, stiff_ref)))
     total = got_ref[0]
     for d in range(1, got_ref.shape[0]):
         total = total + got_ref[d]
@@ -165,109 +221,65 @@
         t_theirs = t_theirs + plain_dot(w, theirs[SIDE_C:])
         term = -coupling * lane_sum(t_mine * t_theirs)
         tlt = term if tlt is None else tlt + term
+    copies[1].wait()
     both = lax.dot_general(halves(t), op_ref[0], (((1,), (1,)), ((), ())), preferred_element_type=F32)
     tlt = tlt + lane_sum(t * (both[:CASES] + both[CASES:]))
     rest = keep_ref[KEEP_REST : KEEP_REST + 8]
     block = keep_ref[KEEP_S : KEEP_S + 8, :LANES]
     block = block + at_lanes((lane_sum(p * q), lane_sum(q * t), tlt, lane_sum(t * rest)), PQ)
+    copies[2].wait()
+    u = corner_values(t, spot_ref[...])
+    pt = tt = None
+    for a in range(8):
+        one, two = u[a] * spot_kp_ref[a], u[a] * stiff_row(stiff_ref, a, u)
+        pt, tt = (one, two) if pt is None else (pt + one, tt + two)
+    lane = lax.broadcasted_iota(jnp.int32, (CASES, LANES), 1)
+    pt, tt = jnp.where(lane < 4, pt, 0.0), jnp.where(lane < 4, spot_kp_ref[8] * tt, 0.0)
+    block = block + pltpu.roll(pt, CORNER_PT, 1) + pltpu.roll(tt, CORNER_TT, 1)
     for d in range(send_ref.shape[0]):
         send_ref[d, :CASES] = g
         send_ref[d, CASES:] = block
 
 
-def make_table(table_ref, vec):
-    for c in range(CASES):
-        for h in range(8):
-            table_ref[c, h] = jnp.broadcast_to(vec[c : c + 1, LANES * h : LANES * (h + 1)], (8, LANES))
-
-
-def gather_tile(dofs, table_ref, u_ref):
+def make_tables(table_ref, *vectors):
+    for i, vec in enumerate(vectors):
+        for c in range(CASES):
+            for h in range(8):
+                row = vec[c : c + 1, LANES * h : LANES * (h + 1)]
+                table_ref[i, c, h] = jnp.broadcast_to(row, (8, LANES))
+
+
+def tile_fields(dofs, scale, stiff_ref, table_ref, u_ref, put):
     for a in range(8):
         where = pattern(dofs(a))
         for c in range(CASES):
-            u_ref[a, c] = pick([table_ref[c, h] for h in range(8)], where)
-
-
-def stiff_row(stiff_ref, a, u):
-    v = stiff_ref[a, 0] * u[0]
-    for b in range(1, 8):
-        v = v + stiff_ref[a, b] * u[b]
-    return v
-
-
-def edge_tiles(first, second):
-    ex, ey = first.shape
-    lane = lax.broadcasted_iota(jnp.int32, (1, LANES), 1)
-    turned = jnp.transpose(jnp.concatenate([first, second], axis=0))
-    swapped = pltpu.roll(turned, LANES - ex, 1)
-    out = []
-    for array, low, high in ((first, turned, swapped), (second, swapped, turned)):
-        cols = [jnp.where(lane < ex, low[j : j + 1], high[j + 1 : j + 2]) for j in (0, ey - 2)]
-        out.append(jnp.concatenate([array[0:2], array[ex - 2 :]] + cols + [array[0:2]], axis=0))
-    return out
-
-
-def p_kernel(keep_ref, dofs_ref, stiff_hbm, density_hbm, passive_hbm,
-             kp_ref, pp_ref, pack_ref, weight_ref, table_ref, u_ref, stiff_ref, density_ref, passive_ref, sems):
-    copies = fetch(sems, ((stiff_hbm, stiff_ref), (density_hbm, density_ref), (passive_hbm, passive_ref)))
-    make_table(table_ref, keep_ref[KEEP_P : KEEP_P + 8])
-    for a in range(0, 8, 2):
-        first, second = edge_tiles(dofs_ref[a].astype(F32), dofs_ref[a + 1].astype(F32))
-        pack_ref[a] = first.astype(jnp.int32)
-        pack_ref[a + 1] = second.astype(jnp.int32)
-    for copy in copies:
-        copy.wait()
-    rho = density_ref[...]
-    weight = jnp.where(passive_ref[...] == 1, 0.0, -penalty * rho * rho)
-    count = weight.shape[0] // 8
-    for i in range(count):
-        weight_ref[i] = weight[8 * i : 8 * i + 8]
-    weight_ref[count] = edge_tiles(weight, weight)[0]
-
-    def work(dofs, tile):
-        gather_tile(dofs, table_ref, u_ref)
-        scale = weight_ref[tile]
-        for c in range(CASES):
-            u = [u_ref[a, c] for a in range(8)]
-            pp = None
-            for a in range(8):
-                v = stiff_row(stiff_ref, a, u)
-                kp_ref[tile, a, c] = v
-                pp = u[a] * v if pp is None else pp + u[a] * v
-            pp_ref[tile, c] = scale * pp
-
-    @pl.loop(0, count)
-    def _(tile):
-        rows = pl.ds(pl.multiple_of(8 * tile, 8), 8)
-        work(lambda a: dofs_ref[a, rows, :], tile)
-
-    work(lambda a: pack_ref[a], count)
-
-
-def t_fields(stiff_ref, kp, scale, u_ref, c):
-    u = [u_ref[a, c] for a in range(8)]
-    pt = tt = None
-    for a in range(8):
-        v = stiff_ref[a, a] * u[a]
-        for b in range(a + 1, 8):
-            v = v + (stiff_ref[a, b] + stiff_ref[b, a]) * u[b]
-        one, two = u[a] * kp(a, c), u[a] * v
-        pt, tt = (one, two) if pt is None else (pt + one, tt + two)
-    return scale * pt, scale * tt
-
-
-def edge_kernel(t_ref, pack_ref, kp_ref, pp_ref, weight_ref, stiff_hbm,
+            for i in range(2):
+                u_ref[i, a, c] = pick([table_ref[i, c, h] for h in range(8)], where)
+    for c in range(CASES):
+        p = [u_ref[0, a, c] for a in range(8)]
+        t = [u_ref[1, a, c] for a in range(8)]
+        pp = pt = tt = None
+        for a in range(8):
+            v = stiff_row(stiff_ref, a, p)
+            w = stiff_ref[a, a] * t[a]
+            for b in range(a + 1, 8):
+                w = w + (stiff_ref[a, b] + stiff_ref[b, a]) * t[b]
+            terms = p[a] * v, t[a] * v, t[a] * w
+            pp, pt, tt = terms if pp is None else (pp + terms[0], pt + terms[1], tt + terms[2])
+        put(c, scale * pp, scale * pt, scale * tt)
+
+
+def edge_kernel(keep_ref, t_ref, pack_ref, weight_ref, stiff_hbm,
                 row_e_ref, row_o_ref, col_e_ref, col_o_ref, table_ref, u_ref, field_ref, stiff_ref, sems):
     copies = fetch(sems, ((stiff_hbm, stiff_ref),))
-    make_table(table_ref, t_ref[...])
-    gather_tile(lambda a: pack_ref[a], table_ref, u_ref)
+    make_tables(table_ref, keep_ref[KEEP_P : KEEP_P + 8], t_ref[...])
     copies[0].wait()
-    tile = kp_ref.shape[0] - 1
-    for c in range(CASES):
-        pt, tt = t_fields(stiff_ref, lambda a, c: kp_ref[tile, a, c], weight_ref[tile], u_ref, c)
-        field_ref[c] = pp_ref[tile, c]
-        field_ref[CASES + c] = pt
-        field_ref[2 * CASES + c] = tt
+
+    def put(c, *fields):
+        for i, field in enumerate(fields):
+            field_ref[CASES * i + c] = field
+
+    tile_fields(lambda a: pack_ref[a], weight_ref[weight_ref.shape[0] - 1], stiff_ref, table_ref, u_ref, put)
     x_odd = jnp.broadcast_to(is_odd("gx"), (FIELDS, LANES))
     y_odd = jnp.broadcast_to(is_odd("gy"), (FIELDS, LANES))
     for i in range(2):
@@ -279,22 +291,24 @@
     col_o_ref[...] = jnp.where(y_odd, high, low)
 
 
-def t_kernel(t_ref, dofs_ref, kp_ref, weight_ref, stiff_hbm, pt_ref, tt_ref, table_ref, u_ref, stiff_ref, sems):
+def field_kernel(keep_ref, t_ref, dofs_ref, weight_ref, stiff_hbm, pp_ref, pt_ref, tt_ref,
+                 table_ref, u_ref, stiff_ref, sems):
     copies = fetch(sems, ((stiff_hbm, stiff_ref),))
-    make_table(table_ref, t_ref[...])
+    make_tables(table_ref, keep_ref[KEEP_P : KEEP_P + 8], t_ref[...])
     copies[0].wait()
 
-    @pl.loop(0, pt_ref.shape[0])
+    @pl.loop(0, pp_ref.shape[0])
     def _(tile):
         rows = pl.ds(pl.multiple_of(8 * tile, 8), 8)
-        gather_tile(lambda a: dofs_ref[a, rows, :], table_ref, u_ref)
-        for c in range(CASES):
-            pt_ref[tile, c], tt_ref[tile, c] = t_fields(
-                stiff_ref, lambda a, c: kp_ref[tile, a, c], weight_ref[tile], u_ref, c)
+
+        def put(c, pp, pt, tt):
+            pp_ref[tile, c], pt_ref[tile, c], tt_ref[tile, c] = pp, pt, tt
+
+        tile_fields(lambda a: dofs_ref[a, rows, :], weight_ref[tile], stiff_ref, table_ref, u_ref, put)
 
 
 def last_kernel(got_ref, coarse_ref, keep_ref, t_ref, pp_ref, pt_ref, tt_ref,
-                mine_ye_ref, mine_yo_ref, xe_ref, xo_ref, ye_ref, yo_ref, ee_ref, eo_ref, oe_ref, oo_ref,
+                mine_ye_ref, mine_yo_ref, xe_ref, xo_ref, ye_ref, yo_ref,
                 adj_ref, out_ref):
     total = got_ref[0]
     for d in range(1, got_ref.shape[0]):
@@ -345,14 +359,19 @@
     g_below2, g_above2 = two(rows[0][1], rows[1][1], x_odd)
     before, after = two(combine(ye_ref[...]), combine(yo_ref[...]), y_odd)
     col_low, col_high = two(combine(mine_ye_ref[...]), combine(mine_yo_ref[...]), y_odd)
-    ee, eo, oe, oo = (combine(ref[:FIELDS]) for ref in (ee_ref, eo_ref, oe_ref, oo_ref))
-    below_e, above_e = two(ee, oe, x_odd)
-    below_o, above_o = two(eo, oo, x_odd)
-    below_before, below_after = two(below_e, below_o, y_odd)
-    above_before, above_after = two(above_e, above_o, y_odd)
-    last = LANES - 1
-    corner = [below_before[:, last:] / diag, below_after[:, :1] / diag,
-              above_before[:, last:] / diag, above_after[:, :1] / diag]
+    wide_lane = lax.broadcasted_iota(jnp.int32, (CASES, LANES), 1)
+    of_lane = jnp.where(wide_lane < CORNER_PT, wide[0], jnp.where(wide_lane < CORNER_TT, wide[1], wide[2]))
+    x, y = lax.axis_index("gx"), lax.axis_index("gy")
+    nx, ny = lax.axis_size("gx"), lax.axis_size("gy")
+
+    def corner_of(dx, dy, there, k):
+        whose = jnp.clip(x + dx, 0, nx - 1) * ny + jnp.clip(y + dy, 0, ny - 1)
+        row = jnp.sum(of_lane * got_ref[whose, CASES:, :], axis=0, keepdims=True)
+        parts = [row[:, at + k : at + k + 1] for at in (CORNER_PP, CORNER_PT, CORNER_TT)]
+        return there * (parts[0] + parts[1] + parts[2]) / diag
+
+    corner = [corner_of(-1, -1, has[0] * has[2], 3), corner_of(-1, 1, has[0] * has[3], 2),
+              corner_of(1, -1, has[1] * has[2], 1), corner_of(1, 1, has[1] * has[3], 0)]
     lane = lax.broadcasted_iota(jnp.int32, (1, LANES), 1)
 
     def shifted(row, low, high, length):
@@ -434,62 +453,56 @@
     def held(array):
         return pltpu.VMEM(array.shape, array.dtype)
 
+    def in_hbm(array):
+        return pltpu.with_memory_space_constraint(array, pltpu.HBM)
+
     def copies(n):
         return pltpu.SemaphoreType.DMA((n,))
 
     stiff = pltpu.SMEM(elem_stiff.shape, F32)
-    table = pltpu.VMEM((CASES, 8, 8, LANES), F32)
-    gathered = pltpu.VMEM((8, CASES, 8, LANES), F32)
+    table = pltpu.VMEM((2, CASES, 8, 8, LANES), F32)
+    gathered = pltpu.VMEM((2, 8, CASES, 8, LANES), F32)
 
     send = call(first_kernel, "first", f32(everyone, CASES, modes), [HBM] * 3,
                 [held(loads), held(precond), held(corner_map), copies(3)], 4_000_000,
-                )(loads, precond, corner_map)
+                )(in_hbm(loads), in_hbm(precond), in_hbm(corner_map))
     got = lax.all_to_all(send, ("gx", "gy"), 0, 0)
 
     side = f32(SIDE_C + modes, R)
-    keep, mine_e, mine_o, inverse = call(
+    params = (loads, dual_op, iface, precond, corner_map, elem_stiff, elem_dofs, density, passive)
+    keep, mine_e, mine_o, inverse, pack, weight, spot, spot_kp = call(
         side_kernel, "sides",
-        (f32(KEEP_S + 8, unknowns), side, side, jax.ShapeDtypeStruct((2, 8, unknowns), jnp.int32)),
-        [HBM] * 5,
-        [held(loads), held(dual_op), held(iface), held(precond), held(corner_map), copies(5)], 8_000_000,
-    )(loads, dual_op, iface, precond, corner_map)
+        (f32(KEEP_S + 8, unknowns), side, side, jax.ShapeDtypeStruct((2, 8, unknowns), jnp.int32),
+         jax.ShapeDtypeStruct((8, 8, LANES), jnp.int32), f32(tiles + 1, 8, LANES),
+         jax.ShapeDtypeStruct((8, LANES), jnp.int32), f32(9, 8, LANES)),
+        [HBM] * 9, [stiff if a is elem_stiff else held(a) for a in params] + [copies(9)], 10_000_000,
+    )(*(in_hbm(a) for a in params))
     theirs_e = swap_over(mine_e, "gx", x_even)
     theirs_o = swap_over(mine_o, "gx", x_odd)
 
-    kp, pp, pack, weight = call(
-        p_kernel, "pfields",
-        (f32(tiles + 1, 8, CASES, 8, LANES), f32(tiles + 1, CASES, 8, LANES),
-         jax.ShapeDtypeStruct((8, 8, LANES), jnp.int32), f32(tiles + 1, 8, LANES)),
-        [VMEM] * 2 + [HBM] * 3, [table, gathered, stiff, held(density), held(passive), copies(3)], 24_000_000,
-    )(keep, elem_dofs, elem_stiff, density, passive)
-    got, pack = lax.optimization_barrier((got, pack))
-
     send, t = call(
         second_kernel, "second", (f32(everyone, 2 * CASES, modes), f32(CASES, unknowns)),
-        [VMEM] * 10 + [HBM], [held(precond), copies(1)], 9_000_000,
-    )(got, keep, mine_e, mine_o, theirs_e, theirs_o, inverse, coarse_inv, corner_map, dual_op, precond)
+        [VMEM] * 11 + [HBM] * 3, [held(precond), held(dual_op), stiff, copies(3)], 9_000_000,
+    )(got, keep, mine_e, mine_o, theirs_e, theirs_o, inverse, spot, spot_kp, coarse_inv, corner_map,
+      in_hbm(precond), in_hbm(dual_op), in_hbm(elem_stiff))
     got = lax.all_to_all(send, ("gx", "gy"), 0, 0)
 
     row = f32(2 * FIELDS, LANES)
     col = f32(FIELDS, LANES)
     row_e, row_o, col_e, col_o = call(
-        edge_kernel, "edges", (row, row, col, col), [VMEM] * 5 + [HBM],
+        edge_kernel, "edges", (row, row, col, col), [VMEM] * 4 + [HBM],
         [table, gathered, pltpu.VMEM((FIELDS, 8, LANES), F32), stiff, copies(1)], 4_000_000,
-    )(t, pack, kp, pp, weight, elem_stiff)
+    )(keep, t, pack, weight, in_hbm(elem_stiff))
     near = [swap_over(row_e, "gx", x_even), swap_over(row_o, "gx", x_odd),
             swap_over(col_e, "gy", y_even), swap_over(col_o, "gy", y_odd)]
-    for array, px in ((row_e, x_even), (row_o, x_odd)):
-        for py in (y_even, y_odd):
-            pairs = [(a * ny + c, b * ny + d) for a, b in px for c, d in py]
-            near.append(swap_over(array, ("gx", "gy"), pairs))
 
     field = f32(tiles, CASES, 8, LANES)
-    pt, tt = call(
-        t_kernel, "tfields", (field, field), [VMEM] * 4 + [HBM], [table, gathered, stiff, copies(1)], 22_000_000,
-    )(t, elem_dofs, kp, weight, elem_stiff)
+    pp, pt, tt = call(
+        field_kernel, "fields", (field,) * 3, [VMEM] * 4 + [HBM], [table, gathered, stiff, copies(1)], 36_000_000,
+    )(keep, t, elem_dofs, weight, in_hbm(elem_stiff))
 
     adjoint, sens = call(
-        last_kernel, "last", (f32(CASES, 1, unknowns), f32(ex, ey)), [VMEM] * 17, [], 4_000_000,
+        last_kernel, "last", (f32(CASES, 1, unknowns), f32(ex, ey)), [VMEM] * 13, [], 4_000_000,
     )(got, coarse_inv, keep, t, pp, pt, tt, col_e, col_o, *near)
     return adjoint, sens
 

time: 70.1 us -> 48.6 us (0.69); the launches traced: 69 us -> 48.2 us
  local copies, waits for them, and re-layouts: 21 us -> 0.02 us
  starting transfers between devices: 25 us -> 21.6 us
  waiting for transfers between devices: 0.02 us -> 2.28 us
  Pallas kernels: 22.1 us -> 23.5 us
    unnamed x70 -> x6, local copies, waits for them, and re-layouts: 21 us -> 0.02 us
    ppermute x7 -> x5, starting transfers between devices: 13.2 us -> 8.74 us  [swap_over(): return lax.ppermute(array, axis, pairs) if pairs else jnp.zeros_like(array)]
    ppermute x7 -> x5, waiting for transfers between devices: 0.02 us -> 2.28 us  [swap_over(): return lax.ppermute(array, axis, pairs) if pairs else jnp.zeros_like(array)]
    pallas_call x3 -> x2, Pallas kernels: 14 us -> 12.8 us  [the longest x1 10.8 us: on_device(): call(field_kernel, 'fields', (field,) * 3, [VMEM] * 4 + [HBM], [table, ga...]
    all_to_all x2, starting transfers between devices: 11.8 us -> 12.9 us  [on_device(): got = lax.all_to_all(send, ('gx', 'gy'), 0, 0)]
    pallas_call x1, Pallas kernels: 1.29 us -> 2.35 us  [on_device(): call(first_kernel, 'first', f32(everyone, CASES, modes), [HBM] * 3, [held...]
    pallas_call x1, Pallas kernels: 2.2 us -> 3.24 us  [on_device(): call(side_kernel, 'sides', (f32(KEEP_S + 8, unknowns), side, side, jax.Sh...]
  transfers between devices with their start and end apart: 9 -> 7, of which waited for: 0 -> 1; matrix products, arithmetic and copies ran while one was open for 0% -> 0% of each run, Pallas kernels for 23% -> 33%
where the time goes in v4:
time: 48.6 us; the launch traced here: 48.2 us
  Pallas kernels  23.5 us (48%)
  starting transfers between devices  21.6 us (44%)
  waiting for transfers between devices  2.28 us (5%)
  between operations  0.78 us (2%)
    all_to_all x2, starting transfers between devices, on_device(): got = lax.all_to_all(send, ('gx', 'gy'), 0, 0)  12.9 us
    pallas_call x1, Pallas kernels, on_device(): call(field_kernel, 'fields', (field,) * 3, [VMEM] * 4 + [HBM], [table, ga...  10.8 us
    ppermute x5, starting transfers between devices, swap_over(): return lax.ppermute(array, axis, pairs) if pairs else jnp.zeros_like(array)  8.74 us
    pallas_call x1, Pallas kernels, on_device(): call(second_kernel, 'second', (f32(everyone, 2 * CASES, modes), f32(CASES...  3.6 us
    pallas_call x1, Pallas kernels, on_device(): call(side_kernel, 'sides', (f32(KEEP_S + 8, unknowns), side, side, jax.Sh...  3.24 us
    pallas_call x1, Pallas kernels, on_device(): call(first_kernel, 'first', f32(everyone, CASES, modes), [HBM] * 3, [held...  2.35 us
    ppermute x5, waiting for transfers between devices, swap_over(): return lax.ppermute(array, axis, pairs) if pairs else jnp.zeros_like(array)  2.28 us
    pallas_call x1, Pallas kernels, on_device(): call(edge_kernel, 'edges', (row, row, col, col), [VMEM] * 4 + [HBM], [tab...  2.03 us
  transfers between devices with their start and end apart: 7, of which 1 were waited for; matrix products, arithmetic and copies ran while one was open for 0% of the time, Pallas kernels for 33%

profile of v4, /device:TPU:1, one launch (start us, length us, event | category | flops | bytes accessed | tf_op | source)
XLA Modules:
  0.0 48.2 jit_solution(7615346545066115270)
XLA Ops:
  0.6 0.0 copy-start
  0.6 0.0 copy-start.2
  0.7 2.4 %first.1 = f32[32,8,128]{2,1,0:T(8,128)} custom-call(f32[8,1,1024]{2,1,0:T(1,128)} %loads_hbm.3, f32[1,1024]{1,0:T(1,128)} %pre_hbm.5, f32[1,128,1024]{2,1,0:T(8,128)} %corner_ref.1), custom_call_target="tpu_custom_call" | custom-call | flops 1000000 | bytes 4000000 | tf_op jit(solution)/shard_map/first/pallas_call | solution.py:466
  3.0 7.1 %all-to-all-start = ((f32[32,8,128]{2,1,0:T(8,128)}), f32[32,8,128]{2,1,0:T(8,128)S(1)}, u32[]{:S(2)}, u32[]{:S(2)}) async-start(f32[32,8,128]{2,1,0:T(8,128)} %first.1), calls=%async_computation | async-start | bytes 262144 | tf_op jit(solution)/shard_map/all_to_all | solution.py:469
  10.1 3.2 %sides.1 = (f32[32,1024]{1,0:T(8,128)S(1)}, f32[152,128]{1,0:T(8,128)S(1)}, f32[152,128]{1,0:T(8,128)S(1)}, s32[2,8,1024]{2,1,0:T(8,128)S(1)}, s32[8,8,128]{2,1,...) custom-call(f32[8,1,1024]{2,1,0:T(1,128)} %loads_hbm.3, ...), custom_call_target="tpu_custom_call" | custom-call | flops 1000000 | bytes 10000000 | tf_op jit(solution)/shard_map/sides/pallas_call | solution.py:473
  13.4 0.0 copy-start.1
  13.4 0.3 collective-permute-start
  13.7 3.4 %collective-permute-start.1 = (f32[152,128]{1,0:T(8,128)S(1)}, f32[152,128]{1,0:T(8,128)S(1)}, u32[]{:S(2)}, u32[]{:S(2)}) collective-permute-start(f32[152,128]{1,0:T(8,128)S(1)} %get-tuple-element.21.mine_o_ref), channel_id=1, source_target_pairs={{2,4},{6,8},{10,12},{14,16},{18,20},{22,24},{26,28},{4,2},{8,6},{1... | collective-permute-start | bytes 233480 | tf_op jit(solution)/shard_map/ppermute | solution.py:423
  17.1 0.0 collective-permute-done.theirs_e_ref
  17.1 2.3 %collective-permute-done.1.theirs_o_ref = f32[152,128]{1,0:T(8,128)S(1)} collective-permute-done((f32[152,128]{1,0:T(8,128)S(1)}, f32[152,128]{1,0:T(8,128)S(1)}, u32[]{:S(2)}, u32[]{:S(2)}) %collective-permute-start.1) | collective-permute-done | bytes 77856 | tf_op jit(solution)/shard_map/ppermute | solution.py:423
  19.4 0.0 all-to-all-done.got_ref
  19.4 0.0 copy-done
  19.4 0.0 copy-done.2
  19.4 3.6 %second.1 = (f32[32,16,128]{2,1,0:T(8,128)}, f32[8,1024]{1,0:T(8,128)S(1)}) custom-call(f32[32,8,128]{2,1,0:T(8,128)S(1)} %all-to-all-done.got_ref, f32[32,1024]{1,0:T(8,128)S(1)} %get-tuple-element.19.keep_ref, f32[152,128]{1,0:T(8,128)S(1)} %get-tuple-element.20.mine_e_ref, f32[152,128]{1,0:T(8,128)S(1)} %get-tuple-element.21.mine_o_ref, ...), custom_call_target="tpu_custom_call" | custom-call | flops 1000000 | bytes 9000000 | tf_op jit(solution)/shard_map/second/pallas_call | solution.py:483
  23.0 5.8 %all-to-all-start.1 = ((f32[32,16,128]{2,1,0:T(8,128)}), f32[32,16,128]{2,1,0:T(8,128)S(1)}, u32[]{:S(2)}, u32[]{:S(2)}) async-start(f32[32,16,128]{2,1,0:T(8,128)} %get-tuple-element.25), calls=%async_computation.1 | async-start | bytes 524288 | tf_op jit(solution)/shard_map/all_to_all | solution.py:488
  28.8 2.0 %edges.1 = (f32[48,128]{1,0:T(8,128)S(1)}, f32[48,128]{1,0:T(8,128)S(1)}, f32[24,128]{1,0:T(8,128)S(1)}, f32[24,128]{1,0:T(8,128)S(1)}) custom-call(f32[32,1024]{1,0:T(8,128)S(1)} %get-tuple-element.19.keep_ref, f32[8,1024]{1,0:T(8,128)S(1)} %get-tuple-element.26.t_ref, s32[8,8,128]{2,1,0:T(8,128)S(1)} %get-tuple-element.31.pack_ref, ...), custom_call_target="tpu_custom_call" | custom-call | flops 1000000 | bytes 4000000 | tf_op jit(solution)/shard_map/edges/pallas_call | solution.py:492
  30.9 0.3 collective-permute-start.2
  31.2 3.4 %collective-permute-start.3 = (f32[48,128]{1,0:T(8,128)S(1)}, f32[48,128]{1,0:T(8,128)S(1)}, u32[]{:S(2)}, u32[]{:S(2)}) collective-permute-start(f32[48,128]{1,0:T(8,128)S(1)} %get-tuple-element.35), channel_id=1, source_target_pairs={{2,4},{6,8},{10,12},{14,16},{18,20},{22,24},{26,28},{4,2},{8,6},{1... | collective-permute-start | bytes 73736 | tf_op jit(solution)/shard_map/ppermute | solution.py:423
  34.6 1.2 %collective-permute-start.4 = (f32[24,128]{1,0:T(8,128)S(1)}, f32[24,128]{1,0:T(8,128)S(1)}, u32[]{:S(2)}, u32[]{:S(2)}) collective-permute-start(f32[24,128]{1,0:T(8,128)S(1)} %get-tuple-element.32.mine_ye_ref), channel_id=1, source_target_pairs={{0,1},{1,0},{2,3},{3,2},{4,5},{5,4},{6,7},{7,6},{8,9},{9,8},{10,11... | collective-permute-start | bytes 36872 | tf_op jit(solution)/shard_map/ppermute | solution.py:423
  35.9 0.0 copy-done.1
  35.9 10.8 %fields.1 = (f32[8,8,8,128]{3,2,1,0:T(8,128)S(1)}, f32[8,8,8,128]{3,2,1,0:T(8,128)S(1)}, f32[8,8,8,128]{3,2,1,0:T(8,128)S(1)}) custom-call(f32[32,1024]{1,0:T(8,128)S(1)} %get-tuple-element.19.keep_ref, f32[8,1024]{1,0:T(8,128)S(1)} %get-tuple-element.26.t_ref, s32[8,64,128]{2,1,0:T(8,128)S(1)} %copy-done.1, f32[9,8,128]{2,1,0:T(8,128)S(1)} %get-tuple-element.27.weight_ref, ...), custom_call_target="tpu_custom_call" | custom-call | flops 1000000 | bytes 36000000 | tf_op jit(solution)/shard_map/fields/pallas_call | solution.py:500
  46.7 0.0 collective-permute-done.4.ye_ref
  46.7 0.0 collective-permute-done.2.xe_ref
  46.7 0.0 collective-permute-done.3.xo_ref
  46.7 0.0 all-to-all-done.1.got_ref
  46.7 1.5 %last.1 = (f32[8,1,1024]{2,1,0:T(1,128)}, f32[64,128]{1,0:T(8,128)}) custom-call(f32[32,16,128]{2,1,0:T(8,128)S(1)} %all-to-all-done.1.got_ref, f32[128,128]{1,0:T(8,128)S(1)} %copy-done.2, f32[32,1024]{1,0:T(8,128)S(1)} %get-tuple-element.19.keep_ref, f32[8,1024]{1,0:T(8,128)S(1)} %get-tuple-element.26.t_ref, ...), custom_call_target="tpu_custom_call" | custom-call | flops 1000000 | bytes 4000000 | tf_op jit(solution)/shard_map/last/pallas_call | solution.py:504
  (1 shorter events, 0.0 us)
Async XLA Ops:
  0.6 18.8 %copy-start = (f32[1,128,1024]{2,1,0:T(8,128)S(1)}, f32[1,128,1024]{2,1,0:T(8,128)}, u32[]{:S(2)}) copy-start(f32[1,128,1024]{2,1,0:T(8,128)} %corner_ref.1) | copy-start | bytes 1572868
  0.6 18.8 %copy-start.2 = (f32[128,128]{1,0:T(8,128)S(1)}, f32[128,128]{1,0:T(8,128)}, u32[]{:S(2)}) copy-start(f32[128,128]{1,0:T(8,128)} %coarse_ref.3) | copy-start | bytes 196612
  3.0 16.4 %all-to-all-start = ((f32[32,8,128]{2,1,0:T(8,128)}), f32[32,8,128]{2,1,0:T(8,128)S(1)}, u32[]{:S(2)}, u32[]{:S(2)}) async-start(f32[32,8,128]{2,1,0:T(8,128)} %first.1), calls=%async_computation | async-start | bytes 262144 | tf_op jit(solution)/shard_map/all_to_all | solution.py:469
  13.4 22.5 %copy-start.1 = (s32[8,64,128]{2,1,0:T(8,128)S(1)}, s32[8,64,128]{2,1,0:T(8,128)}, u32[]{:S(2)}) copy-start(s32[8,64,128]{2,1,0:T(8,128)} %dofs_ref.1) | copy-start | bytes 786436
  13.4 3.8 %collective-permute-start = (f32[152,128]{1,0:T(8,128)S(1)}, f32[152,128]{1,0:T(8,128)S(1)}, u32[]{:S(2)}, u32[]{:S(2)}) collective-permute-start(f32[152,128]{1,0:T(8,128)S(1)} %get-tuple-element.20.mine_e_ref), channel_id=1, source_target_pairs={{0,2},{4,6},{8,10},{12,14},{16,18},{20,22},{24,26},{28,30},{2,0},{... | collective-permute-start | bytes 233480 | tf_op jit(solution)/shard_map/ppermute | solution.py:423
  13.7 5.7 %collective-permute-start.1 = (f32[152,128]{1,0:T(8,128)S(1)}, f32[152,128]{1,0:T(8,128)S(1)}, u32[]{:S(2)}, u32[]{:S(2)}) collective-permute-start(f32[152,128]{1,0:T(8,128)S(1)} %get-tuple-element.21.mine_o_ref), channel_id=1, source_target_pairs={{2,4},{6,8},{10,12},{14,16},{18,20},{22,24},{26,28},{4,2},{8,6},{1... | collective-permute-start | bytes 233480 | tf_op jit(solution)/shard_map/ppermute | solution.py:423
  23.0 23.7 %all-to-all-start.1 = ((f32[32,16,128]{2,1,0:T(8,128)}), f32[32,16,128]{2,1,0:T(8,128)S(1)}, u32[]{:S(2)}, u32[]{:S(2)}) async-start(f32[32,16,128]{2,1,0:T(8,128)} %get-tuple-element.25), calls=%async_computation.1 | async-start | bytes 524288 | tf_op jit(solution)/shard_map/all_to_all | solution.py:488
  30.9 15.8 %collective-permute-start.2 = (f32[48,128]{1,0:T(8,128)S(1)}, f32[48,128]{1,0:T(8,128)S(1)}, u32[]{:S(2)}, u32[]{:S(2)}) collective-permute-start(f32[48,128]{1,0:T(8,128)S(1)} %get-tuple-element.34), channel_id=1, source_target_pairs={{0,2},{4,6},{8,10},{12,14},{16,18},{20,22},{24,26},{28,30},{2,0},{... | collective-permute-start | bytes 73736 | tf_op jit(solution)/shard_map/ppermute | solution.py:423
  31.2 15.5 %collective-permute-start.3 = (f32[48,128]{1,0:T(8,128)S(1)}, f32[48,128]{1,0:T(8,128)S(1)}, u32[]{:S(2)}, u32[]{:S(2)}) collective-permute-start(f32[48,128]{1,0:T(8,128)S(1)} %get-tuple-element.35), channel_id=1, source_target_pairs={{2,4},{6,8},{10,12},{14,16},{18,20},{22,24},{26,28},{4,2},{8,6},{1... | collective-permute-start | bytes 73736 | tf_op jit(solution)/shard_map/ppermute | solution.py:423
  34.6 12.1 %collective-permute-start.4 = (f32[24,128]{1,0:T(8,128)S(1)}, f32[24,128]{1,0:T(8,128)S(1)}, u32[]{:S(2)}, u32[]{:S(2)}) collective-permute-start(f32[24,128]{1,0:T(8,128)S(1)} %get-tuple-element.32.mine_ye_ref), channel_id=1, source_target_pairs={{0,1},{1,0},{2,3},{3,2},{4,5},{5,4},{6,7},{7,6},{8,9},{9,8},{10,11... | collective-permute-start | bytes 36872 | tf_op jit(solution)/shard_map/ppermute | solution.py:423

commit v5 on v4

--- a/solution.py
+++ b/solution.py
@@ -24,6 +24,7 @@
 RZ, PE, PQ, QMQ, TLT, TE = range(6)
 KEEP_P, KEEP_Y, KEEP_REST, KEEP_S = 0, 8, 16, 24
 FIELDS = 3 * CASES
+EARLY = 5
 CORNER_PP, CORNER_PT, CORNER_TT = 8, 12, 16
 
 
@@ -39,6 +40,19 @@
     high = x.astype(BF16)
     low = (x - high.astype(F32)).astype(BF16)
     return jnp.concatenate([high, low], axis=0)
+
+
+def split(x):
+    high = x.astype(BF16)
+    return high, (x - high.astype(F32)).astype(BF16)
+
+
+def split_dot(a, pair, dim):
+    stack = halves(a)
+    dims = (((1,), (dim,)), ((), ()))
+    main = lax.dot_general(stack, pair[0], dims, preferred_element_type=F32)
+    rest = lax.dot_general(stack, pair[1], dims, preferred_element_type=F32)
+    return main[:8] + main[8:] + rest[:8]
 
 
 def lane_sum(x):
@@ -81,10 +95,18 @@
 
 
 def first_kernel(loads_hbm, pre_hbm, corner_hbm, send_ref, loads_ref, pre_ref, corner_ref, sems):
-    copies = fetch(sems, ((loads_hbm, loads_ref), (pre_hbm, pre_ref), (corner_hbm, corner_ref)))
-    for copy in copies:
-        copy.wait()
-    part = rows_dot(pre_ref[...] * loads_ref[:, 0, :], corner_ref[0])
+    piece = corner_ref.shape[2] // 4
+    parts = [pl.ds(piece * i, piece) for i in range(4)]
+    copies = fetch(sems, [(loads_hbm, loads_ref), (pre_hbm, pre_ref)]
+                   + [(corner_hbm.at[:, :, k], corner_ref.at[:, :, k]) for k in parts])
+    copies[0].wait()
+    copies[1].wait()
+    p = pre_ref[...] * loads_ref[:, 0, :]
+    part = None
+    for i, k in enumerate(parts):
+        copies[2 + i].wait()
+        term = split_dot(p[:, piece * i : piece * (i + 1)], split(corner_ref[0, :, k]), 1)
+        part = term if part is None else part + term
     for d in range(send_ref.shape[0]):
         send_ref[d] = part
 
@@ -118,51 +140,66 @@
     return v
 
 
-def side_kernel(loads_hbm, op_hbm, iface_hbm, pre_hbm, corner_hbm, stiff_hbm, dofs_hbm, density_hbm, passive_hbm,
-                keep_ref, even_ref, odd_ref, inverse_ref, pack_ref, weight_ref, spot_ref, spot_kp_ref,
-                loads_ref, op_ref, iface_ref, pre_ref, corner_ref, stiff_ref, dofs_ref, density_ref, passive_ref,
-                sems):
+def side_indices(iface_ref):
+    left = jnp.broadcast_to(iface_ref[0, :, :R], (8, R))
+    right = jnp.broadcast_to(iface_ref[0, :, R : 2 * R], (8, R))
+    x_odd = jnp.broadcast_to(is_odd("gx"), (8, R))
+    return jnp.where(x_odd, left, right), jnp.where(x_odd, right, left)
+
+
+def side_kernel(loads_hbm, op_hbm, iface_hbm, pre_hbm, corner_hbm,
+                keep_ref, even_ref, odd_ref, loads_ref, op_ref, iface_ref, pre_ref, corner_ref, sems):
     copies = fetch(sems, ((loads_hbm, loads_ref), (pre_hbm, pre_ref), (iface_hbm, iface_ref),
-                          (corner_hbm, corner_ref), (op_hbm, op_ref), (stiff_hbm, stiff_ref),
-                          (dofs_hbm, dofs_ref), (density_hbm, density_ref), (passive_hbm, passive_ref)))
-    for copy in copies[:3]:
+                          (corner_hbm, corner_ref), (op_hbm, op_ref)))
+    for copy in copies[:4]:
         copy.wait()
     loads = loads_ref[:, 0, :]
     p = pre_ref[...] * loads
     keep_ref[KEEP_P : KEEP_P + 8] = p
     pre = jnp.broadcast_to(pre_ref[...], (8, pre_ref.shape[1]))
-    left = iface_ref[0, :, :R]
-    right = iface_ref[0, :, R : 2 * R]
-    x_odd = jnp.broadcast_to(is_odd("gx"), (1, R))
-    sides = ((jnp.where(x_odd, left, right), even_ref), (jnp.where(x_odd, right, left), odd_ref))
-    copies[3].wait()
+    chosen = []
+    for idx, out in zip(side_indices(iface_ref), (even_ref, odd_ref)):
+        where = pattern(idx)
+        scale = pick(blocks_of(pre), where)
+        chosen.append((where, scale, out))
+        out[SIDE_P : SIDE_P + 8] = pick(blocks_of(p), where)
+        out[SIDE_M : SIDE_M + 8] = scale
+        for j in range(corner_ref.shape[1] // 8):
+            rows = corner_ref[0, 8 * j : 8 * j + 8]
+            out[SIDE_C + 8 * j : SIDE_C + 8 * j + 8] = scale * pick(blocks_of(rows), where)
     copies[4].wait()
     both = lax.dot_general(halves(p), op_ref[0], (((1,), (1,)), ((), ())), preferred_element_type=F32)
     y, rest = both[:CASES], both[CASES:]
     keep_ref[KEEP_Y : KEEP_Y + 8] = y
     keep_ref[KEEP_REST : KEEP_REST + 8] = rest
-    for idx, out in sides:
-        where = pattern(jnp.broadcast_to(idx, (8, R)))
-        scale = pick(blocks_of(pre), where)
-        out[SIDE_P : SIDE_P + 8] = pick(blocks_of(p), where)
-        out[SIDE_M : SIDE_M + 8] = scale
-        for j in range(corner_ref.shape[1] // 8):
-            rows = corner_ref[0, 8 * j : 8 * j + 8]
-            out[SIDE_C + 8 * j : SIDE_C + 8 * j + 8] = scale * pick(blocks_of(rows), where)
+    keep_ref[KEEP_S : KEEP_S + 8, :LANES] = at_lanes((lane_sum(loads * p), lane_sum(p * rest)))
+    for where, scale, out in chosen:
         out[SIDE_Y : SIDE_Y + 8] = scale * pick(blocks_of(y), where)
-    for side, (idx, _) in enumerate(sides):
-        column = jnp.transpose(jnp.broadcast_to(idx, (R, R)))
+
+
+def early_kernel(keep_ref, dofs_ref, iface_hbm, corner_hbm, stiff_hbm, density_hbm, passive_hbm,
+                 index_ref, inverse_ref, chigh_ref, clow_ref, pack_ref, weight_ref, spot_ref, spot_kp_ref,
+                 kp_ref, pp_ref,
+                 table_ref, u_ref, iface_ref, corner_ref, stiff_ref, density_ref, passive_ref, sems):
+    copies = fetch(sems, ((iface_hbm, iface_ref), (stiff_hbm, stiff_ref), (density_hbm, density_ref),
+                          (passive_hbm, passive_ref), (corner_hbm, corner_ref)))
+    p = keep_ref[KEEP_P : KEEP_P + 8]
+    make_tables(table_ref, p)
+    for a in range(0, 8, 2):
+        first, second = edge_tiles(dofs_ref[a].astype(F32), dofs_ref[a + 1].astype(F32))
+        pack_ref[a] = first.astype(jnp.int32)
+        pack_ref[a + 1] = second.astype(jnp.int32)
+    for copy in copies:
+        copy.wait()
+    for side, idx in enumerate(side_indices(iface_ref)):
+        index_ref[side] = idx
+        column = jnp.transpose(jnp.broadcast_to(idx[0:1], (R, R)))
         number = lax.broadcasted_iota(jnp.int32, (R, LANES), 0) + 1
         for h in range(8):
             at = lax.broadcasted_iota(jnp.int32, (R, LANES), 1) + LANES * h
             found = jnp.sum(jnp.where(column == at, number, 0), axis=0, keepdims=True)
             inverse_ref[side, :, LANES * h : LANES * (h + 1)] = jnp.broadcast_to(found, (8, LANES))
-    for copy in copies[5:]:
-        copy.wait()
-    for a in range(0, 8, 2):
-        first, second = edge_tiles(dofs_ref[a].astype(F32), dofs_ref[a + 1].astype(F32))
-        pack_ref[a] = first.astype(jnp.int32)
-        pack_ref[a + 1] = second.astype(jnp.int32)
+    chigh_ref[...], clow_ref[...] = split(corner_ref[0])
     rho = density_ref[...]
     weight = jnp.where(passive_ref[...] == 1, 0.0, -penalty * rho * rho)
     ex = weight.shape[0]
@@ -178,11 +215,27 @@
         v = stiff_row(stiff_ref, a, u)
         spot_kp_ref[a] = spot_weight * v
         pp = u[a] * v if pp is None else pp + u[a] * v
+    lane = lax.broadcasted_iota(jnp.int32, (CASES, LANES), 1)
     spot_kp_ref[8] = spot_weight
-    block = at_lanes((lane_sum(loads * p), lane_sum(p * rest)))
-    lane = lax.broadcasted_iota(jnp.int32, (CASES, LANES), 1)
-    pp = jnp.where(lane < 4, spot_weight * pp, 0.0)
-    keep_ref[KEEP_S : KEEP_S + 8, :LANES] = block + pltpu.roll(pp, CORNER_PP, 1)
+    spot_kp_ref[9] = pltpu.roll(jnp.where(lane < 4, spot_weight * pp, 0.0), CORNER_PP, 1)
+
+    def work(dofs, at, scale):
+        gather_tile(dofs, table_ref, u_ref, 0)
+        for c in range(CASES):
+            u = [u_ref[0, a, c] for a in range(8)]
+            pp = None
+            for a in range(8):
+                v = stiff_row(stiff_ref, a, u)
+                kp_ref[at, a, c] = v
+                pp = u[a] * v if pp is None else pp + u[a] * v
+            pp_ref[at, c] = scale * pp
+
+    @pl.loop(0, EARLY)
+    def _(tile):
+        rows = pl.ds(pl.multiple_of(8 * tile, 8), 8)
+        work(lambda a: dofs_ref[a, rows, :], tile, weight_ref[tile])
+
+    work(lambda a: pack_ref[a], EARLY, weight_ref[ex // 8])
 
 
 def spread(values, inverse):
@@ -194,40 +247,36 @@
     return jnp.concatenate(out, axis=1)
 
 
-def second_kernel(got_ref, keep_ref, mine_e_ref, mine_o_ref, theirs_e_ref, theirs_o_ref, inverse_ref,
-                  spot_ref, spot_kp_ref, coarse_ref, corner_ref, pre_hbm, op_hbm, stiff_hbm,
+def second_kernel(got_ref, keep_ref, mine_e_ref, mine_o_ref, theirs_e_ref, theirs_o_ref, index_ref, inverse_ref,
+                  spot_ref, spot_kp_ref, coarse_ref, chigh_ref, clow_ref, pre_hbm, op_hbm, stiff_hbm,
                   send_ref, t_ref, pre_ref, op_ref, stiff_ref, sems):
     copies = fetch(sems, ((pre_hbm, pre_ref), (op_hbm, op_ref), (stiff_hbm, stiff_ref)))
     total = got_ref[0]
     for d in range(1, got_ref.shape[0]):
         total = total + got_ref[d]
+    corner = chigh_ref[...], clow_ref[...]
     p = keep_ref[KEEP_P : KEEP_P + 8]
     base = keep_ref[KEEP_Y : KEEP_Y + 8]
     pairs = ((mine_e_ref, theirs_e_ref), (mine_o_ref, theirs_o_ref))
     for side, (_, theirs) in enumerate(pairs):
         base = base + spread(-coupling * theirs[SIDE_P : SIDE_P + 8], inverse_ref[side])
-    w = rows_dot(total, coarse_ref[...])
-    q = base + plain_dot(w, corner_ref[0])
-    copies[0].wait()
+    w = split_dot(total, split(coarse_ref[...]), 1)
+    q = base + split_dot(w, corner, 0)
+    for copy in copies:
+        copy.wait()
     t = pre_ref[...] * q
     t_ref[...] = t
-    g = rows_dot(t, corner_ref[0])
-    tlt = None
-    for mine, theirs in pairs:
-        p_mine, p_theirs = mine[SIDE_P : SIDE_P + 8], theirs[SIDE_P : SIDE_P + 8]
-        t_mine = mine[SIDE_Y : SIDE_Y + 8] - coupling * mine[SIDE_M : SIDE_M + 8] * p_theirs
-        t_mine = t_mine + plain_dot(w, mine[SIDE_C:])
-        t_theirs = theirs[SIDE_Y : SIDE_Y + 8] - coupling * theirs[SIDE_M : SIDE_M + 8] * p_mine
-        t_theirs = t_theirs + plain_dot(w, theirs[SIDE_C:])
-        term = -coupling * lane_sum(t_mine * t_theirs)
-        tlt = term if tlt is None else tlt + term
-    copies[1].wait()
     both = lax.dot_general(halves(t), op_ref[0], (((1,), (1,)), ((), ())), preferred_element_type=F32)
-    tlt = tlt + lane_sum(t * (both[:CASES] + both[CASES:]))
+    g = split_dot(t, corner, 1)
+    tlt = lane_sum(t * (both[:CASES] + both[CASES:]))
+    for side, (mine, theirs) in enumerate(pairs):
+        t_mine = pick(blocks_of(t), pattern(index_ref[side]))
+        t_theirs = theirs[SIDE_Y : SIDE_Y + 8] - coupling * theirs[SIDE_M : SIDE_M + 8] * mine[SIDE_P : SIDE_P + 8]
+        t_theirs = t_theirs + split_dot(w, split(theirs[SIDE_C:]), 0)
+        tlt = tlt - coupling * lane_sum(t_mine * t_theirs)
     rest = keep_ref[KEEP_REST : KEEP_REST + 8]
     block = keep_ref[KEEP_S : KEEP_S + 8, :LANES]
     block = block + at_lanes((lane_sum(p * q), lane_sum(q * t), tlt, lane_sum(t * rest)), PQ)
-    copies[2].wait()
     u = corner_values(t, spot_ref[...])
     pt = tt = None
     for a in range(8):
@@ -235,7 +284,7 @@
         pt, tt = (one, two) if pt is None else (pt + one, tt + two)
     lane = lax.broadcasted_iota(jnp.int32, (CASES, LANES), 1)
     pt, tt = jnp.where(lane < 4, pt, 0.0), jnp.where(lane < 4, spot_kp_ref[8] * tt, 0.0)
-    block = block + pltpu.roll(pt, CORNER_PT, 1) + pltpu.roll(tt, CORNER_TT, 1)
+    block = block + spot_kp_ref[9] + pltpu.roll(pt, CORNER_PT, 1) + pltpu.roll(tt, CORNER_TT, 1)
     for d in range(send_ref.shape[0]):
         send_ref[d, :CASES] = g
         send_ref[d, CASES:] = block
@@ -249,37 +298,37 @@
                 table_ref[i, c, h] = jnp.broadcast_to(row, (8, LANES))
 
 
-def tile_fields(dofs, scale, stiff_ref, table_ref, u_ref, put):
+def gather_tile(dofs, table_ref, u_ref, *which):
     for a in range(8):
         where = pattern(dofs(a))
         for c in range(CASES):
-            for i in range(2):
+            for i in which:
                 u_ref[i, a, c] = pick([table_ref[i, c, h] for h in range(8)], where)
-    for c in range(CASES):
-        p = [u_ref[0, a, c] for a in range(8)]
-        t = [u_ref[1, a, c] for a in range(8)]
-        pp = pt = tt = None
-        for a in range(8):
-            v = stiff_row(stiff_ref, a, p)
-            w = stiff_ref[a, a] * t[a]
-            for b in range(a + 1, 8):
-                w = w + (stiff_ref[a, b] + stiff_ref[b, a]) * t[b]
-            terms = p[a] * v, t[a] * v, t[a] * w
-            pp, pt, tt = terms if pp is None else (pp + terms[0], pt + terms[1], tt + terms[2])
-        put(c, scale * pp, scale * pt, scale * tt)
-
-
-def edge_kernel(keep_ref, t_ref, pack_ref, weight_ref, stiff_hbm,
+
+
+def t_fields(t, kp, stiff_ref):
+    pt = tt = None
+    for a in range(8):
+        w = stiff_ref[a, a] * t[a]
+        for b in range(a + 1, 8):
+            w = w + (stiff_ref[a, b] + stiff_ref[b, a]) * t[b]
+        one, two = t[a] * kp[a], t[a] * w
+        pt, tt = (one, two) if pt is None else (pt + one, tt + two)
+    return pt, tt
+
+
+def edge_kernel(t_ref, pack_ref, weight_ref, kp_ref, pp_ref, stiff_hbm,
                 row_e_ref, row_o_ref, col_e_ref, col_o_ref, table_ref, u_ref, field_ref, stiff_ref, sems):
     copies = fetch(sems, ((stiff_hbm, stiff_ref),))
-    make_tables(table_ref, keep_ref[KEEP_P : KEEP_P + 8], t_ref[...])
+    make_tables(table_ref, t_ref[...])
+    gather_tile(lambda a: pack_ref[a], table_ref, u_ref, 0)
     copies[0].wait()
-
-    def put(c, *fields):
-        for i, field in enumerate(fields):
-            field_ref[CASES * i + c] = field
-
-    tile_fields(lambda a: pack_ref[a], weight_ref[weight_ref.shape[0] - 1], stiff_ref, table_ref, u_ref, put)
+    scale = weight_ref[weight_ref.shape[0] - 1]
+    for c in range(CASES):
+        pt, tt = t_fields([u_ref[0, a, c] for a in range(8)], [kp_ref[EARLY, a, c] for a in range(8)], stiff_ref)
+        field_ref[c] = pp_ref[EARLY, c]
+        field_ref[CASES + c] = scale * pt
+        field_ref[2 * CASES + c] = scale * tt
     x_odd = jnp.broadcast_to(is_odd("gx"), (FIELDS, LANES))
     y_odd = jnp.broadcast_to(is_odd("gy"), (FIELDS, LANES))
     for i in range(2):
@@ -291,23 +340,43 @@
     col_o_ref[...] = jnp.where(y_odd, high, low)
 
 
-def field_kernel(keep_ref, t_ref, dofs_ref, weight_ref, stiff_hbm, pp_ref, pt_ref, tt_ref,
+def field_kernel(keep_ref, t_ref, dofs_ref, weight_ref, kp_ref, stiff_hbm, pp_ref, pt_ref, tt_ref,
                  table_ref, u_ref, stiff_ref, sems):
     copies = fetch(sems, ((stiff_hbm, stiff_ref),))
-    make_tables(table_ref, keep_ref[KEEP_P : KEEP_P + 8], t_ref[...])
+    make_tables(table_ref, t_ref[...], keep_ref[KEEP_P : KEEP_P + 8])
     copies[0].wait()
 
-    @pl.loop(0, pp_ref.shape[0])
+    def rows_of(tile):
+        return pl.ds(pl.multiple_of(8 * tile, 8), 8)
+
+    def t_at(c):
+        return [u_ref[0, a, c] for a in range(8)]
+
+    @pl.loop(0, EARLY)
     def _(tile):
-        rows = pl.ds(pl.multiple_of(8 * tile, 8), 8)
-
-        def put(c, pp, pt, tt):
-            pp_ref[tile, c], pt_ref[tile, c], tt_ref[tile, c] = pp, pt, tt
-
-        tile_fields(lambda a: dofs_ref[a, rows, :], weight_ref[tile], stiff_ref, table_ref, u_ref, put)
-
-
-def last_kernel(got_ref, coarse_ref, keep_ref, t_ref, pp_ref, pt_ref, tt_ref,
+        rows = rows_of(tile)
+        gather_tile(lambda a: dofs_ref[a, rows, :], table_ref, u_ref, 0)
+        scale = weight_ref[tile]
+        for c in range(CASES):
+            pt, tt = t_fields(t_at(c), [kp_ref[tile, a, c] for a in range(8)], stiff_ref)
+            pt_ref[tile, c], tt_ref[tile, c] = scale * pt, scale * tt
+
+    @pl.loop(EARLY, pt_ref.shape[0])
+    def _(tile):
+        rows = rows_of(tile)
+        gather_tile(lambda a: dofs_ref[a, rows, :], table_ref, u_ref, 0, 1)
+        scale = weight_ref[tile]
+        for c in range(CASES):
+            p = [u_ref[1, a, c] for a in range(8)]
+            kp = [stiff_row(stiff_ref, a, p) for a in range(8)]
+            pp = p[0] * kp[0]
+            for a in range(1, 8):
+                pp = pp + p[a] * kp[a]
+            pt, tt = t_fields(t_at(c), kp, stiff_ref)
+            pp_ref[tile - EARLY, c], pt_ref[tile, c], tt_ref[tile, c] = scale * pp, scale * pt, scale * tt
+
+
+def last_kernel(got_ref, coarse_ref, keep_ref, t_ref, early_ref, late_ref, pt_ref, tt_ref,
                 mine_ye_ref, mine_yo_ref, xe_ref, xo_ref, ye_ref, yo_ref,
                 adj_ref, out_ref):
     total = got_ref[0]
@@ -330,9 +399,10 @@
     tiles = []
     for i in range(pt_ref.shape[0]):
         tile = None
-        for ref, factor in zip((pp_ref, pt_ref, tt_ref), splat):
+        pp = early_ref.at[i] if i < EARLY else late_ref.at[i - EARLY]
+        for ref, factor in zip((pp, pt_ref.at[i], tt_ref.at[i]), splat):
             for c in range(CASES):
-                term = factor[c] * ref[i, c]
+                term = factor[c] * ref[c]
                 tile = term if tile is None else tile + term
         tiles.append(tile)
     grad = jnp.concatenate(tiles, axis=0)
@@ -427,6 +497,14 @@
     return jax.ShapeDtypeStruct(shape, F32)
 
 
+def s32(*shape):
+    return jax.ShapeDtypeStruct(shape, jnp.int32)
+
+
+def bf16(*shape):
+    return jax.ShapeDtypeStruct(shape, BF16)
+
+
 def call(kernel, name, out_shape, in_specs, scratch, moved):
     single = not isinstance(out_shape, tuple)
     return pl.pallas_call(
@@ -460,50 +538,61 @@
         return pltpu.SemaphoreType.DMA((n,))
 
     stiff = pltpu.SMEM(elem_stiff.shape, F32)
+    one_table = pltpu.VMEM((1, CASES, 8, 8, LANES), F32)
+    one_gathered = pltpu.VMEM((1, 8, CASES, 8, LANES), F32)
     table = pltpu.VMEM((2, CASES, 8, 8, LANES), F32)
     gathered = pltpu.VMEM((2, 8, CASES, 8, LANES), F32)
 
     send = call(first_kernel, "first", f32(everyone, CASES, modes), [HBM] * 3,
-                [held(loads), held(precond), held(corner_map), copies(3)], 4_000_000,
+                [held(loads), held(precond), held(corner_map), copies(6)], 4_000_000,
                 )(in_hbm(loads), in_hbm(precond), in_hbm(corner_map))
     got = lax.all_to_all(send, ("gx", "gy"), 0, 0)
 
     side = f32(SIDE_C + modes, R)
-    params = (loads, dual_op, iface, precond, corner_map, elem_stiff, elem_dofs, density, passive)
-    keep, mine_e, mine_o, inverse, pack, weight, spot, spot_kp = call(
-        side_kernel, "sides",
-        (f32(KEEP_S + 8, unknowns), side, side, jax.ShapeDtypeStruct((2, 8, unknowns), jnp.int32),
-         jax.ShapeDtypeStruct((8, 8, LANES), jnp.int32), f32(tiles + 1, 8, LANES),
-         jax.ShapeDtypeStruct((8, LANES), jnp.int32), f32(9, 8, LANES)),
-        [HBM] * 9, [stiff if a is elem_stiff else held(a) for a in params] + [copies(9)], 10_000_000,
+    params = (loads, dual_op, iface, precond, corner_map)
+    keep, mine_e, mine_o = call(
+        side_kernel, "sides", (f32(KEEP_S + 8, unknowns), side, side),
+        [HBM] * 5, [held(a) for a in params] + [copies(5)], 8_000_000,
     )(*(in_hbm(a) for a in params))
     theirs_e = swap_over(mine_e, "gx", x_even)
     theirs_o = swap_over(mine_o, "gx", x_odd)
 
+    field = f32(EARLY + 1, CASES, 8, LANES)
+    params = (iface, corner_map, elem_stiff, density, passive)
+    index, inverse, chigh, clow, pack, weight, spot, spot_kp, kp, pp = call(
+        early_kernel, "early",
+        (s32(2, 8, R), s32(2, 8, unknowns), bf16(modes, unknowns), bf16(modes, unknowns), s32(8, 8, LANES),
+         f32(tiles + 1, 8, LANES), s32(8, LANES), f32(10, 8, LANES), f32(EARLY + 1, 8, CASES, 8, LANES), field),
+        [VMEM] * 2 + [HBM] * 5,
+        [one_table, one_gathered] + [stiff if a is elem_stiff else held(a) for a in params] + [copies(5)], 18_000_000,
+    )(keep, elem_dofs, *(in_hbm(a) for a in params))
+    got, spot = lax.optimization_barrier((got, spot))
+
     send, t = call(
         second_kernel, "second", (f32(everyone, 2 * CASES, modes), f32(CASES, unknowns)),
-        [VMEM] * 11 + [HBM] * 3, [held(precond), held(dual_op), stiff, copies(3)], 9_000_000,
-    )(got, keep, mine_e, mine_o, theirs_e, theirs_o, inverse, spot, spot_kp, coarse_inv, corner_map,
+        [VMEM] * 13 + [HBM] * 3, [held(precond), held(dual_op), stiff, copies(3)], 9_000_000,
+    )(got, keep, mine_e, mine_o, theirs_e, theirs_o, index, inverse, spot, spot_kp, coarse_inv, chigh, clow,
       in_hbm(precond), in_hbm(dual_op), in_hbm(elem_stiff))
     got = lax.all_to_all(send, ("gx", "gy"), 0, 0)
 
     row = f32(2 * FIELDS, LANES)
     col = f32(FIELDS, LANES)
     row_e, row_o, col_e, col_o = call(
-        edge_kernel, "edges", (row, row, col, col), [VMEM] * 4 + [HBM],
-        [table, gathered, pltpu.VMEM((FIELDS, 8, LANES), F32), stiff, copies(1)], 4_000_000,
-    )(keep, t, pack, weight, in_hbm(elem_stiff))
+        edge_kernel, "edges", (row, row, col, col), [VMEM] * 5 + [HBM],
+        [one_table, one_gathered, pltpu.VMEM((FIELDS, 8, LANES), F32), stiff, copies(1)], 4_000_000,
+    )(t, pack, weight, kp, pp, in_hbm(elem_stiff))
     near = [swap_over(row_e, "gx", x_even), swap_over(row_o, "gx", x_odd),
             swap_over(col_e, "gy", y_even), swap_over(col_o, "gy", y_odd)]
 
-    field = f32(tiles, CASES, 8, LANES)
-    pp, pt, tt = call(
-        field_kernel, "fields", (field,) * 3, [VMEM] * 4 + [HBM], [table, gathered, stiff, copies(1)], 36_000_000,
-    )(keep, t, elem_dofs, weight, in_hbm(elem_stiff))
+    late, pt, tt = call(
+        field_kernel, "fields",
+        (f32(tiles - EARLY, CASES, 8, LANES), f32(tiles, CASES, 8, LANES), f32(tiles, CASES, 8, LANES)),
+        [VMEM] * 5 + [HBM], [table, gathered, stiff, copies(1)], 36_000_000,
+    )(keep, t, elem_dofs, weight, kp, in_hbm(elem_stiff))
 
     adjoint, sens = call(
-        last_kernel, "last", (f32(CASES, 1, unknowns), f32(ex, ey)), [VMEM] * 13, [], 4_000_000,
-    )(got, coarse_inv, keep, t, pp, pt, tt, col_e, col_o, *near)
+        last_kernel, "last", (f32(CASES, 1, unknowns), f32(ex, ey)), [VMEM] * 14, [], 4_000_000,
+    )(got, coarse_inv, keep, t, pp, late, pt, tt, col_e, col_o, *near)
     return adjoint, sens
 
 

time: 48.6 us -> 46.5 us (0.957)
  waiting for transfers between devices: 2.28 us -> 0.02 us
  Pallas kernels: 23.5 us -> 24.6 us
  starting transfers between devices: 21.6 us -> 20.5 us
    ppermute x5, waiting for transfers between devices: 2.28 us -> 0.01 us  [swap_over(): return lax.ppermute(array, axis, pairs) if pairs else jnp.zeros_like(array)]
    pallas_call x3 -> x4, Pallas kernels: 16.1 us -> 17.3 us  [the longest x1 7.63 us: on_device(): call(field_kernel, 'fields', (f32(tiles - EARLY, CASES, 8, LANES), f32(ti...]
    all_to_all x2, starting transfers between devices: 12.9 us -> 11.8 us  [on_device(): got = lax.all_to_all(send, ('gx', 'gy'), 0, 0)]
  transfers between devices with their start and end apart: 7 -> 7, of which waited for: 1 -> 0; matrix products, arithmetic and copies ran while one was open for 0% -> 0% of each run, Pallas kernels for 33% -> 38%
where the time goes in v5:
time: 46.5 us; the launch traced here: 46 us
  Pallas kernels  24.6 us (53%)
  starting transfers between devices  20.5 us (44%)
  between operations  0.8 us (2%)
    all_to_all x2, starting transfers between devices, on_device(): got = lax.all_to_all(send, ('gx', 'gy'), 0, 0)  11.8 us
    ppermute x5, starting transfers between devices, swap_over(): return lax.ppermute(array, axis, pairs) if pairs else jnp.zeros_like(array)  8.74 us
    pallas_call x1, Pallas kernels, on_device(): call(field_kernel, 'fields', (f32(tiles - EARLY, CASES, 8, LANES), f32(ti...  7.63 us
    pallas_call x1, Pallas kernels, on_device(): call(early_kernel, 'early', (s32(2, 8, R), s32(2, 8, unknowns), bf16(mode...  5.68 us
    pallas_call x1, Pallas kernels, on_device(): call(second_kernel, 'second', (f32(everyone, 2 * CASES, modes), f32(CASES...  3.5 us
    pallas_call x1, Pallas kernels, on_device(): call(side_kernel, 'sides', (f32(KEEP_S + 8, unknowns), side, side), [HBM]...  2.6 us
    pallas_call x1, Pallas kernels, on_device(): call(first_kernel, 'first', f32(everyone, CASES, modes), [HBM] * 3, [held...  2.31 us
    pallas_call x1, Pallas kernels, on_device(): call(last_kernel, 'last', (f32(CASES, 1, unknowns), f32(ex, ey)), [VMEM]...  1.5 us
  transfers between devices with their start and end apart: 7, of which 0 were waited for; matrix products, arithmetic and copies ran while one was open for 0% of the time, Pallas kernels for 38%

profile of v5, /device:TPU:1, one launch (start us, length us, event | category | flops | bytes accessed | tf_op | source)
XLA Modules:
  0.0 46.0 jit_solution(4484212619590273558)
XLA Ops:
  0.6 0.0 copy-start
  0.6 2.3 %first.1 = f32[32,8,128]{2,1,0:T(8,128)} custom-call(f32[8,1,1024]{2,1,0:T(1,128)} %loads_hbm.3, f32[1,1024]{1,0:T(1,128)} %pre_hbm.5, f32[1,128,1024]{2,1,0:T(8,128)} %corner_hbm.5), custom_call_target="tpu_custom_call" | custom-call | flops 1000000 | bytes 4000000 | tf_op jit(solution)/shard_map/first/pallas_call | solution.py:546
  3.0 0.0 copy-start.1
  3.0 7.1 %all-to-all-start = ((f32[32,8,128]{2,1,0:T(8,128)}), f32[32,8,128]{2,1,0:T(8,128)S(1)}, u32[]{:S(2)}, u32[]{:S(2)}) async-start(f32[32,8,128]{2,1,0:T(8,128)} %first.1), calls=%async_computation | async-start | bytes 262144 | tf_op jit(solution)/shard_map/all_to_all | solution.py:549
  10.1 2.6 %sides.1 = (f32[32,1024]{1,0:T(8,128)S(1)}, f32[152,128]{1,0:T(8,128)S(1)}, f32[152,128]{1,0:T(8,128)S(1)}) custom-call(f32[8,1,1024]{2,1,0:T(1,128)} %loads_hbm.3, bf16[1,1024,1024]{2,1,0:T(8,128)(2,1)} %op_hbm.3, s32[1,1,1024]{2,1,0:T(1,128)} %iface_hbm.3, f32[1,1024]{1,0:T(1,128)} %pre_hbm.5, f32[1,128,1024]{2,1,0:T(8,128)} %corner_hbm.5), custom_call_target="tpu_custom_call" | custom-call | flops 1000000 | bytes 8000000 | tf_op jit(solution)/shard_map/sides/pallas_call | solution.py:553
  12.7 0.3 collective-permute-start
  13.0 3.4 %collective-permute-start.1 = (f32[152,128]{1,0:T(8,128)S(1)}, f32[152,128]{1,0:T(8,128)S(1)}, u32[]{:S(2)}, u32[]{:S(2)}) collective-permute-start(f32[152,128]{1,0:T(8,128)S(1)} %get-tuple-element.30.mine_o_ref), channel_id=1, source_target_pairs={{2,4},{6,8},{10,12},{14,16},{18,20},{22,24},{26,28},{4,2},{8,6},{1... | collective-permute-start | bytes 233480 | tf_op jit(solution)/shard_map/ppermute | solution.py:493
  16.4 0.0 copy-done
  16.5 5.7 %early.1 = (s32[2,8,128]{2,1,0:T(8,128)S(1)}, s32[2,8,1024]{2,1,0:T(8,128)S(1)}, bf16[128,1024]{1,0:T(8,128)(2,1)S(1)}, bf16[128,1024]{1,0:T(8,128)(2,1)S(1)}, s...) custom-call(f32[32,1024]{1,0:T(8,128)S(1)} %get-tuple-element.26.kee, ...), custom_call_target="tpu_custom_call" | custom-call | flops 1000000 | bytes 18000000 | tf_op jit(solution)/shard_map/early/pallas_call | solution.py:562
  22.1 0.0 all-to-all-done.got_ref
  22.1 0.0 collective-permute-done.theirs_e_ref
  22.2 0.0 collective-permute-done.1.theirs_o_ref
  22.2 0.0 copy-done.1
  22.2 3.5 %second.1 = (f32[32,16,128]{2,1,0:T(8,128)}, f32[8,1024]{1,0:T(8,128)S(1)}) custom-call(f32[32,8,128]{2,1,0:T(8,128)S(1)} %all-to-all-done.got_ref, f32[32,1024]{1,0:T(8,128)S(1)} %get-tuple-element.26.keep_ref, f32[152,128]{1,0:T(8,128)S(1)} %get-tuple-element.29.mine_e_ref, f32[152,128]{1,0:T(8,128)S(1)} %get-tuple-element.30.mine_o_ref, ...), custom_call_target="tpu_custom_call" | custom-call | flops 1000000 | bytes 9000000 | tf_op jit(solution)/shard_map/second/pallas_call | solution.py:571
  25.7 4.7 %all-to-all-start.1 = ((f32[32,16,128]{2,1,0:T(8,128)}), f32[32,16,128]{2,1,0:T(8,128)S(1)}, u32[]{:S(2)}, u32[]{:S(2)}) async-start(f32[32,16,128]{2,1,0:T(8,128)} %get-tuple-element.37), calls=%async_computation.1 | async-start | bytes 524288 | tf_op jit(solution)/shard_map/all_to_all | solution.py:576
  30.4 1.4 %edges.1 = (f32[48,128]{1,0:T(8,128)S(1)}, f32[48,128]{1,0:T(8,128)S(1)}, f32[24,128]{1,0:T(8,128)S(1)}, f32[24,128]{1,0:T(8,128)S(1)}) custom-call(f32[8,1024]{1,0:T(8,128)S(1)} %get-tuple-element.38.t_ref, s32[8,8,128]{2,1,0:T(8,128)S(1)} %get-tuple-element.45.pack_ref, f32[9,8,128]{2,1,0:T(8,128)S(1)} %get-tuple-element.40.weight_ref, ...), custom_call_target="tpu_custom_call" | custom-call | flops 1000000 | bytes 4000000 | tf_op jit(solution)/shard_map/edges/pallas_call | solution.py:580
  31.8 0.3 collective-permute-start.2
  32.1 3.4 %collective-permute-start.3 = (f32[48,128]{1,0:T(8,128)S(1)}, f32[48,128]{1,0:T(8,128)S(1)}, u32[]{:S(2)}, u32[]{:S(2)}) collective-permute-start(f32[48,128]{1,0:T(8,128)S(1)} %get-tuple-element.49), channel_id=1, source_target_pairs={{2,4},{6,8},{10,12},{14,16},{18,20},{22,24},{26,28},{4,2},{8,6},{1... | collective-permute-start | bytes 73736 | tf_op jit(solution)/shard_map/ppermute | solution.py:493
  35.6 1.2 %collective-permute-start.4 = (f32[24,128]{1,0:T(8,128)S(1)}, f32[24,128]{1,0:T(8,128)S(1)}, u32[]{:S(2)}, u32[]{:S(2)}) collective-permute-start(f32[24,128]{1,0:T(8,128)S(1)} %get-tuple-element.46.mine_ye_ref), channel_id=1, source_target_pairs={{0,1},{1,0},{2,3},{3,2},{4,5},{5,4},{6,7},{7,6},{8,9},{9,8},{10,11... | collective-permute-start | bytes 36872 | tf_op jit(solution)/shard_map/ppermute | solution.py:493
  36.8 7.6 %fields.1 = (f32[3,8,8,128]{3,2,1,0:T(8,128)S(1)}, f32[8,8,8,128]{3,2,1,0:T(8,128)S(1)}, f32[8,8,8,128]{3,2,1,0:T(8,128)S(1)}) custom-call(f32[32,1024]{1,0:T(8,128)S(1)} %get-tuple-element.26.keep_ref, f32[8,1024]{1,0:T(8,128)S(1)} %get-tuple-element.38.t_ref, s32[8,64,128]{2,1,0:T(8,128)S(1)} %copy-done, f32[9,8,128]{2,1,0:T(8,128)S(1)} %get-tuple-element.40.weight_ref, ...), custom_call_target="tpu_custom_call" | custom-call | flops 1000000 | bytes 36000000 | tf_op jit(solution)/shard_map/fields/pallas_call | solution.py:587
  44.5 0.0 collective-permute-done.4.ye_ref
  44.5 0.0 collective-permute-done.2.xe_ref
  44.5 0.0 collective-permute-done.3.xo_ref
  44.5 0.0 all-to-all-done.1.got_ref
  44.5 1.5 %last.1 = (f32[8,1,1024]{2,1,0:T(1,128)}, f32[64,128]{1,0:T(8,128)}) custom-call(f32[32,16,128]{2,1,0:T(8,128)S(1)} %all-to-all-done.1.got_ref, f32[128,128]{1,0:T(8,128)S(1)} %copy-done.1, f32[32,1024]{1,0:T(8,128)S(1)} %get-tuple-element.26.keep_ref, f32[8,1024]{1,0:T(8,128)S(1)} %get-tuple-element.38.t_ref, ...), custom_call_target="tpu_custom_call" | custom-call | flops 1000000 | bytes 4000000 | tf_op jit(solution)/shard_map/last/pallas_call | solution.py:593
  (1 shorter events, 0.0 us)
Async XLA Ops:
  0.6 15.8 %copy-start = (s32[8,64,128]{2,1,0:T(8,128)S(1)}, s32[8,64,128]{2,1,0:T(8,128)}, u32[]{:S(2)}) copy-start(s32[8,64,128]{2,1,0:T(8,128)} %dofs_ref.3) | copy-start | bytes 786436
  3.0 19.2 %copy-start.1 = (f32[128,128]{1,0:T(8,128)S(1)}, f32[128,128]{1,0:T(8,128)}, u32[]{:S(2)}) copy-start(f32[128,128]{1,0:T(8,128)} %coarse_ref.3) | copy-start | bytes 196612
  3.0 19.2 %all-to-all-start = ((f32[32,8,128]{2,1,0:T(8,128)}), f32[32,8,128]{2,1,0:T(8,128)S(1)}, u32[]{:S(2)}, u32[]{:S(2)}) async-start(f32[32,8,128]{2,1,0:T(8,128)} %first.1), calls=%async_computation | async-start | bytes 262144 | tf_op jit(solution)/shard_map/all_to_all | solution.py:549
  12.7 9.5 %collective-permute-start = (f32[152,128]{1,0:T(8,128)S(1)}, f32[152,128]{1,0:T(8,128)S(1)}, u32[]{:S(2)}, u32[]{:S(2)}) collective-permute-start(f32[152,128]{1,0:T(8,128)S(1)} %get-tuple-element.29.mine_e_ref), channel_id=1, source_target_pairs={{0,2},{4,6},{8,10},{12,14},{16,18},{20,22},{24,26},{28,30},{2,0},{... | collective-permute-start | bytes 233480 | tf_op jit(solution)/shard_map/ppermute | solution.py:493
  13.0 9.1 %collective-permute-start.1 = (f32[152,128]{1,0:T(8,128)S(1)}, f32[152,128]{1,0:T(8,128)S(1)}, u32[]{:S(2)}, u32[]{:S(2)}) collective-permute-start(f32[152,128]{1,0:T(8,128)S(1)} %get-tuple-element.30.mine_o_ref), channel_id=1, source_target_pairs={{2,4},{6,8},{10,12},{14,16},{18,20},{22,24},{26,28},{4,2},{8,6},{1... | collective-permute-start | bytes 233480 | tf_op jit(solution)/shard_map/ppermute | solution.py:493
  25.7 18.8 %all-to-all-start.1 = ((f32[32,16,128]{2,1,0:T(8,128)}), f32[32,16,128]{2,1,0:T(8,128)S(1)}, u32[]{:S(2)}, u32[]{:S(2)}) async-start(f32[32,16,128]{2,1,0:T(8,128)} %get-tuple-element.37), calls=%async_computation.1 | async-start | bytes 524288 | tf_op jit(solution)/shard_map/all_to_all | solution.py:576
  31.8 12.7 %collective-permute-start.2 = (f32[48,128]{1,0:T(8,128)S(1)}, f32[48,128]{1,0:T(8,128)S(1)}, u32[]{:S(2)}, u32[]{:S(2)}) collective-permute-start(f32[48,128]{1,0:T(8,128)S(1)} %get-tuple-element.48), channel_id=1, source_target_pairs={{0,2},{4,6},{8,10},{12,14},{16,18},{20,22},{24,26},{28,30},{2,0},{... | collective-permute-start | bytes 73736 | tf_op jit(solution)/shard_map/ppermute | solution.py:493
  32.1 12.3 %collective-permute-start.3 = (f32[48,128]{1,0:T(8,128)S(1)}, f32[48,128]{1,0:T(8,128)S(1)}, u32[]{:S(2)}, u32[]{:S(2)}) collective-permute-start(f32[48,128]{1,0:T(8,128)S(1)} %get-tuple-element.49), channel_id=1, source_target_pairs={{2,4},{6,8},{10,12},{14,16},{18,20},{22,24},{26,28},{4,2},{8,6},{1... | collective-permute-start | bytes 73736 | tf_op jit(solution)/shard_map/ppermute | solution.py:493
  35.6 8.9 %collective-permute-start.4 = (f32[24,128]{1,0:T(8,128)S(1)}, f32[24,128]{1,0:T(8,128)S(1)}, u32[]{:S(2)}, u32[]{:S(2)}) collective-permute-start(f32[24,128]{1,0:T(8,128)S(1)} %get-tuple-element.46.mine_ye_ref), channel_id=1, source_target_pairs={{0,1},{1,0},{2,3},{3,2},{4,5},{5,4},{6,7},{7,6},{8,9},{9,8},{10,11... | collective-permute-start | bytes 36872 | tf_op jit(solution)/shard_map/ppermute | solution.py:493

commit v6 on v5

--- a/solution.py
+++ b/solution.py
@@ -77,6 +77,16 @@
 
 def is_odd(axis):
     return lax.axis_index(axis) & 1 == 1
+
+
+def sides_there(axis):
+    at, size = lax.axis_index(axis), lax.axis_size(axis)
+    return jnp.where(at > 0, 1.0, 0.0), jnp.where(at < size - 1, 1.0, 0.0)
+
+
+def op_dot(vec, op_ref):
+    out = lax.dot_general(halves(vec), op_ref[0], (((1,), (1,)), ((), ())), preferred_element_type=F32)
+    return out[:CASES], out[CASES:]
 
 
 def at_lanes(columns, first=0):
@@ -148,7 +158,8 @@
 
 
 def side_kernel(loads_hbm, op_hbm, iface_hbm, pre_hbm, corner_hbm,
-                keep_ref, even_ref, odd_ref, loads_ref, op_ref, iface_ref, pre_ref, corner_ref, sems):
+                keep_ref, even_ref, odd_ref, index_ref, inverse_ref, chigh_ref, clow_ref,
+                loads_ref, op_ref, iface_ref, pre_ref, corner_ref, sems):
     copies = fetch(sems, ((loads_hbm, loads_ref), (pre_hbm, pre_ref), (iface_hbm, iface_ref),
                           (corner_hbm, corner_ref), (op_hbm, op_ref)))
     for copy in copies[:4]:
@@ -167,30 +178,6 @@
         for j in range(corner_ref.shape[1] // 8):
             rows = corner_ref[0, 8 * j : 8 * j + 8]
             out[SIDE_C + 8 * j : SIDE_C + 8 * j + 8] = scale * pick(blocks_of(rows), where)
-    copies[4].wait()
-    both = lax.dot_general(halves(p), op_ref[0], (((1,), (1,)), ((), ())), preferred_element_type=F32)
-    y, rest = both[:CASES], both[CASES:]
-    keep_ref[KEEP_Y : KEEP_Y + 8] = y
-    keep_ref[KEEP_REST : KEEP_REST + 8] = rest
-    keep_ref[KEEP_S : KEEP_S + 8, :LANES] = at_lanes((lane_sum(loads * p), lane_sum(p * rest)))
-    for where, scale, out in chosen:
-        out[SIDE_Y : SIDE_Y + 8] = scale * pick(blocks_of(y), where)
-
-
-def early_kernel(keep_ref, dofs_ref, iface_hbm, corner_hbm, stiff_hbm, density_hbm, passive_hbm,
-                 index_ref, inverse_ref, chigh_ref, clow_ref, pack_ref, weight_ref, spot_ref, spot_kp_ref,
-                 kp_ref, pp_ref,
-                 table_ref, u_ref, iface_ref, corner_ref, stiff_ref, density_ref, passive_ref, sems):
-    copies = fetch(sems, ((iface_hbm, iface_ref), (stiff_hbm, stiff_ref), (density_hbm, density_ref),
-                          (passive_hbm, passive_ref), (corner_hbm, corner_ref)))
-    p = keep_ref[KEEP_P : KEEP_P + 8]
-    make_tables(table_ref, p)
-    for a in range(0, 8, 2):
-        first, second = edge_tiles(dofs_ref[a].astype(F32), dofs_ref[a + 1].astype(F32))
-        pack_ref[a] = first.astype(jnp.int32)
-        pack_ref[a + 1] = second.astype(jnp.int32)
-    for copy in copies:
-        copy.wait()
     for side, idx in enumerate(side_indices(iface_ref)):
         index_ref[side] = idx
         column = jnp.transpose(jnp.broadcast_to(idx[0:1], (R, R)))
@@ -200,6 +187,28 @@
             found = jnp.sum(jnp.where(column == at, number, 0), axis=0, keepdims=True)
             inverse_ref[side, :, LANES * h : LANES * (h + 1)] = jnp.broadcast_to(found, (8, LANES))
     chigh_ref[...], clow_ref[...] = split(corner_ref[0])
+    copies[4].wait()
+    y, rest = op_dot(p, op_ref)
+    keep_ref[KEEP_Y : KEEP_Y + 8] = y
+    keep_ref[KEEP_REST : KEEP_REST + 8] = rest
+    keep_ref[KEEP_S : KEEP_S + 8, :LANES] = at_lanes((lane_sum(loads * p), lane_sum(p * rest)))
+    for where, scale, out in chosen:
+        out[SIDE_Y : SIDE_Y + 8] = scale * pick(blocks_of(y), where)
+
+
+def early_kernel(keep_ref, dofs_ref, stiff_hbm, density_hbm, passive_hbm,
+                 pack_ref, weight_ref, spot_ref, spot_kp_ref,
+                 kp_ref, pp_ref, table_ref, u_ref, other_ref, all_dofs_ref, all_weight_ref,
+                 stiff_ref, density_ref, passive_ref, sems):
+    copies = fetch(sems, ((stiff_hbm, stiff_ref), (density_hbm, density_ref), (passive_hbm, passive_ref)))
+    p = keep_ref[KEEP_P : KEEP_P + 8]
+    make_tables(table_ref, p)
+    for a in range(0, 8, 2):
+        first, second = edge_tiles(dofs_ref[a].astype(F32), dofs_ref[a + 1].astype(F32))
+        pack_ref[a] = first.astype(jnp.int32)
+        pack_ref[a + 1] = second.astype(jnp.int32)
+    for copy in copies:
+        copy.wait()
     rho = density_ref[...]
     weight = jnp.where(passive_ref[...] == 1, 0.0, -penalty * rho * rho)
     ex = weight.shape[0]
@@ -219,23 +228,29 @@
     spot_kp_ref[8] = spot_weight
     spot_kp_ref[9] = pltpu.roll(jnp.where(lane < 4, spot_weight * pp, 0.0), CORNER_PP, 1)
 
-    def work(dofs, at, scale):
-        gather_tile(dofs, table_ref, u_ref, 0)
+    for i in range(EARLY):
+        for a in range(8):
+            all_dofs_ref[i, a] = dofs_ref[a, 8 * i : 8 * i + 8]
+        all_weight_ref[i] = weight[8 * i : 8 * i + 8]
+    for a in range(8):
+        all_dofs_ref[EARLY, a] = pack_ref[a]
+    all_weight_ref[EARLY] = weight_ref[ex // 8]
+
+    def gather(i, ref):
+        gather_tile(lambda a: all_dofs_ref[i, a], table_ref, ref, 0)
+
+    def fields(i, ref):
+        scale = all_weight_ref[i]
         for c in range(CASES):
-            u = [u_ref[0, a, c] for a in range(8)]
+            u = [ref[0, a, c] for a in range(8)]
             pp = None
             for a in range(8):
                 v = stiff_row(stiff_ref, a, u)
-                kp_ref[at, a, c] = v
+                kp_ref[i, a, c] = v
                 pp = u[a] * v if pp is None else pp + u[a] * v
-            pp_ref[at, c] = scale * pp
-
-    @pl.loop(0, EARLY)
-    def _(tile):
-        rows = pl.ds(pl.multiple_of(8 * tile, 8), 8)
-        work(lambda a: dofs_ref[a, rows, :], tile, weight_ref[tile])
-
-    work(lambda a: pack_ref[a], EARLY, weight_ref[ex // 8])
+            pp_ref[i, c] = scale * pp
+
+    staggered(EARLY + 1, gather, fields, (u_ref, other_ref))
 
 
 def spread(values, inverse):
@@ -250,7 +265,7 @@
 def second_kernel(got_ref, keep_ref, mine_e_ref, mine_o_ref, theirs_e_ref, theirs_o_ref, index_ref, inverse_ref,
                   spot_ref, spot_kp_ref, coarse_ref, chigh_ref, clow_ref, pre_hbm, op_hbm, stiff_hbm,
                   send_ref, t_ref, pre_ref, op_ref, stiff_ref, sems):
-    copies = fetch(sems, ((pre_hbm, pre_ref), (op_hbm, op_ref), (stiff_hbm, stiff_ref)))
+    copies = fetch(sems, ((pre_hbm, pre_ref), (stiff_hbm, stiff_ref), (op_hbm, op_ref)))
     total = got_ref[0]
     for d in range(1, got_ref.shape[0]):
         total = total + got_ref[d]
@@ -258,25 +273,25 @@
     p = keep_ref[KEEP_P : KEEP_P + 8]
     base = keep_ref[KEEP_Y : KEEP_Y + 8]
     pairs = ((mine_e_ref, theirs_e_ref), (mine_o_ref, theirs_o_ref))
+    below, above = sides_there("gx")
+    x_odd = is_odd("gx")
+    couplings = [-coupling * jnp.where(x_odd, a, b) for a, b in ((below, above), (above, below))]
     for side, (_, theirs) in enumerate(pairs):
-        base = base + spread(-coupling * theirs[SIDE_P : SIDE_P + 8], inverse_ref[side])
+        base = base + spread(couplings[side] * theirs[SIDE_P : SIDE_P + 8], inverse_ref[side])
     w = split_dot(total, split(coarse_ref[...]), 1)
     q = base + split_dot(w, corner, 0)
-    for copy in copies:
-        copy.wait()
+    copies[0].wait()
     t = pre_ref[...] * q
     t_ref[...] = t
-    both = lax.dot_general(halves(t), op_ref[0], (((1,), (1,)), ((), ())), preferred_element_type=F32)
     g = split_dot(t, corner, 1)
-    tlt = lane_sum(t * (both[:CASES] + both[CASES:]))
+    tlt = None
     for side, (mine, theirs) in enumerate(pairs):
         t_mine = pick(blocks_of(t), pattern(index_ref[side]))
         t_theirs = theirs[SIDE_Y : SIDE_Y + 8] - coupling * theirs[SIDE_M : SIDE_M + 8] * mine[SIDE_P : SIDE_P + 8]
         t_theirs = t_theirs + split_dot(w, split(theirs[SIDE_C:]), 0)
-        tlt = tlt - coupling * lane_sum(t_mine * t_theirs)
-    rest = keep_ref[KEEP_REST : KEEP_REST + 8]
-    block = keep_ref[KEEP_S : KEEP_S + 8, :LANES]
-    block = block + at_lanes((lane_sum(p * q), lane_sum(q * t), tlt, lane_sum(t * rest)), PQ)
+        term = couplings[side] * lane_sum(t_mine * t_theirs)
+        tlt = term if tlt is None else tlt + term
+    copies[1].wait()
     u = corner_values(t, spot_ref[...])
     pt = tt = None
     for a in range(8):
@@ -284,9 +299,16 @@
         pt, tt = (one, two) if pt is None else (pt + one, tt + two)
     lane = lax.broadcasted_iota(jnp.int32, (CASES, LANES), 1)
     pt, tt = jnp.where(lane < 4, pt, 0.0), jnp.where(lane < 4, spot_kp_ref[8] * tt, 0.0)
+    rest = keep_ref[KEEP_REST : KEEP_REST + 8]
+    block = keep_ref[KEEP_S : KEEP_S + 8, :LANES]
     block = block + spot_kp_ref[9] + pltpu.roll(pt, CORNER_PT, 1) + pltpu.roll(tt, CORNER_TT, 1)
+    block = block + at_lanes((lane_sum(p * q), lane_sum(q * t), tlt, lane_sum(t * rest)), PQ)
     for d in range(send_ref.shape[0]):
         send_ref[d, :CASES] = g
+    copies[2].wait()
+    high, low = op_dot(t, op_ref)
+    block = block + at_lanes((lane_sum(t * (high + low)),), TLT)
+    for d in range(send_ref.shape[0]):
         send_ref[d, CASES:] = block
 
 
@@ -304,6 +326,28 @@
         for c in range(CASES):
             for i in which:
                 u_ref[i, a, c] = pick([table_ref[i, c, h] for h in range(8)], where)
+
+
+def staggered(count, gather, fields, refs, ready=()):
+    gather(0, refs[0])
+    for copy in ready:
+        copy.wait()
+    pairs = (count - 1) // 2
+
+    @pl.loop(0, pairs)
+    def _(k):
+        i = 2 * k
+        gather(i + 1, refs[1])
+        fields(i, refs[0])
+        gather(i + 2, refs[0])
+        fields(i + 1, refs[1])
+
+    if count % 2 == 0:
+        gather(count - 1, refs[1])
+        fields(count - 2, refs[0])
+        fields(count - 1, refs[1])
+    else:
+        fields(count - 1, refs[0])
 
 
 def t_fields(t, kp, stiff_ref):
@@ -341,39 +385,42 @@
 
 
 def field_kernel(keep_ref, t_ref, dofs_ref, weight_ref, kp_ref, stiff_hbm, pp_ref, pt_ref, tt_ref,
-                 table_ref, u_ref, stiff_ref, sems):
+                 table_ref, u_ref, other_ref, stiff_ref, sems):
     copies = fetch(sems, ((stiff_hbm, stiff_ref),))
     make_tables(table_ref, t_ref[...], keep_ref[KEEP_P : KEEP_P + 8])
-    copies[0].wait()
 
     def rows_of(tile):
         return pl.ds(pl.multiple_of(8 * tile, 8), 8)
 
-    def t_at(c):
-        return [u_ref[0, a, c] for a in range(8)]
-
-    @pl.loop(0, EARLY)
-    def _(tile):
-        rows = rows_of(tile)
-        gather_tile(lambda a: dofs_ref[a, rows, :], table_ref, u_ref, 0)
+    def t_at(ref, c):
+        return [ref[0, a, c] for a in range(8)]
+
+    def gather(tile, ref):
+        gather_tile(lambda a: dofs_ref[a, rows_of(tile), :], table_ref, ref, 0)
+
+    def fields(tile, ref):
         scale = weight_ref[tile]
         for c in range(CASES):
-            pt, tt = t_fields(t_at(c), [kp_ref[tile, a, c] for a in range(8)], stiff_ref)
+            pt, tt = t_fields(t_at(ref, c), [kp_ref[tile, a, c] for a in range(8)], stiff_ref)
             pt_ref[tile, c], tt_ref[tile, c] = scale * pt, scale * tt
 
-    @pl.loop(EARLY, pt_ref.shape[0])
-    def _(tile):
-        rows = rows_of(tile)
-        gather_tile(lambda a: dofs_ref[a, rows, :], table_ref, u_ref, 0, 1)
-        scale = weight_ref[tile]
+    staggered(EARLY, gather, fields, (u_ref, other_ref), copies)
+
+    def gather_both(i, ref):
+        gather_tile(lambda a: dofs_ref[a, rows_of(i + EARLY), :], table_ref, ref, 0, 1)
+
+    def fields_both(i, ref):
+        scale = weight_ref[i + EARLY]
         for c in range(CASES):
-            p = [u_ref[1, a, c] for a in range(8)]
+            p = [ref[1, a, c] for a in range(8)]
             kp = [stiff_row(stiff_ref, a, p) for a in range(8)]
             pp = p[0] * kp[0]
             for a in range(1, 8):
                 pp = pp + p[a] * kp[a]
-            pt, tt = t_fields(t_at(c), kp, stiff_ref)
-            pp_ref[tile - EARLY, c], pt_ref[tile, c], tt_ref[tile, c] = scale * pp, scale * pt, scale * tt
+            pt, tt = t_fields(t_at(ref, c), kp, stiff_ref)
+            pp_ref[i, c], pt_ref[i + EARLY, c], tt_ref[i + EARLY, c] = scale * pp, scale * pt, scale * tt
+
+    staggered(pt_ref.shape[0] - EARLY, gather_both, fields_both, (u_ref, other_ref))
 
 
 def last_kernel(got_ref, coarse_ref, keep_ref, t_ref, early_ref, late_ref, pt_ref, tt_ref,
@@ -413,10 +460,7 @@
 
     ex, ey = grad.shape
     x_odd, y_odd = is_odd("gx"), is_odd("gy")
-    has = []
-    for axis in ("gx", "gy"):
-        at, size = lax.axis_index(axis), lax.axis_size(axis)
-        has += [jnp.where(at > 0, 1.0, 0.0), jnp.where(at < size - 1, 1.0, 0.0)]
+    has = sides_there("gx") + sides_there("gy")
 
     def choose(flag, a, b):
         return jnp.where(jnp.broadcast_to(flag, a.shape), a, b)
@@ -424,10 +468,13 @@
     def two(a, b, flag):
         return choose(flag, a, b), choose(flag, b, a)
 
+    def both(values, there):
+        return [v * flag for v, flag in zip(values, there)]
+
     rows = [[combine(ref[FIELDS * i : FIELDS * (i + 1)]) for i in range(2)] for ref in (xe_ref, xo_ref)]
-    g_below1, g_above1 = two(rows[0][0], rows[1][0], x_odd)
-    g_below2, g_above2 = two(rows[0][1], rows[1][1], x_odd)
-    before, after = two(combine(ye_ref[...]), combine(yo_ref[...]), y_odd)
+    g_below1, g_above1 = both(two(rows[0][0], rows[1][0], x_odd), has[:2])
+    g_below2, g_above2 = both(two(rows[0][1], rows[1][1], x_odd), has[:2])
+    before, after = both(two(combine(ye_ref[...]), combine(yo_ref[...]), y_odd), has[2:])
     col_low, col_high = two(combine(mine_ye_ref[...]), combine(mine_yo_ref[...]), y_odd)
     wide_lane = lax.broadcasted_iota(jnp.int32, (CASES, LANES), 1)
     of_lane = jnp.where(wide_lane < CORNER_PT, wide[0], jnp.where(wide_lane < CORNER_TT, wide[1], wide[2]))
@@ -485,6 +532,8 @@
     out = []
     for first in (0, 1):
         pairs = [(i, i + 1) for i in range(first, size - 1, 2)]
+        if first == 1 and size % 2 == 0 and size > 2:
+            pairs.append((size - 1, 0))
         out.append(pairs + [(j, i) for i, j in pairs])
     return out
 
@@ -550,21 +599,23 @@
 
     side = f32(SIDE_C + modes, R)
     params = (loads, dual_op, iface, precond, corner_map)
-    keep, mine_e, mine_o = call(
-        side_kernel, "sides", (f32(KEEP_S + 8, unknowns), side, side),
+    keep, mine_e, mine_o, index, inverse, chigh, clow = call(
+        side_kernel, "sides",
+        (f32(KEEP_S + 8, unknowns), side, side, s32(2, 8, R), s32(2, 8, unknowns), bf16(modes, unknowns),
+         bf16(modes, unknowns)),
         [HBM] * 5, [held(a) for a in params] + [copies(5)], 8_000_000,
     )(*(in_hbm(a) for a in params))
+    theirs_o = swap_over(mine_o, "gx", x_odd)
     theirs_e = swap_over(mine_e, "gx", x_even)
-    theirs_o = swap_over(mine_o, "gx", x_odd)
 
     field = f32(EARLY + 1, CASES, 8, LANES)
-    params = (iface, corner_map, elem_stiff, density, passive)
-    index, inverse, chigh, clow, pack, weight, spot, spot_kp, kp, pp = call(
+    params = (elem_stiff, density, passive)
+    pack, weight, spot, spot_kp, kp, pp = call(
         early_kernel, "early",
-        (s32(2, 8, R), s32(2, 8, unknowns), bf16(modes, unknowns), bf16(modes, unknowns), s32(8, 8, LANES),
-         f32(tiles + 1, 8, LANES), s32(8, LANES), f32(10, 8, LANES), f32(EARLY + 1, 8, CASES, 8, LANES), field),
-        [VMEM] * 2 + [HBM] * 5,
-        [one_table, one_gathered] + [stiff if a is elem_stiff else held(a) for a in params] + [copies(5)], 18_000_000,
+        (s32(8, 8, LANES), f32(tiles + 1, 8, LANES), s32(8, LANES), f32(10, 8, LANES), f32(EARLY + 1, 8, CASES, 8, LANES), field),
+        [VMEM] * 2 + [HBM] * 3,
+        [one_table, one_gathered, one_gathered, pltpu.VMEM((EARLY + 1, 8, 8, LANES), jnp.int32),
+         pltpu.VMEM((EARLY + 1, 8, LANES), F32)] + [stiff if a is elem_stiff else held(a) for a in params] + [copies(3)], 18_000_000,
     )(keep, elem_dofs, *(in_hbm(a) for a in params))
     got, spot = lax.optimization_barrier((got, spot))
 
@@ -581,18 +632,19 @@
         edge_kernel, "edges", (row, row, col, col), [VMEM] * 5 + [HBM],
         [one_table, one_gathered, pltpu.VMEM((FIELDS, 8, LANES), F32), stiff, copies(1)], 4_000_000,
     )(t, pack, weight, kp, pp, in_hbm(elem_stiff))
-    near = [swap_over(row_e, "gx", x_even), swap_over(row_o, "gx", x_odd),
-            swap_over(col_e, "gy", y_even), swap_over(col_o, "gy", y_odd)]
+    ye, yo = swap_over(col_e, "gy", y_even), swap_over(col_o, "gy", y_odd)
+    xo = swap_over(row_o, "gx", x_odd)
+    xe = swap_over(row_e, "gx", x_even)
 
     late, pt, tt = call(
         field_kernel, "fields",
         (f32(tiles - EARLY, CASES, 8, LANES), f32(tiles, CASES, 8, LANES), f32(tiles, CASES, 8, LANES)),
-        [VMEM] * 5 + [HBM], [table, gathered, stiff, copies(1)], 36_000_000,
+        [VMEM] * 5 + [HBM], [table, gathered, gathered, stiff, copies(1)], 36_000_000,
     )(keep, t, elem_dofs, weight, kp, in_hbm(elem_stiff))
 
     adjoint, sens = call(
         last_kernel, "last", (f32(CASES, 1, unknowns), f32(ex, ey)), [VMEM] * 14, [], 4_000_000,
-    )(got, coarse_inv, keep, t, pp, late, pt, tt, col_e, col_o, *near)
+    )(got, coarse_inv, keep, t, pp, late, pt, tt, col_e, col_o, xe, xo, ye, yo)
     return adjoint, sens
 
 

time: 46.5 us -> 45.1 us (0.970)
  the two profiles are of different devices: /device:TPU:1 before, /device:TPU:0 now
where the time goes in v6:
time: 45.1 us; the launch traced here: 44.6 us
  Pallas kernels  22.8 us (51%)
  starting transfers between devices  21.1 us (47%)
  between operations  0.78 us (2%)
    ppermute x5, starting transfers between devices, swap_over(): return lax.ppermute(array, axis, pairs) if pairs else jnp.zeros_like(array)  10.9 us
    all_to_all x2, starting transfers between devices, on_device(): got = lax.all_to_all(send, ('gx', 'gy'), 0, 0)  10.1 us
    pallas_call x1, Pallas kernels, on_device(): call(field_kernel, 'fields', (f32(tiles - EARLY, CASES, 8, LANES), f32(ti...  6.7 us
    pallas_call x1, Pallas kernels, on_device(): call(early_kernel, 'early', (s32(8, 8, LANES), f32(tiles + 1, 8, LANES),...  4.92 us
    pallas_call x1, Pallas kernels, on_device(): call(second_kernel, 'second', (f32(everyone, 2 * CASES, modes), f32(CASES...  3.29 us
    pallas_call x1, Pallas kernels, on_device(): call(side_kernel, 'sides', (f32(KEEP_S + 8, unknowns), side, side, s32(2,...  2.6 us
    pallas_call x1, Pallas kernels, on_device(): call(first_kernel, 'first', f32(everyone, CASES, modes), [HBM] * 3, [held...  2.31 us
    pallas_call x1, Pallas kernels, on_device(): call(last_kernel, 'last', (f32(CASES, 1, unknowns), f32(ex, ey)), [VMEM]...  1.5 us
  transfers between devices with their start and end apart: 7, of which 0 were waited for; matrix products, arithmetic and copies ran while one was open for 0% of the time, Pallas kernels for 35%

profile of v6, /device:TPU:0, one launch (start us, length us, event | category | flops | bytes accessed | tf_op | source)
XLA Modules:
  0.0 44.6 jit_solution(8315386406935054803)
XLA Ops:
  0.6 0.0 copy-start
  0.6 0.0 copy-start.1
  0.6 2.3 %first.1 = f32[32,8,128]{2,1,0:T(8,128)} custom-call(f32[8,1,1024]{2,1,0:T(1,128)} %loads_hbm.3, f32[1,1024]{1,0:T(1,128)} %pre_hbm.5, f32[1,128,1024]{2,1,0:T(8,128)} %corner_hbm.3), custom_call_target="tpu_custom_call" | custom-call | flops 1000000 | bytes 4000000 | tf_op jit(solution)/shard_map/first/pallas_call | solution.py:595
  3.0 7.3 %all-to-all-start = ((f32[32,8,128]{2,1,0:T(8,128)}), f32[32,8,128]{2,1,0:T(8,128)S(1)}, u32[]{:S(2)}, u32[]{:S(2)}) async-start(f32[32,8,128]{2,1,0:T(8,128)} %first.1), calls=%async_computation | async-start | bytes 262144 | tf_op jit(solution)/shard_map/all_to_all | solution.py:598
  10.3 2.6 %sides.1 = (f32[32,1024]{1,0:T(8,128)S(1)}, f32[152,128]{1,0:T(8,128)S(1)}, f32[152,128]{1,0:T(8,128)S(1)}, s32[2,8,128]{2,1,0:T(8,128)S(1)}, s32[2,8,1024]{2,1,...) custom-call(f32[8,1,1024]{2,1,0:T(1,128)} %loads_hbm.3, bf16[1,1024,1024]{2,1,0:T(8,128)(2,1)} %op_hbm.3, ...), custom_call_target="tpu_custom_call" | custom-call | flops 1000000 | bytes 8000000 | tf_op jit(solution)/shard_map/sides/pallas_call | solution.py:602
  12.9 0.3 collective-permute-start
  13.2 4.4 %collective-permute-start.1 = (f32[152,128]{1,0:T(8,128)S(1)}, f32[152,128]{1,0:T(8,128)S(1)}, u32[]{:S(2)}, u32[]{:S(2)}) collective-permute-start(f32[152,128]{1,0:T(8,128)S(1)} %get-tuple-element.30.mine_o_ref), channel_id=1, source_target_pairs={{2,4},{6,8},{10,12},{14,16},{18,20},{22,24},{26,28},{30,0},{4,2},{... | collective-permute-start | bytes 233480 | tf_op jit(solution)/shard_map/ppermute | solution.py:542
  17.6 0.0 copy-done
  17.6 4.9 %early.1 = (s32[8,8,128]{2,1,0:T(8,128)S(1)}, f32[9,8,128]{2,1,0:T(8,128)S(1)}, s32[8,128]{1,0:T(8,128)S(1)}, f32[10,8,128]{2,1,0:T(8,128)S(1)}, f32[6,8,8,8,128...) custom-call(f32[32,1024]{1,0:T(8,128)S(1)} %get-tuple-element.26.keep_ref, s32[8,64,128]{2,1,0:T(8,128)S(1)} %copy-done, ...), custom_call_target="tpu_custom_call" | custom-call | flops 1000000 | bytes 18000000 | tf_op jit(solution)/shard_map/early/pallas_call | solution.py:613
  22.6 0.0 all-to-all-done.got_ref
  22.6 0.0 collective-permute-done.theirs_e_ref
  22.6 0.0 collective-permute-done.1.theirs_o_ref
  22.6 0.0 copy-done.1
  22.6 3.3 %second.1 = (f32[32,16,128]{2,1,0:T(8,128)}, f32[8,1024]{1,0:T(8,128)S(1)}) custom-call(f32[32,8,128]{2,1,0:T(8,128)S(1)} %all-to-all-done.got_ref, f32[32,1024]{1,0:T(8,128)S(1)} %get-tuple-element.26.keep_ref, f32[152,128]{1,0:T(8,128)S(1)} %get-tuple-element.29.mine_e_ref, f32[152,128]{1,0:T(8,128)S(1)} %get-tuple-element.30.mine_o_ref, ...), custom_call_target="tpu_custom_call" | custom-call | flops 1000000 | bytes 9000000 | tf_op jit(solution)/shard_map/second/pallas_call | solution.py:622
  25.9 2.8 %all-to-all-start.1 = ((f32[32,16,128]{2,1,0:T(8,128)}), f32[32,16,128]{2,1,0:T(8,128)S(1)}, u32[]{:S(2)}, u32[]{:S(2)}) async-start(f32[32,16,128]{2,1,0:T(8,128)} %get-tuple-element.37), calls=%async_computation.1 | async-start | bytes 524288 | tf_op jit(solution)/shard_map/all_to_all | solution.py:627
  28.7 1.4 %edges.1 = (f32[48,128]{1,0:T(8,128)S(1)}, f32[48,128]{1,0:T(8,128)S(1)}, f32[24,128]{1,0:T(8,128)S(1)}, f32[24,128]{1,0:T(8,128)S(1)}) custom-call(f32[8,1024]{1,0:T(8,128)S(1)} %get-tuple-element.38.t_ref, s32[8,8,128]{2,1,0:T(8,128)S(1)} %get-tuple-element.45.pack_ref, f32[9,8,128]{2,1,0:T(8,128)S(1)} %get-tuple-element.40.weight_ref, ...), custom_call_target="tpu_custom_call" | custom-call | flops 1000000 | bytes 4000000 | tf_op jit(solution)/shard_map/edges/pallas_call | solution.py:631
  30.2 0.3 collective-permute-start.2
  30.5 4.4 %collective-permute-start.3 = (f32[48,128]{1,0:T(8,128)S(1)}, f32[48,128]{1,0:T(8,128)S(1)}, u32[]{:S(2)}, u32[]{:S(2)}) collective-permute-start(f32[48,128]{1,0:T(8,128)S(1)} %get-tuple-element.49), channel_id=1, source_target_pairs={{2,4},{6,8},{10,12},{14,16},{18,20},{22,24},{26,28},{30,0},{4,2},{... | collective-permute-start | bytes 73736 | tf_op jit(solution)/shard_map/ppermute | solution.py:542
  34.9 1.5 %collective-permute-start.4 = (f32[24,128]{1,0:T(8,128)S(1)}, f32[24,128]{1,0:T(8,128)S(1)}, u32[]{:S(2)}, u32[]{:S(2)}) collective-permute-start(f32[24,128]{1,0:T(8,128)S(1)} %get-tuple-element.46.mine_ye_ref), channel_id=1, source_target_pairs={{0,1},{1,0},{2,3},{3,2},{4,5},{5,4},{6,7},{7,6},{8,9},{9,8},{10,11... | collective-permute-start | bytes 36872 | tf_op jit(solution)/shard_map/ppermute | solution.py:542
  36.4 6.7 %fields.1 = (f32[3,8,8,128]{3,2,1,0:T(8,128)S(1)}, f32[8,8,8,128]{3,2,1,0:T(8,128)S(1)}, f32[8,8,8,128]{3,2,1,0:T(8,128)S(1)}) custom-call(f32[32,1024]{1,0:T(8,128)S(1)} %get-tuple-element.26.keep_ref, f32[8,1024]{1,0:T(8,128)S(1)} %get-tuple-element.38.t_ref, s32[8,64,128]{2,1,0:T(8,128)S(1)} %copy-done, f32[9,8,128]{2,1,0:T(8,128)S(1)} %get-tuple-element.40.weight_ref, ...), custom_call_target="tpu_custom_call" | custom-call | flops 1000000 | bytes 36000000 | tf_op jit(solution)/shard_map/fields/pallas_call | solution.py:639
  43.1 0.0 collective-permute-done.4.ye_ref
  43.1 0.0 collective-permute-done.2.xe_ref
  43.1 0.0 collective-permute-done.3.xo_ref
  43.1 0.0 all-to-all-done.1.got_ref
  43.1 1.5 %last.1 = (f32[8,1,1024]{2,1,0:T(1,128)}, f32[64,128]{1,0:T(8,128)}) custom-call(f32[32,16,128]{2,1,0:T(8,128)S(1)} %all-to-all-done.1.got_ref, f32[128,128]{1,0:T(8,128)S(1)} %copy-done.1, f32[32,1024]{1,0:T(8,128)S(1)} %get-tuple-element.26.keep_ref, f32[8,1024]{1,0:T(8,128)S(1)} %get-tuple-element.38.t_ref, ...), custom_call_target="tpu_custom_call" | custom-call | flops 1000000 | bytes 4000000 | tf_op jit(solution)/shard_map/last/pallas_call | solution.py:645
  (1 shorter events, 0.0 us)
Async XLA Ops:
  0.6 17.0 %copy-start = (s32[8,64,128]{2,1,0:T(8,128)S(1)}, s32[8,64,128]{2,1,0:T(8,128)}, u32[]{:S(2)}) copy-start(s32[8,64,128]{2,1,0:T(8,128)} %dofs_ref.3) | copy-start | bytes 786436
  0.6 22.0 %copy-start.1 = (f32[128,128]{1,0:T(8,128)S(1)}, f32[128,128]{1,0:T(8,128)}, u32[]{:S(2)}) copy-start(f32[128,128]{1,0:T(8,128)} %coarse_ref.3) | copy-start | bytes 196612
  3.0 19.6 %all-to-all-start = ((f32[32,8,128]{2,1,0:T(8,128)}), f32[32,8,128]{2,1,0:T(8,128)S(1)}, u32[]{:S(2)}, u32[]{:S(2)}) async-start(f32[32,8,128]{2,1,0:T(8,128)} %first.1), calls=%async_computation | async-start | bytes 262144 | tf_op jit(solution)/shard_map/all_to_all | solution.py:598
  12.9 9.7 %collective-permute-start = (f32[152,128]{1,0:T(8,128)S(1)}, f32[152,128]{1,0:T(8,128)S(1)}, u32[]{:S(2)}, u32[]{:S(2)}) collective-permute-start(f32[152,128]{1,0:T(8,128)S(1)} %get-tuple-element.29.mine_e_ref), channel_id=1, source_target_pairs={{0,2},{4,6},{8,10},{12,14},{16,18},{20,22},{24,26},{28,30},{2,0},{... | collective-permute-start | bytes 233480 | tf_op jit(solution)/shard_map/ppermute | solution.py:542
  13.2 9.4 %collective-permute-start.1 = (f32[152,128]{1,0:T(8,128)S(1)}, f32[152,128]{1,0:T(8,128)S(1)}, u32[]{:S(2)}, u32[]{:S(2)}) collective-permute-start(f32[152,128]{1,0:T(8,128)S(1)} %get-tuple-element.30.mine_o_ref), channel_id=1, source_target_pairs={{2,4},{6,8},{10,12},{14,16},{18,20},{22,24},{26,28},{30,0},{4,2},{... | collective-permute-start | bytes 233480 | tf_op jit(solution)/shard_map/ppermute | solution.py:542
  25.9 17.2 %all-to-all-start.1 = ((f32[32,16,128]{2,1,0:T(8,128)}), f32[32,16,128]{2,1,0:T(8,128)S(1)}, u32[]{:S(2)}, u32[]{:S(2)}) async-start(f32[32,16,128]{2,1,0:T(8,128)} %get-tuple-element.37), calls=%async_computation.1 | async-start | bytes 524288 | tf_op jit(solution)/shard_map/all_to_all | solution.py:627
  30.2 12.9 %collective-permute-start.2 = (f32[48,128]{1,0:T(8,128)S(1)}, f32[48,128]{1,0:T(8,128)S(1)}, u32[]{:S(2)}, u32[]{:S(2)}) collective-permute-start(f32[48,128]{1,0:T(8,128)S(1)} %get-tuple-element.48), channel_id=1, source_target_pairs={{0,2},{4,6},{8,10},{12,14},{16,18},{20,22},{24,26},{28,30},{2,0},{... | collective-permute-start | bytes 73736 | tf_op jit(solution)/shard_map/ppermute | solution.py:542
  30.5 12.6 %collective-permute-start.3 = (f32[48,128]{1,0:T(8,128)S(1)}, f32[48,128]{1,0:T(8,128)S(1)}, u32[]{:S(2)}, u32[]{:S(2)}) collective-permute-start(f32[48,128]{1,0:T(8,128)S(1)} %get-tuple-element.49), channel_id=1, source_target_pairs={{2,4},{6,8},{10,12},{14,16},{18,20},{22,24},{26,28},{30,0},{4,2},{... | collective-permute-start | bytes 73736 | tf_op jit(solution)/shard_map/ppermute | solution.py:542
  34.9 8.2 %collective-permute-start.4 = (f32[24,128]{1,0:T(8,128)S(1)}, f32[24,128]{1,0:T(8,128)S(1)}, u32[]{:S(2)}, u32[]{:S(2)}) collective-permute-start(f32[24,128]{1,0:T(8,128)S(1)} %get-tuple-element.46.mine_ye_ref), channel_id=1, source_target_pairs={{0,1},{1,0},{2,3},{3,2},{4,5},{5,4},{6,7},{7,6},{8,9},{9,8},{10,11... | collective-permute-start | bytes 36872 | tf_op jit(solution)/shard_map/ppermute | solution.py:542

commit v7 on v6

--- a/solution.py
+++ b/solution.py
@@ -528,18 +528,24 @@
     out_ref[...] = sweep(s, n_below, n_above, columns[:, 2:3], columns[:, 3:4])
 
 
-def swaps(size):
+def swaps(nx, ny, along_y):
+    def number(along, across):
+        return across * ny + along if along_y else along * ny + across
+
+    size, other = (ny, nx) if along_y else (nx, ny)
     out = []
     for first in (0, 1):
-        pairs = [(i, i + 1) for i in range(first, size - 1, 2)]
-        if first == 1 and size % 2 == 0 and size > 2:
-            pairs.append((size - 1, 0))
-        out.append(pairs + [(j, i) for i, j in pairs])
+        inner = [(i, i + 1) for i in range(first, size - 1, 2)]
+        pairs = [(number(i, k), number(j, k)) for i, j in inner for k in range(other)]
+        alone = [i for i in range(size) if not any(i in pair for pair in inner)]
+        if inner and other % 2 == 0:
+            pairs += [(number(i, k), number(i, k + 1)) for i in alone for k in range(0, other, 2)]
+        out.append(pairs + [(b, a) for a, b in pairs])
     return out
 
 
-def swap_over(array, axis, pairs):
-    return lax.ppermute(array, axis, pairs) if pairs else jnp.zeros_like(array)
+def swap_over(array, pairs):
+    return lax.ppermute(array, ("gx", "gy"), pairs) if pairs else jnp.zeros_like(array)
 
 
 def f32(*shape):
@@ -574,8 +580,8 @@
     modes = corner_map.shape[1]
     ex, ey = density.shape
     tiles = ex // 8
-    x_even, x_odd = swaps(nx)
-    y_even, y_odd = swaps(ny)
+    x_even, x_odd = swaps(nx, ny, False)
+    y_even, y_odd = swaps(nx, ny, True)
 
     def held(array):
         return pltpu.VMEM(array.shape, array.dtype)
@@ -605,8 +611,8 @@
          bf16(modes, unknowns)),
         [HBM] * 5, [held(a) for a in params] + [copies(5)], 8_000_000,
     )(*(in_hbm(a) for a in params))
-    theirs_o = swap_over(mine_o, "gx", x_odd)
-    theirs_e = swap_over(mine_e, "gx", x_even)
+    theirs_o = swap_over(mine_o, x_odd)
+    theirs_e = swap_over(mine_e, x_even)
 
     field = f32(EARLY + 1, CASES, 8, LANES)
     params = (elem_stiff, density, passive)
@@ -632,9 +638,9 @@
         edge_kernel, "edges", (row, row, col, col), [VMEM] * 5 + [HBM],
         [one_table, one_gathered, pltpu.VMEM((FIELDS, 8, LANES), F32), stiff, copies(1)], 4_000_000,
     )(t, pack, weight, kp, pp, in_hbm(elem_stiff))
-    ye, yo = swap_over(col_e, "gy", y_even), swap_over(col_o, "gy", y_odd)
-    xo = swap_over(row_o, "gx", x_odd)
-    xe = swap_over(row_e, "gx", x_even)
+    ye, yo = swap_over(col_e, y_even), swap_over(col_o, y_odd)
+    xo = swap_over(row_o, x_odd)
+    xe = swap_over(row_e, x_even)
 
     late, pt, tt = call(
         field_kernel, "fields",

time: 45.1 us -> 40.7 us (0.902)
  the two profiles are of different devices: /device:TPU:0 before, /device:TPU:1 now
where the time goes in v7:
time: 40.7 us; the launch traced here: 40.2 us
  Pallas kernels  22.8 us (56%)
  starting transfers between devices  16.7 us (41%)
  between operations  0.78 us (2%)
    all_to_all x2, starting transfers between devices, on_device(): got = lax.all_to_all(send, ('gx', 'gy'), 0, 0)  11.8 us
    pallas_call x1, Pallas kernels, on_device(): call(field_kernel, 'fields', (f32(tiles - EARLY, CASES, 8, LANES), f32(ti...  6.7 us
    pallas_call x1, Pallas kernels, on_device(): call(early_kernel, 'early', (s32(8, 8, LANES), f32(tiles + 1, 8, LANES),...  4.92 us
    ppermute x5, starting transfers between devices, swap_over(): lax.ppermute(array, ('gx', 'gy'), pairs)  4.88 us
    pallas_call x1, Pallas kernels, on_device(): call(second_kernel, 'second', (f32(everyone, 2 * CASES, modes), f32(CASES...  3.29 us
    pallas_call x1, Pallas kernels, on_device(): call(side_kernel, 'sides', (f32(KEEP_S + 8, unknowns), side, side, s32(2,...  2.6 us
    pallas_call x1, Pallas kernels, on_device(): call(first_kernel, 'first', f32(everyone, CASES, modes), [HBM] * 3, [held...  2.31 us
    pallas_call x1, Pallas kernels, on_device(): call(last_kernel, 'last', (f32(CASES, 1, unknowns), f32(ex, ey)), [VMEM]...  1.5 us
  transfers between devices with their start and end apart: 7, of which 0 were waited for; matrix products, arithmetic and copies ran while one was open for 0% of the time, Pallas kernels for 39%

profile of v7, /device:TPU:1, one launch (start us, length us, event | category | flops | bytes accessed | tf_op | source)
XLA Modules:
  0.0 40.2 jit_solution(1380327881201637128)
XLA Ops:
  0.6 0.0 copy-start
  0.6 0.0 copy-start.1
  0.6 2.3 %first.1 = f32[32,8,128]{2,1,0:T(8,128)} custom-call(f32[8,1,1024]{2,1,0:T(1,128)} %loads_hbm.3, f32[1,1024]{1,0:T(1,128)} %pre_hbm.5, f32[1,128,1024]{2,1,0:T(8,128)} %corner_hbm.3), custom_call_target="tpu_custom_call" | custom-call | flops 1000000 | bytes 4000000 | tf_op jit(solution)/shard_map/first/pallas_call | solution.py:601
  3.0 7.1 %all-to-all-start = ((f32[32,8,128]{2,1,0:T(8,128)}), f32[32,8,128]{2,1,0:T(8,128)S(1)}, u32[]{:S(2)}, u32[]{:S(2)}) async-start(f32[32,8,128]{2,1,0:T(8,128)} %first.1), calls=%async_computation | async-start | bytes 262144 | tf_op jit(solution)/shard_map/all_to_all | solution.py:604
  10.1 2.6 %sides.1 = (f32[32,1024]{1,0:T(8,128)S(1)}, f32[152,128]{1,0:T(8,128)S(1)}, f32[152,128]{1,0:T(8,128)S(1)}, s32[2,8,128]{2,1,0:T(8,128)S(1)}, s32[2,8,1024]{2,1,...) custom-call(f32[8,1,1024]{2,1,0:T(1,128)} %loads_hbm.3, bf16[1,1024,1024]{2,1,0:T(8,128)(2,1)} %op_hbm.3, ...), custom_call_target="tpu_custom_call" | custom-call | flops 1000000 | bytes 8000000 | tf_op jit(solution)/shard_map/sides/pallas_call | solution.py:608
  12.7 0.3 collective-permute-start
  13.0 1.5 %collective-permute-start.1 = (f32[152,128]{1,0:T(8,128)S(1)}, f32[152,128]{1,0:T(8,128)S(1)}, u32[]{:S(2)}, u32[]{:S(2)}) collective-permute-start(f32[152,128]{1,0:T(8,128)S(1)} %get-tuple-element.30.mine_o_ref), channel_id=1, source_target_pairs={{2,4},{3,5},{6,8},{7,9},{10,12},{11,13},{14,16},{15,17},{18,20},{1... | collective-permute-start | bytes 233480 | tf_op jit(solution)/shard_map/ppermute | solution.py:548
  14.5 0.0 copy-done
  14.5 4.9 %early.1 = (s32[8,8,128]{2,1,0:T(8,128)S(1)}, f32[9,8,128]{2,1,0:T(8,128)S(1)}, s32[8,128]{1,0:T(8,128)S(1)}, f32[10,8,128]{2,1,0:T(8,128)S(1)}, f32[6,8,8,8,128...) custom-call(f32[32,1024]{1,0:T(8,128)S(1)} %get-tuple-element.26.keep_ref, s32[8,64,128]{2,1,0:T(8,128)S(1)} %copy-done, ...), custom_call_target="tpu_custom_call" | custom-call | flops 1000000 | bytes 18000000 | tf_op jit(solution)/shard_map/early/pallas_call | solution.py:619
  19.5 0.0 all-to-all-done.got_ref
  19.5 0.0 collective-permute-done.theirs_e_ref
  19.5 0.0 collective-permute-done.1.theirs_o_ref
  19.5 0.0 copy-done.1
  19.5 3.3 %second.1 = (f32[32,16,128]{2,1,0:T(8,128)}, f32[8,1024]{1,0:T(8,128)S(1)}) custom-call(f32[32,8,128]{2,1,0:T(8,128)S(1)} %all-to-all-done.got_ref, f32[32,1024]{1,0:T(8,128)S(1)} %get-tuple-element.26.keep_ref, f32[152,128]{1,0:T(8,128)S(1)} %get-tuple-element.29.mine_e_ref, f32[152,128]{1,0:T(8,128)S(1)} %get-tuple-element.30.mine_o_ref, ...), custom_call_target="tpu_custom_call" | custom-call | flops 1000000 | bytes 9000000 | tf_op jit(solution)/shard_map/second/pallas_call | solution.py:628
  22.8 4.7 %all-to-all-start.1 = ((f32[32,16,128]{2,1,0:T(8,128)}), f32[32,16,128]{2,1,0:T(8,128)S(1)}, u32[]{:S(2)}, u32[]{:S(2)}) async-start(f32[32,16,128]{2,1,0:T(8,128)} %get-tuple-element.37), calls=%async_computation.1 | async-start | bytes 524288 | tf_op jit(solution)/shard_map/all_to_all | solution.py:633
  27.5 1.4 %edges.1 = (f32[48,128]{1,0:T(8,128)S(1)}, f32[48,128]{1,0:T(8,128)S(1)}, f32[24,128]{1,0:T(8,128)S(1)}, f32[24,128]{1,0:T(8,128)S(1)}) custom-call(f32[8,1024]{1,0:T(8,128)S(1)} %get-tuple-element.38.t_ref, s32[8,8,128]{2,1,0:T(8,128)S(1)} %get-tuple-element.45.pack_ref, f32[9,8,128]{2,1,0:T(8,128)S(1)} %get-tuple-element.40.weight_ref, ...), custom_call_target="tpu_custom_call" | custom-call | flops 1000000 | bytes 4000000 | tf_op jit(solution)/shard_map/edges/pallas_call | solution.py:637
  29.0 0.3 collective-permute-start.2
  29.3 1.5 %collective-permute-start.3 = (f32[48,128]{1,0:T(8,128)S(1)}, f32[48,128]{1,0:T(8,128)S(1)}, u32[]{:S(2)}, u32[]{:S(2)}) collective-permute-start(f32[48,128]{1,0:T(8,128)S(1)} %get-tuple-element.49), channel_id=1, source_target_pairs={{2,4},{3,5},{6,8},{7,9},{10,12},{11,13},{14,16},{15,17},{18,20},{1... | collective-permute-start | bytes 73736 | tf_op jit(solution)/shard_map/ppermute | solution.py:548
  30.8 1.2 %collective-permute-start.4 = (f32[24,128]{1,0:T(8,128)S(1)}, f32[24,128]{1,0:T(8,128)S(1)}, u32[]{:S(2)}, u32[]{:S(2)}) collective-permute-start(f32[24,128]{1,0:T(8,128)S(1)} %get-tuple-element.46.mine_ye_ref), channel_id=1, source_target_pairs={{0,1},{2,3},{4,5},{6,7},{8,9},{10,11},{12,13},{14,15},{16,17},{18,... | collective-permute-start | bytes 36872 | tf_op jit(solution)/shard_map/ppermute | solution.py:548
  32.0 6.7 %fields.1 = (f32[3,8,8,128]{3,2,1,0:T(8,128)S(1)}, f32[8,8,8,128]{3,2,1,0:T(8,128)S(1)}, f32[8,8,8,128]{3,2,1,0:T(8,128)S(1)}) custom-call(f32[32,1024]{1,0:T(8,128)S(1)} %get-tuple-element.26.keep_ref, f32[8,1024]{1,0:T(8,128)S(1)} %get-tuple-element.38.t_ref, s32[8,64,128]{2,1,0:T(8,128)S(1)} %copy-done, f32[9,8,128]{2,1,0:T(8,128)S(1)} %get-tuple-element.40.weight_ref, ...), custom_call_target="tpu_custom_call" | custom-call | flops 1000000 | bytes 36000000 | tf_op jit(solution)/shard_map/fields/pallas_call | solution.py:645
  38.7 0.0 collective-permute-done.4.ye_ref
  38.7 0.0 collective-permute-done.2.xe_ref
  38.7 0.0 collective-permute-done.3.xo_ref
  38.7 0.0 all-to-all-done.1.got_ref
  38.7 1.5 %last.1 = (f32[8,1,1024]{2,1,0:T(1,128)}, f32[64,128]{1,0:T(8,128)}) custom-call(f32[32,16,128]{2,1,0:T(8,128)S(1)} %all-to-all-done.1.got_ref, f32[128,128]{1,0:T(8,128)S(1)} %copy-done.1, f32[32,1024]{1,0:T(8,128)S(1)} %get-tuple-element.26.keep_ref, f32[8,1024]{1,0:T(8,128)S(1)} %get-tuple-element.38.t_ref, ...), custom_call_target="tpu_custom_call" | custom-call | flops 1000000 | bytes 4000000 | tf_op jit(solution)/shard_map/last/pallas_call | solution.py:651
  (1 shorter events, 0.0 us)
Async XLA Ops:
  0.6 13.9 %copy-start = (s32[8,64,128]{2,1,0:T(8,128)S(1)}, s32[8,64,128]{2,1,0:T(8,128)}, u32[]{:S(2)}) copy-start(s32[8,64,128]{2,1,0:T(8,128)} %dofs_ref.3) | copy-start | bytes 786436
  0.6 18.9 %copy-start.1 = (f32[128,128]{1,0:T(8,128)S(1)}, f32[128,128]{1,0:T(8,128)}, u32[]{:S(2)}) copy-start(f32[128,128]{1,0:T(8,128)} %coarse_ref.3) | copy-start | bytes 196612
  3.0 16.5 %all-to-all-start = ((f32[32,8,128]{2,1,0:T(8,128)}), f32[32,8,128]{2,1,0:T(8,128)S(1)}, u32[]{:S(2)}, u32[]{:S(2)}) async-start(f32[32,8,128]{2,1,0:T(8,128)} %first.1), calls=%async_computation | async-start | bytes 262144 | tf_op jit(solution)/shard_map/all_to_all | solution.py:604
  12.7 6.8 %collective-permute-start = (f32[152,128]{1,0:T(8,128)S(1)}, f32[152,128]{1,0:T(8,128)S(1)}, u32[]{:S(2)}, u32[]{:S(2)}) collective-permute-start(f32[152,128]{1,0:T(8,128)S(1)} %get-tuple-element.29.mine_e_ref), channel_id=1, source_target_pairs={{0,2},{1,3},{4,6},{5,7},{8,10},{9,11},{12,14},{13,15},{16,18},{17,... | collective-permute-start | bytes 233480 | tf_op jit(solution)/shard_map/ppermute | solution.py:548
  13.0 6.5 %collective-permute-start.1 = (f32[152,128]{1,0:T(8,128)S(1)}, f32[152,128]{1,0:T(8,128)S(1)}, u32[]{:S(2)}, u32[]{:S(2)}) collective-permute-start(f32[152,128]{1,0:T(8,128)S(1)} %get-tuple-element.30.mine_o_ref), channel_id=1, source_target_pairs={{2,4},{3,5},{6,8},{7,9},{10,12},{11,13},{14,16},{15,17},{18,20},{1... | collective-permute-start | bytes 233480 | tf_op jit(solution)/shard_map/ppermute | solution.py:548
  22.8 15.9 %all-to-all-start.1 = ((f32[32,16,128]{2,1,0:T(8,128)}), f32[32,16,128]{2,1,0:T(8,128)S(1)}, u32[]{:S(2)}, u32[]{:S(2)}) async-start(f32[32,16,128]{2,1,0:T(8,128)} %get-tuple-element.37), calls=%async_computation.1 | async-start | bytes 524288 | tf_op jit(solution)/shard_map/all_to_all | solution.py:633
  29.0 9.8 %collective-permute-start.2 = (f32[48,128]{1,0:T(8,128)S(1)}, f32[48,128]{1,0:T(8,128)S(1)}, u32[]{:S(2)}, u32[]{:S(2)}) collective-permute-start(f32[48,128]{1,0:T(8,128)S(1)} %get-tuple-element.48), channel_id=1, source_target_pairs={{0,2},{1,3},{4,6},{5,7},{8,10},{9,11},{12,14},{13,15},{16,18},{17,... | collective-permute-start | bytes 73736 | tf_op jit(solution)/shard_map/ppermute | solution.py:548
  29.3 9.4 %collective-permute-start.3 = (f32[48,128]{1,0:T(8,128)S(1)}, f32[48,128]{1,0:T(8,128)S(1)}, u32[]{:S(2)}, u32[]{:S(2)}) collective-permute-start(f32[48,128]{1,0:T(8,128)S(1)} %get-tuple-element.49), channel_id=1, source_target_pairs={{2,4},{3,5},{6,8},{7,9},{10,12},{11,13},{14,16},{15,17},{18,20},{1... | collective-permute-start | bytes 73736 | tf_op jit(solution)/shard_map/ppermute | solution.py:548
  30.8 7.9 %collective-permute-start.4 = (f32[24,128]{1,0:T(8,128)S(1)}, f32[24,128]{1,0:T(8,128)S(1)}, u32[]{:S(2)}, u32[]{:S(2)}) collective-permute-start(f32[24,128]{1,0:T(8,128)S(1)} %get-tuple-element.46.mine_ye_ref), channel_id=1, source_target_pairs={{0,1},{2,3},{4,5},{6,7},{8,9},{10,11},{12,13},{14,15},{16,17},{18,... | collective-permute-start | bytes 36872 | tf_op jit(solution)/shard_map/ppermute | solution.py:548

commit v8 on v7

--- a/solution.py
+++ b/solution.py
@@ -104,11 +104,36 @@
     return copies
 
 
-def first_kernel(loads_hbm, pre_hbm, corner_hbm, send_ref, loads_ref, pre_ref, corner_ref, sems):
+def edge_tiles(first, second):
+    ex, ey = first.shape
+    lane = lax.broadcasted_iota(jnp.int32, (1, LANES), 1)
+    turned = jnp.transpose(jnp.concatenate([first, second], axis=0))
+    swapped = pltpu.roll(turned, LANES - ex, 1)
+    out = []
+    for array, low, high in ((first, turned, swapped), (second, swapped, turned)):
+        cols = [jnp.where(lane < ex, low[j : j + 1], high[j + 1 : j + 2]) for j in (0, ey - 2)]
+        out.append(jnp.concatenate([array[0:2], array[ex - 2 :]] + cols + [array[0:2]], axis=0))
+    return out
+
+
+def corner_lanes(low, high):
+    lane = lax.broadcasted_iota(jnp.int32, low.shape, 1)
+    out = jnp.where(lane == 0, low, jnp.where(lane == 1, pltpu.roll(low, 2, 1), 0))
+    return jnp.where(lane == 2, pltpu.roll(high, 2, 1), jnp.where(lane == 3, pltpu.roll(high, 4, 1), out))
+
+
+def corner_values(vec, where):
+    return [pick(blocks_of(vec), pattern(jnp.broadcast_to(where[a : a + 1], (8, LANES)))) for a in range(8)]
+
+
+def first_kernel(loads_hbm, pre_hbm, corner_hbm, dofs_hbm, density_hbm, passive_hbm,
+                 send_hbm, pack_ref, weight_ref, spot_ref,
+                 send_ref, loads_ref, pre_ref, corner_ref, dofs_ref, density_ref, passive_ref, sems):
     piece = corner_ref.shape[2] // 4
     parts = [pl.ds(piece * i, piece) for i in range(4)]
     copies = fetch(sems, [(loads_hbm, loads_ref), (pre_hbm, pre_ref)]
-                   + [(corner_hbm.at[:, :, k], corner_ref.at[:, :, k]) for k in parts])
+                   + [(corner_hbm.at[:, :, k], corner_ref.at[:, :, k]) for k in parts]
+                   + [(dofs_hbm, dofs_ref), (density_hbm, density_ref), (passive_hbm, passive_ref)])
     copies[0].wait()
     copies[1].wait()
     p = pre_ref[...] * loads_ref[:, 0, :]
@@ -119,28 +144,23 @@
         part = term if part is None else part + term
     for d in range(send_ref.shape[0]):
         send_ref[d] = part
-
-
-def edge_tiles(first, second):
-    ex, ey = first.shape
-    lane = lax.broadcasted_iota(jnp.int32, (1, LANES), 1)
-    turned = jnp.transpose(jnp.concatenate([first, second], axis=0))
-    swapped = pltpu.roll(turned, LANES - ex, 1)
-    out = []
-    for array, low, high in ((first, turned, swapped), (second, swapped, turned)):
-        cols = [jnp.where(lane < ex, low[j : j + 1], high[j + 1 : j + 2]) for j in (0, ey - 2)]
-        out.append(jnp.concatenate([array[0:2], array[ex - 2 :]] + cols + [array[0:2]], axis=0))
-    return out
-
-
-def corner_lanes(low, high):
-    lane = lax.broadcasted_iota(jnp.int32, low.shape, 1)
-    out = jnp.where(lane == 0, low, jnp.where(lane == 1, pltpu.roll(low, 2, 1), 0))
-    return jnp.where(lane == 2, pltpu.roll(high, 2, 1), jnp.where(lane == 3, pltpu.roll(high, 4, 1), out))
-
-
-def corner_values(vec, where):
-    return [pick(blocks_of(vec), pattern(jnp.broadcast_to(where[a : a + 1], (8, LANES)))) for a in range(8)]
+    out = pltpu.make_async_copy(send_ref, send_hbm, sems.at[9])
+    out.start()
+    for copy in copies[6:]:
+        copy.wait()
+    for a in range(0, 8, 2):
+        first, second = edge_tiles(dofs_ref[a].astype(F32), dofs_ref[a + 1].astype(F32))
+        pack_ref[a] = first.astype(jnp.int32)
+        pack_ref[a + 1] = second.astype(jnp.int32)
+    rho = density_ref[...]
+    weight = jnp.where(passive_ref[...] == 1, 0.0, -penalty * rho * rho)
+    ex = weight.shape[0]
+    for i in range(ex // 8):
+        weight_ref[i] = weight[8 * i : 8 * i + 8]
+    weight_ref[ex // 8] = edge_tiles(weight, weight)[0]
+    spot_ref[0] = corner_lanes(dofs_ref[:, 0, :], dofs_ref[:, ex - 1, :]).astype(F32)
+    spot_ref[1] = jnp.broadcast_to(corner_lanes(weight[0:1], weight[ex - 1 :]), (8, LANES))
+    out.wait()
 
 
 def stiff_row(stiff_ref, a, u):
@@ -196,45 +216,19 @@
         out[SIDE_Y : SIDE_Y + 8] = scale * pick(blocks_of(y), where)
 
 
-def early_kernel(keep_ref, dofs_ref, stiff_hbm, density_hbm, passive_hbm,
-                 pack_ref, weight_ref, spot_ref, spot_kp_ref,
+def early_kernel(keep_ref, dofs_ref, pack_ref, weight_ref, spot_ref, stiff_hbm, spot_kp_ref,
                  kp_ref, pp_ref, table_ref, u_ref, other_ref, all_dofs_ref, all_weight_ref,
-                 stiff_ref, density_ref, passive_ref, sems):
-    copies = fetch(sems, ((stiff_hbm, stiff_ref), (density_hbm, density_ref), (passive_hbm, passive_ref)))
+                 stiff_ref, sems):
+    copies = fetch(sems, ((stiff_hbm, stiff_ref),))
     p = keep_ref[KEEP_P : KEEP_P + 8]
     make_tables(table_ref, p)
-    for a in range(0, 8, 2):
-        first, second = edge_tiles(dofs_ref[a].astype(F32), dofs_ref[a + 1].astype(F32))
-        pack_ref[a] = first.astype(jnp.int32)
-        pack_ref[a + 1] = second.astype(jnp.int32)
-    for copy in copies:
-        copy.wait()
-    rho = density_ref[...]
-    weight = jnp.where(passive_ref[...] == 1, 0.0, -penalty * rho * rho)
-    ex = weight.shape[0]
-    for i in range(ex // 8):
-        weight_ref[i] = weight[8 * i : 8 * i + 8]
-    weight_ref[ex // 8] = edge_tiles(weight, weight)[0]
-    spot = corner_lanes(dofs_ref[:, 0, :], dofs_ref[:, ex - 1, :])
-    spot_ref[...] = spot
-    spot_weight = jnp.broadcast_to(corner_lanes(weight[0:1], weight[ex - 1 :]), (8, LANES))
-    u = corner_values(p, spot)
-    pp = None
-    for a in range(8):
-        v = stiff_row(stiff_ref, a, u)
-        spot_kp_ref[a] = spot_weight * v
-        pp = u[a] * v if pp is None else pp + u[a] * v
-    lane = lax.broadcasted_iota(jnp.int32, (CASES, LANES), 1)
-    spot_kp_ref[8] = spot_weight
-    spot_kp_ref[9] = pltpu.roll(jnp.where(lane < 4, spot_weight * pp, 0.0), CORNER_PP, 1)
-
     for i in range(EARLY):
         for a in range(8):
             all_dofs_ref[i, a] = dofs_ref[a, 8 * i : 8 * i + 8]
-        all_weight_ref[i] = weight[8 * i : 8 * i + 8]
+        all_weight_ref[i] = weight_ref[i]
     for a in range(8):
         all_dofs_ref[EARLY, a] = pack_ref[a]
-    all_weight_ref[EARLY] = weight_ref[ex // 8]
+    all_weight_ref[EARLY] = weight_ref[weight_ref.shape[0] - 1]
 
     def gather(i, ref):
         gather_tile(lambda a: all_dofs_ref[i, a], table_ref, ref, 0)
@@ -250,7 +244,16 @@
                 pp = u[a] * v if pp is None else pp + u[a] * v
             pp_ref[i, c] = scale * pp
 
-    staggered(EARLY + 1, gather, fields, (u_ref, other_ref))
+    staggered(EARLY + 1, gather, fields, (u_ref, other_ref), copies)
+    spot_weight = spot_ref[1]
+    u = corner_values(p, spot_ref[0].astype(jnp.int32))
+    pp = None
+    for a in range(8):
+        v = stiff_row(stiff_ref, a, u)
+        spot_kp_ref[a] = spot_weight * v
+        pp = u[a] * v if pp is None else pp + u[a] * v
+    lane = lax.broadcasted_iota(jnp.int32, (CASES, LANES), 1)
+    spot_kp_ref[8] = pltpu.roll(jnp.where(lane < 4, spot_weight * pp, 0.0), CORNER_PP, 1)
 
 
 def spread(values, inverse):
@@ -263,8 +266,10 @@
 
 
 def second_kernel(got_ref, keep_ref, mine_e_ref, mine_o_ref, theirs_e_ref, theirs_o_ref, index_ref, inverse_ref,
-                  spot_ref, spot_kp_ref, coarse_ref, chigh_ref, clow_ref, pre_hbm, op_hbm, stiff_hbm,
-                  send_ref, t_ref, pre_ref, op_ref, stiff_ref, sems):
+                  spot_ref, spot_kp_ref, coarse_ref, chigh_ref, clow_ref, pack_ref, weight_ref, kp_ref, pp_ref,
+                  pre_hbm, op_hbm, stiff_hbm,
+                  send_hbm, t_ref, row_e_ref, row_o_ref, col_e_ref, col_o_ref,
+                  send_ref, table_ref, u_ref, field_ref, pre_ref, op_ref, stiff_ref, sems):
     copies = fetch(sems, ((pre_hbm, pre_ref), (stiff_hbm, stiff_ref), (op_hbm, op_ref)))
     total = got_ref[0]
     for d in range(1, got_ref.shape[0]):
@@ -292,16 +297,16 @@
         term = couplings[side] * lane_sum(t_mine * t_theirs)
         tlt = term if tlt is None else tlt + term
     copies[1].wait()
-    u = corner_values(t, spot_ref[...])
+    u = corner_values(t, spot_ref[0].astype(jnp.int32))
     pt = tt = None
     for a in range(8):
         one, two = u[a] * spot_kp_ref[a], u[a] * stiff_row(stiff_ref, a, u)
         pt, tt = (one, two) if pt is None else (pt + one, tt + two)
     lane = lax.broadcasted_iota(jnp.int32, (CASES, LANES), 1)
-    pt, tt = jnp.where(lane < 4, pt, 0.0), jnp.where(lane < 4, spot_kp_ref[8] * tt, 0.0)
+    pt, tt = jnp.where(lane < 4, pt, 0.0), jnp.where(lane < 4, spot_ref[1] * tt, 0.0)
     rest = keep_ref[KEEP_REST : KEEP_REST + 8]
     block = keep_ref[KEEP_S : KEEP_S + 8, :LANES]
-    block = block + spot_kp_ref[9] + pltpu.roll(pt, CORNER_PT, 1) + pltpu.roll(tt, CORNER_TT, 1)
+    block = block + spot_kp_ref[8] + pltpu.roll(pt, CORNER_PT, 1) + pltpu.roll(tt, CORNER_TT, 1)
     block = block + at_lanes((lane_sum(p * q), lane_sum(q * t), tlt, lane_sum(t * rest)), PQ)
     for d in range(send_ref.shape[0]):
         send_ref[d, :CASES] = g
@@ -310,6 +315,11 @@
     block = block + at_lanes((lane_sum(t * (high + low)),), TLT)
     for d in range(send_ref.shape[0]):
         send_ref[d, CASES:] = block
+    out = pltpu.make_async_copy(send_ref, send_hbm, sems.at[3])
+    out.start()
+    edge_fields(t, pack_ref, weight_ref, kp_ref, pp_ref, row_e_ref, row_o_ref, col_e_ref, col_o_ref,
+                table_ref, u_ref, field_ref, stiff_ref)
+    out.wait()
 
 
 def make_tables(table_ref, *vectors):
@@ -361,12 +371,10 @@
     return pt, tt
 
 
-def edge_kernel(t_ref, pack_ref, weight_ref, kp_ref, pp_ref, stiff_hbm,
-                row_e_ref, row_o_ref, col_e_ref, col_o_ref, table_ref, u_ref, field_ref, stiff_ref, sems):
-    copies = fetch(sems, ((stiff_hbm, stiff_ref),))
-    make_tables(table_ref, t_ref[...])
+def edge_fields(t, pack_ref, weight_ref, kp_ref, pp_ref, row_e_ref, row_o_ref, col_e_ref, col_o_ref,
+                table_ref, u_ref, field_ref, stiff_ref):
+    make_tables(table_ref, t)
     gather_tile(lambda a: pack_ref[a], table_ref, u_ref, 0)
-    copies[0].wait()
     scale = weight_ref[weight_ref.shape[0] - 1]
     for c in range(CASES):
         pt, tt = t_fields([u_ref[0, a, c] for a in range(8)], [kp_ref[EARLY, a, c] for a in range(8)], stiff_ref)
@@ -560,12 +568,13 @@
     return jax.ShapeDtypeStruct(shape, BF16)
 
 
-def call(kernel, name, out_shape, in_specs, scratch, moved):
+def call(kernel, name, out_shape, in_specs, scratch, moved, in_hbm_too=(), extra=0):
     single = not isinstance(out_shape, tuple)
     return pl.pallas_call(
         kernel, out_shape=out_shape, in_specs=in_specs,
-        out_specs=VMEM if single else (VMEM,) * len(out_shape), scratch_shapes=scratch, name=name,
-        compiler_params=pltpu.CompilerParams(vmem_limit_bytes=LIMIT),
+        out_specs=VMEM if single else tuple(HBM if i in in_hbm_too else VMEM for i in range(len(out_shape))),
+        scratch_shapes=scratch, name=name,
+        compiler_params=pltpu.CompilerParams(vmem_limit_bytes=LIMIT + extra),
         cost_estimate=pl.CostEstimate(flops=1_000_000, bytes_accessed=moved, transcendentals=0),
     )
 
@@ -598,9 +607,13 @@
     table = pltpu.VMEM((2, CASES, 8, 8, LANES), F32)
     gathered = pltpu.VMEM((2, 8, CASES, 8, LANES), F32)
 
-    send = call(first_kernel, "first", f32(everyone, CASES, modes), [HBM] * 3,
-                [held(loads), held(precond), held(corner_map), copies(6)], 4_000_000,
-                )(in_hbm(loads), in_hbm(precond), in_hbm(corner_map))
+    params = (loads, precond, corner_map, elem_dofs, density, passive)
+    send, pack, weight, spot = call(
+        first_kernel, "first",
+        (pltpu.HBM((everyone, CASES, modes), F32), s32(8, 8, LANES), f32(tiles + 1, 8, LANES), f32(2, 8, LANES)),
+        [HBM] * 6, [pltpu.VMEM((everyone, CASES, modes), F32)] + [held(a) for a in params] + [copies(10)], 5_000_000,
+        in_hbm_too=(0,), extra=4 * everyone * CASES * modes,
+    )(*(in_hbm(a) for a in params))
     got = lax.all_to_all(send, ("gx", "gy"), 0, 0)
 
     side = f32(SIDE_C + modes, R)
@@ -615,29 +628,27 @@
     theirs_e = swap_over(mine_e, x_even)
 
     field = f32(EARLY + 1, CASES, 8, LANES)
-    params = (elem_stiff, density, passive)
-    pack, weight, spot, spot_kp, kp, pp = call(
-        early_kernel, "early",
-        (s32(8, 8, LANES), f32(tiles + 1, 8, LANES), s32(8, LANES), f32(10, 8, LANES), f32(EARLY + 1, 8, CASES, 8, LANES), field),
-        [VMEM] * 2 + [HBM] * 3,
+    spot_kp, kp, pp = call(
+        early_kernel, "early", (f32(9, 8, LANES), f32(EARLY + 1, 8, CASES, 8, LANES), field),
+        [VMEM] * 5 + [HBM],
         [one_table, one_gathered, one_gathered, pltpu.VMEM((EARLY + 1, 8, 8, LANES), jnp.int32),
-         pltpu.VMEM((EARLY + 1, 8, LANES), F32)] + [stiff if a is elem_stiff else held(a) for a in params] + [copies(3)], 18_000_000,
-    )(keep, elem_dofs, *(in_hbm(a) for a in params))
-    got, spot = lax.optimization_barrier((got, spot))
-
-    send, t = call(
-        second_kernel, "second", (f32(everyone, 2 * CASES, modes), f32(CASES, unknowns)),
-        [VMEM] * 13 + [HBM] * 3, [held(precond), held(dual_op), stiff, copies(3)], 9_000_000,
-    )(got, keep, mine_e, mine_o, theirs_e, theirs_o, index, inverse, spot, spot_kp, coarse_inv, chigh, clow,
-      in_hbm(precond), in_hbm(dual_op), in_hbm(elem_stiff))
-    got = lax.all_to_all(send, ("gx", "gy"), 0, 0)
+         pltpu.VMEM((EARLY + 1, 8, LANES), F32), stiff, copies(1)], 18_000_000,
+    )(keep, elem_dofs, pack, weight, spot, in_hbm(elem_stiff))
+    got, spot_kp = lax.optimization_barrier((got, spot_kp))
 
     row = f32(2 * FIELDS, LANES)
     col = f32(FIELDS, LANES)
-    row_e, row_o, col_e, col_o = call(
-        edge_kernel, "edges", (row, row, col, col), [VMEM] * 5 + [HBM],
-        [one_table, one_gathered, pltpu.VMEM((FIELDS, 8, LANES), F32), stiff, copies(1)], 4_000_000,
-    )(t, pack, weight, kp, pp, in_hbm(elem_stiff))
+    send, t, row_e, row_o, col_e, col_o = call(
+        second_kernel, "second",
+        (pltpu.HBM((everyone, 2 * CASES, modes), F32), f32(CASES, unknowns), row, row, col, col),
+        [VMEM] * 17 + [HBM] * 3,
+        [pltpu.VMEM((everyone, 2 * CASES, modes), F32), one_table, one_gathered, pltpu.VMEM((FIELDS, 8, LANES), F32),
+         held(precond), held(dual_op), stiff, copies(4)], 10_000_000, in_hbm_too=(0,),
+        extra=8 * everyone * CASES * modes,
+    )(got, keep, mine_e, mine_o, theirs_e, theirs_o, index, inverse, spot, spot_kp, coarse_inv, chigh, clow,
+      pack, weight, kp, pp, in_hbm(precond), in_hbm(dual_op), in_hbm(elem_stiff))
+    got = lax.all_to_all(send, ("gx", "gy"), 0, 0)
+
     ye, yo = swap_over(col_e, y_even), swap_over(col_o, y_odd)
     xo = swap_over(row_o, x_odd)
     xe = swap_over(row_e, x_even)

time: 40.7 us -> 39.6 us (0.973)
  Pallas kernels: 22.8 us -> 20.6 us
  waiting for transfers between devices: 0.02 us -> 0.77 us
    pallas_call x4 -> x3, Pallas kernels: 11.9 us -> 9.79 us  [the longest x1 4.13 us: on_device(): call(early_kernel, 'early', (f32(9, 8, LANES), f32(EARLY + 1, 8, CASES, 8...]
    all_to_all x2, waiting for transfers between devices: 0.01 us -> 0.75 us  [on_device(): got = lax.all_to_all(send, ('gx', 'gy'), 0, 0)]
  transfers between devices with their start and end apart: 7 -> 7, of which waited for: 0 -> 1; matrix products, arithmetic and copies ran while one was open for 0% -> 0% of each run, Pallas kernels for 39% -> 35%
where the time goes in v8:
time: 39.6 us; the launch traced here: 38.8 us
  Pallas kernels  20.6 us (52%)
  starting transfers between devices  16.7 us (42%)
  waiting for transfers between devices  0.77 us (2%)
  between operations  0.76 us (2%)
    all_to_all x2, starting transfers between devices, on_device(): got = lax.all_to_all(send, ('gx', 'gy'), 0, 0)  11.8 us
    pallas_call x1, Pallas kernels, on_device(): call(field_kernel, 'fields', (f32(tiles - EARLY, CASES, 8, LANES), f32(ti...  6.73 us
    ppermute x5, starting transfers between devices, swap_over(): lax.ppermute(array, ('gx', 'gy'), pairs)  4.88 us
    pallas_call x1, Pallas kernels, on_device(): call(early_kernel, 'early', (f32(9, 8, LANES), f32(EARLY + 1, 8, CASES, 8...  4.13 us
    pallas_call x1, Pallas kernels, on_device(): call(second_kernel, 'second', (pltpu.HBM((everyone, 2 * CASES, modes), F3...  3.3 us
    pallas_call x1, Pallas kernels, on_device(): call(side_kernel, 'sides', (f32(KEEP_S + 8, unknowns), side, side, s32(2,...  2.6 us
    pallas_call x1, Pallas kernels, on_device(): call(first_kernel, 'first', (pltpu.HBM((everyone, CASES, modes), F32), s3...  2.35 us
    pallas_call x1, Pallas kernels, on_device(): call(last_kernel, 'last', (f32(CASES, 1, unknowns), f32(ex, ey)), [VMEM]...  1.49 us
  transfers between devices with their start and end apart: 7, of which 1 were waited for; matrix products, arithmetic and copies ran while one was open for 0% of the time, Pallas kernels for 35%

profile of v8, /device:TPU:1, one launch (start us, length us, event | category | flops | bytes accessed | tf_op | source)
XLA Modules:
  0.0 38.8 jit_solution(1678327389025427540)
XLA Ops:
  0.6 0.0 copy-start
  0.6 0.0 copy-start.1
  0.7 2.4 %first.1 = (f32[32,8,128]{2,1,0:T(8,128)}, s32[8,8,128]{2,1,0:T(8,128)S(1)}, f32[9,8,128]{2,1,0:T(8,128)S(1)}, f32[2,8,128]{2,1,0:T(8,128)S(1)}) custom-call(f32[8,1,1024]{2,1,0:T(1,128)} %loads_hbm.3, f32[1,1024]{1,0:T(1,128)} %pre_hbm.5, f32[1,128,1024]{2,1,0:T(8,128)} %corner_hbm.3, s32[8,64,128]{2,1,0:T(8,128)} %dofs_ref.3, f32[64,128]{1,0:T(8,128)} %density_hbm.1, ...), custom_call_target="tpu_custom_call" | custom-call | flops 1000000 | bytes 5000000 | tf_op jit(solution)/shard_map/first/pallas_call | solution.py:611
  3.0 7.1 %all-to-all-start = ((f32[32,8,128]{2,1,0:T(8,128)}), f32[32,8,128]{2,1,0:T(8,128)S(1)}, u32[]{:S(2)}, u32[]{:S(2)}) async-start(f32[32,8,128]{2,1,0:T(8,128)} %get-tuple-element.27), calls=%async_computation | async-start | bytes 262144 | tf_op jit(solution)/shard_map/all_to_all | solution.py:617
  10.1 2.6 %sides.1 = (f32[32,1024]{1,0:T(8,128)S(1)}, f32[152,128]{1,0:T(8,128)S(1)}, f32[152,128]{1,0:T(8,128)S(1)}, s32[2,8,128]{2,1,0:T(8,128)S(1)}, s32[2,8,1024]{2,1,...) custom-call(f32[8,1,1024]{2,1,0:T(1,128)} %loads_hbm.3, bf16[1,1024,1024]{2,1,0:T(8,128)(2,1)} %op_hbm.3, ...), custom_call_target="tpu_custom_call" | custom-call | flops 1000000 | bytes 8000000 | tf_op jit(solution)/shard_map/sides/pallas_call | solution.py:621
  12.7 0.3 collective-permute-start
  13.1 1.5 %collective-permute-start.1 = (f32[152,128]{1,0:T(8,128)S(1)}, f32[152,128]{1,0:T(8,128)S(1)}, u32[]{:S(2)}, u32[]{:S(2)}) collective-permute-start(f32[152,128]{1,0:T(8,128)S(1)} %get-tuple-element.35.mine_o_ref), channel_id=1, source_target_pairs={{2,4},{3,5},{6,8},{7,9},{10,12},{11,13},{14,16},{15,17},{18,20},{1... | collective-permute-start | bytes 233480 | tf_op jit(solution)/shard_map/ppermute | solution.py:556
  14.6 0.0 copy-done
  14.6 4.1 %early.1 = (f32[9,8,128]{2,1,0:T(8,128)S(1)}, f32[6,8,8,8,128]{4,3,2,1,0:T(8,128)S(1)}, f32[6,8,8,128]{3,2,1,0:T(8,128)S(1)}) custom-call(f32[32,1024]{1,0:T(8,128)S(1)} %get-tuple-element.28.keep_ref, s32[8,64,128]{2,1,0:T(8,128)S(1)} %copy-done, s32[8,8,128]{2,1,0:T(8,128)S(1)} %get-tuple-element.29.pack_ref, ...), custom_call_target="tpu_custom_call" | custom-call | flops 1000000 | bytes 18000000 | tf_op jit(solution)/shard_map/early/pallas_call | solution.py:631
  18.7 0.0 all-to-all-done.got_ref
  18.7 0.0 collective-permute-done.theirs_e_ref
  18.7 0.0 collective-permute-done.1.theirs_o_ref
  18.8 0.0 copy-done.1
  18.8 3.3 %second.1 = (f32[32,16,128]{2,1,0:T(8,128)}, f32[8,1024]{1,0:T(8,128)S(1)}, f32[48,128]{1,0:T(8,128)S(1)}, f32[48,128]{1,0:T(8,128)S(1)}, f32[24,128]{1,0:T(8,128)S(1)}, /*index=5*/f32[24,128]{1,0:T(8,128)S(1)}) custom-call(f32[32,8,128]{2,1,0:T(8,128)S(1)} %all-to-all-done.got_ref, f32[32,1024]{1,0:T(8,128)S(1)} %get-tuple-element.28.keep_ref, ...), custom_call_target="tpu_custom_call" | custom-call | flops 1000000 | bytes 10000000 | tf_op jit(solution)/shard_map/second/pallas_call | solution.py:641
  22.1 4.7 %all-to-all-start.1 = ((f32[32,16,128]{2,1,0:T(8,128)}), f32[32,16,128]{2,1,0:T(8,128)S(1)}, u32[]{:S(2)}, u32[]{:S(2)}) async-start(f32[32,16,128]{2,1,0:T(8,128)} %get-tuple-element.43), calls=%async_computation.1 | async-start | bytes 524288 | tf_op jit(solution)/shard_map/all_to_all | solution.py:650
  26.8 0.3 collective-permute-start.2
  27.1 1.5 %collective-permute-start.3 = (f32[48,128]{1,0:T(8,128)S(1)}, f32[48,128]{1,0:T(8,128)S(1)}, u32[]{:S(2)}, u32[]{:S(2)}) collective-permute-start(f32[48,128]{1,0:T(8,128)S(1)} %get-tuple-element.51), channel_id=1, source_target_pairs={{2,4},{3,5},{6,8},{7,9},{10,12},{11,13},{14,16},{15,17},{18,20},{1... | collective-permute-start | bytes 73736 | tf_op jit(solution)/shard_map/ppermute | solution.py:556
  28.6 1.2 %collective-permute-start.4 = (f32[24,128]{1,0:T(8,128)S(1)}, f32[24,128]{1,0:T(8,128)S(1)}, u32[]{:S(2)}, u32[]{:S(2)}) collective-permute-start(f32[24,128]{1,0:T(8,128)S(1)} %get-tuple-element.48.mine_ye_ref), channel_id=1, source_target_pairs={{0,1},{2,3},{4,5},{6,7},{8,9},{10,11},{12,13},{14,15},{16,17},{18,... | collective-permute-start | bytes 36872 | tf_op jit(solution)/shard_map/ppermute | solution.py:556
  29.8 6.7 %fields.1 = (f32[3,8,8,128]{3,2,1,0:T(8,128)S(1)}, f32[8,8,8,128]{3,2,1,0:T(8,128)S(1)}, f32[8,8,8,128]{3,2,1,0:T(8,128)S(1)}) custom-call(f32[32,1024]{1,0:T(8,128)S(1)} %get-tuple-element.28.keep_ref, f32[8,1024]{1,0:T(8,128)S(1)} %get-tuple-element.44.t_ref, s32[8,64,128]{2,1,0:T(8,128)S(1)} %copy-done, f32[9,8,128]{2,1,0:T(8,128)S(1)} %get-tuple-element.30.weight_ref, ...), custom_call_target="tpu_custom_call" | custom-call | flops 1000000 | bytes 36000000 | tf_op jit(solution)/shard_map/fields/pallas_call | solution.py:656
  36.6 0.0 collective-permute-done.4.ye_ref
  36.6 0.0 collective-permute-done.2.xe_ref
  36.6 0.0 collective-permute-done.3.xo_ref
  36.6 0.8 %all-to-all-done.1.got_ref = f32[32,16,128]{2,1,0:T(8,128)S(1)} async-done(((f32[32,16,128]{2,1,0:T(8,128)}), f32[32,16,128]{2,1,0:T(8,128)S(1)}, u32[]{:S(2)}, u32[]{:S(2)}) %all-to-all-start.1) | async-done | bytes 262176 | tf_op jit(solution)/shard_map/all_to_all | solution.py:650
  37.3 1.5 %last.1 = (f32[8,1,1024]{2,1,0:T(1,128)}, f32[64,128]{1,0:T(8,128)}) custom-call(f32[32,16,128]{2,1,0:T(8,128)S(1)} %all-to-all-done.1.got_ref, f32[128,128]{1,0:T(8,128)S(1)} %copy-done.1, f32[32,1024]{1,0:T(8,128)S(1)} %get-tuple-element.28.keep_ref, f32[8,1024]{1,0:T(8,128)S(1)} %get-tuple-element.44.t_ref, ...), custom_call_target="tpu_custom_call" | custom-call | flops 1000000 | bytes 4000000 | tf_op jit(solution)/shard_map/last/pallas_call | solution.py:662
  (1 shorter events, 0.0 us)
Async XLA Ops:
  0.6 13.9 %copy-start = (s32[8,64,128]{2,1,0:T(8,128)S(1)}, s32[8,64,128]{2,1,0:T(8,128)}, u32[]{:S(2)}) copy-start(s32[8,64,128]{2,1,0:T(8,128)} %dofs_ref.3) | copy-start | bytes 786436
  0.6 18.1 %copy-start.1 = (f32[128,128]{1,0:T(8,128)S(1)}, f32[128,128]{1,0:T(8,128)}, u32[]{:S(2)}) copy-start(f32[128,128]{1,0:T(8,128)} %coarse_ref.3) | copy-start | bytes 196612
  3.0 15.7 %all-to-all-start = ((f32[32,8,128]{2,1,0:T(8,128)}), f32[32,8,128]{2,1,0:T(8,128)S(1)}, u32[]{:S(2)}, u32[]{:S(2)}) async-start(f32[32,8,128]{2,1,0:T(8,128)} %get-tuple-element.27), calls=%async_computation | async-start | bytes 262144 | tf_op jit(solution)/shard_map/all_to_all | solution.py:617
  12.7 6.0 %collective-permute-start = (f32[152,128]{1,0:T(8,128)S(1)}, f32[152,128]{1,0:T(8,128)S(1)}, u32[]{:S(2)}, u32[]{:S(2)}) collective-permute-start(f32[152,128]{1,0:T(8,128)S(1)} %get-tuple-element.34.mine_e_ref), channel_id=1, source_target_pairs={{0,2},{1,3},{4,6},{5,7},{8,10},{9,11},{12,14},{13,15},{16,18},{17,... | collective-permute-start | bytes 233480 | tf_op jit(solution)/shard_map/ppermute | solution.py:556
  13.1 5.7 %collective-permute-start.1 = (f32[152,128]{1,0:T(8,128)S(1)}, f32[152,128]{1,0:T(8,128)S(1)}, u32[]{:S(2)}, u32[]{:S(2)}) collective-permute-start(f32[152,128]{1,0:T(8,128)S(1)} %get-tuple-element.35.mine_o_ref), channel_id=1, source_target_pairs={{2,4},{3,5},{6,8},{7,9},{10,12},{11,13},{14,16},{15,17},{18,20},{1... | collective-permute-start | bytes 233480 | tf_op jit(solution)/shard_map/ppermute | solution.py:556
  22.1 15.3 %all-to-all-start.1 = ((f32[32,16,128]{2,1,0:T(8,128)}), f32[32,16,128]{2,1,0:T(8,128)S(1)}, u32[]{:S(2)}, u32[]{:S(2)}) async-start(f32[32,16,128]{2,1,0:T(8,128)} %get-tuple-element.43), calls=%async_computation.1 | async-start | bytes 524288 | tf_op jit(solution)/shard_map/all_to_all | solution.py:650
  26.8 9.8 %collective-permute-start.2 = (f32[48,128]{1,0:T(8,128)S(1)}, f32[48,128]{1,0:T(8,128)S(1)}, u32[]{:S(2)}, u32[]{:S(2)}) collective-permute-start(f32[48,128]{1,0:T(8,128)S(1)} %get-tuple-element.50), channel_id=1, source_target_pairs={{0,2},{1,3},{4,6},{5,7},{8,10},{9,11},{12,14},{13,15},{16,18},{17,... | collective-permute-start | bytes 73736 | tf_op jit(solution)/shard_map/ppermute | solution.py:556
  27.1 9.5 %collective-permute-start.3 = (f32[48,128]{1,0:T(8,128)S(1)}, f32[48,128]{1,0:T(8,128)S(1)}, u32[]{:S(2)}, u32[]{:S(2)}) collective-permute-start(f32[48,128]{1,0:T(8,128)S(1)} %get-tuple-element.51), channel_id=1, source_target_pairs={{2,4},{3,5},{6,8},{7,9},{10,12},{11,13},{14,16},{15,17},{18,20},{1... | collective-permute-start | bytes 73736 | tf_op jit(solution)/shard_map/ppermute | solution.py:556
  28.6 7.9 %collective-permute-start.4 = (f32[24,128]{1,0:T(8,128)S(1)}, f32[24,128]{1,0:T(8,128)S(1)}, u32[]{:S(2)}, u32[]{:S(2)}) collective-permute-start(f32[24,128]{1,0:T(8,128)S(1)} %get-tuple-element.48.mine_ye_ref), channel_id=1, source_target_pairs={{0,1},{2,3},{4,5},{6,7},{8,9},{10,11},{12,13},{14,15},{16,17},{18,... | collective-permute-start | bytes 36872 | tf_op jit(solution)/shard_map/ppermute | solution.py:556

commit v9 on v8

--- a/solution.py
+++ b/solution.py
@@ -102,6 +102,24 @@
     for copy in copies:
         copy.start()
     return copies
+
+
+def to_row(g, block):
+    tails = []
+    for r in range(2):
+        tail = block[4 * r : 4 * r + 1]
+        for c in range(1, 4):
+            tail = tail + pltpu.roll(block[4 * r + c : 4 * r + c + 1], 32 * c, 1)
+        tails.append(tail)
+    return jnp.concatenate([g[c : c + 1] for c in range(CASES)] + tails, axis=1)
+
+
+def block_of(tails):
+    rows = []
+    for c in range(CASES):
+        tail = tails[:, LANES * (c // 4) : LANES * (c // 4 + 1)]
+        rows.append(pltpu.roll(tail, (LANES - 32 * (c % 4)) % LANES, 1))
+    return jnp.concatenate(rows, axis=0)
 
 
 def edge_tiles(first, second):
@@ -308,13 +326,12 @@
     block = keep_ref[KEEP_S : KEEP_S + 8, :LANES]
     block = block + spot_kp_ref[8] + pltpu.roll(pt, CORNER_PT, 1) + pltpu.roll(tt, CORNER_TT, 1)
     block = block + at_lanes((lane_sum(p * q), lane_sum(q * t), tlt, lane_sum(t * rest)), PQ)
-    for d in range(send_ref.shape[0]):
-        send_ref[d, :CASES] = g
     copies[2].wait()
     high, low = op_dot(t, op_ref)
     block = block + at_lanes((lane_sum(t * (high + low)),), TLT)
+    row = to_row(g, block)
     for d in range(send_ref.shape[0]):
-        send_ref[d, CASES:] = block
+        send_ref[d] = row
     out = pltpu.make_async_copy(send_ref, send_hbm, sems.at[3])
     out.start()
     edge_fields(t, pack_ref, weight_ref, kp_ref, pp_ref, row_e_ref, row_o_ref, col_e_ref, col_o_ref,
@@ -434,10 +451,9 @@
 def last_kernel(got_ref, coarse_ref, keep_ref, t_ref, early_ref, late_ref, pt_ref, tt_ref,
                 mine_ye_ref, mine_yo_ref, xe_ref, xo_ref, ye_ref, yo_ref,
                 adj_ref, out_ref):
-    total = got_ref[0]
-    for d in range(1, got_ref.shape[0]):
-        total = total + got_ref[d]
-    g, s = total[:CASES], total[CASES:]
+    total = jnp.sum(got_ref[:, 0, :], axis=0, keepdims=True)
+    g = jnp.concatenate([total[:, LANES * c : LANES * (c + 1)] for c in range(CASES)], axis=0)
+    s = block_of(total[:, LANES * CASES :])
     rz, pq, qmq, tlt, pe, te = (s[:, j : j + 1] for j in (RZ, PQ, QMQ, TLT, PE, TE))
     tat = tlt + lane_sum(g * rows_dot(g, coarse_ref[...]))
     alpha = rz / pq
@@ -491,7 +507,7 @@
 
     def corner_of(dx, dy, there, k):
         whose = jnp.clip(x + dx, 0, nx - 1) * ny + jnp.clip(y + dy, 0, ny - 1)
-        row = jnp.sum(of_lane * got_ref[whose, CASES:, :], axis=0, keepdims=True)
+        row = jnp.sum(of_lane * block_of(got_ref[whose, :, LANES * CASES :]), axis=0, keepdims=True)
         parts = [row[:, at + k : at + k + 1] for at in (CORNER_PP, CORNER_PT, CORNER_TT)]
         return there * (parts[0] + parts[1] + parts[2]) / diag
 
@@ -640,9 +656,9 @@
     col = f32(FIELDS, LANES)
     send, t, row_e, row_o, col_e, col_o = call(
         second_kernel, "second",
-        (pltpu.HBM((everyone, 2 * CASES, modes), F32), f32(CASES, unknowns), row, row, col, col),
+        (pltpu.HBM((everyone, 1, (CASES + 2) * modes), F32), f32(CASES, unknowns), row, row, col, col),
         [VMEM] * 17 + [HBM] * 3,
-        [pltpu.VMEM((everyone, 2 * CASES, modes), F32), one_table, one_gathered, pltpu.VMEM((FIELDS, 8, LANES), F32),
+        [pltpu.VMEM((everyone, 1, (CASES + 2) * modes), F32), one_table, one_gathered, pltpu.VMEM((FIELDS, 8, LANES), F32),
          held(precond), held(dual_op), stiff, copies(4)], 10_000_000, in_hbm_too=(0,),
         extra=8 * everyone * CASES * modes,
     )(got, keep, mine_e, mine_o, theirs_e, theirs_o, index, inverse, spot, spot_kp, coarse_inv, chigh, clow,

time: 39.6 us -> 38.5 us (0.972); the launches traced: 38.8 us -> 38.2 us
  waiting for transfers between devices: 0.77 us -> 0.02 us
    all_to_all x2, waiting for transfers between devices: 0.75 us -> 0.01 us  [on_device(): got = lax.all_to_all(send, ('gx', 'gy'), 0, 0)]
  transfers between devices with their start and end apart: 7 -> 7, of which waited for: 1 -> 0; matrix products, arithmetic and copies ran while one was open for 0% -> 0% of each run, Pallas kernels for 35% -> 35%
where the time goes in v9:
time: 38.5 us; the launch traced here: 38.2 us
  Pallas kernels  20.7 us (54%)
  starting transfers between devices  16.7 us (43%)
  between operations  0.78 us (2%)
    all_to_all x2, starting transfers between devices, on_device(): got = lax.all_to_all(send, ('gx', 'gy'), 0, 0)  11.8 us
    pallas_call x1, Pallas kernels, on_device(): call(field_kernel, 'fields', (f32(tiles - EARLY, CASES, 8, LANES), f32(ti...  6.73 us
    ppermute x5, starting transfers between devices, swap_over(): lax.ppermute(array, ('gx', 'gy'), pairs)  4.88 us
    pallas_call x1, Pallas kernels, on_device(): call(early_kernel, 'early', (f32(9, 8, LANES), f32(EARLY + 1, 8, CASES, 8...  4.13 us
    pallas_call x1, Pallas kernels, on_device(): call(second_kernel, 'second', (pltpu.HBM((everyone, 1, (CASES + 2) * mode...  3.35 us
    pallas_call x1, Pallas kernels, on_device(): call(side_kernel, 'sides', (f32(KEEP_S + 8, unknowns), side, side, s32(2,...  2.6 us
    pallas_call x1, Pallas kernels, on_device(): call(first_kernel, 'first', (pltpu.HBM((everyone, CASES, modes), F32), s3...  2.35 us
    pallas_call x1, Pallas kernels, on_device(): call(last_kernel, 'last', (f32(CASES, 1, unknowns), f32(ex, ey)), [VMEM]...  1.52 us
  transfers between devices with their start and end apart: 7, of which 0 were waited for; matrix products, arithmetic and copies ran while one was open for 0% of the time, Pallas kernels for 35%

profile of v9, /device:TPU:1, one launch (start us, length us, event | category | flops | bytes accessed | tf_op | source)
XLA Modules:
  0.0 38.2 jit_solution(10328733731474502744)
XLA Ops:
  0.6 0.0 copy-start
  0.6 0.0 copy-start.1
  0.7 2.4 %first.1 = (f32[32,8,128]{2,1,0:T(8,128)}, s32[8,8,128]{2,1,0:T(8,128)S(1)}, f32[9,8,128]{2,1,0:T(8,128)S(1)}, f32[2,8,128]{2,1,0:T(8,128)S(1)}) custom-call(f32[8,1,1024]{2,1,0:T(1,128)} %loads_hbm.3, f32[1,1024]{1,0:T(1,128)} %pre_hbm.5, f32[1,128,1024]{2,1,0:T(8,128)} %corner_hbm.3, s32[8,64,128]{2,1,0:T(8,128)} %dofs_ref.3, f32[64,128]{1,0:T(8,128)} %density_hbm.1, ...), custom_call_target="tpu_custom_call" | custom-call | flops 1000000 | bytes 5000000 | tf_op jit(solution)/shard_map/first/pallas_call | solution.py:627
  3.0 7.1 %all-to-all-start = ((f32[32,8,128]{2,1,0:T(8,128)}), f32[32,8,128]{2,1,0:T(8,128)S(1)}, u32[]{:S(2)}, u32[]{:S(2)}) async-start(f32[32,8,128]{2,1,0:T(8,128)} %get-tuple-element.27), calls=%async_computation | async-start | bytes 262144 | tf_op jit(solution)/shard_map/all_to_all | solution.py:633
  10.1 2.6 %sides.1 = (f32[32,1024]{1,0:T(8,128)S(1)}, f32[152,128]{1,0:T(8,128)S(1)}, f32[152,128]{1,0:T(8,128)S(1)}, s32[2,8,128]{2,1,0:T(8,128)S(1)}, s32[2,8,1024]{2,1,...) custom-call(f32[8,1,1024]{2,1,0:T(1,128)} %loads_hbm.3, bf16[1,1024,1024]{2,1,0:T(8,128)(2,1)} %op_hbm.3, ...), custom_call_target="tpu_custom_call" | custom-call | flops 1000000 | bytes 8000000 | tf_op jit(solution)/shard_map/sides/pallas_call | solution.py:637
  12.7 0.3 collective-permute-start
  13.1 1.5 %collective-permute-start.1 = (f32[152,128]{1,0:T(8,128)S(1)}, f32[152,128]{1,0:T(8,128)S(1)}, u32[]{:S(2)}, u32[]{:S(2)}) collective-permute-start(f32[152,128]{1,0:T(8,128)S(1)} %get-tuple-element.35.mine_o_ref), channel_id=1, source_target_pairs={{2,4},{3,5},{6,8},{7,9},{10,12},{11,13},{14,16},{15,17},{18,20},{1... | collective-permute-start | bytes 233480 | tf_op jit(solution)/shard_map/ppermute | solution.py:572
  14.6 0.0 copy-done
  14.6 4.1 %early.1 = (f32[9,8,128]{2,1,0:T(8,128)S(1)}, f32[6,8,8,8,128]{4,3,2,1,0:T(8,128)S(1)}, f32[6,8,8,128]{3,2,1,0:T(8,128)S(1)}) custom-call(f32[32,1024]{1,0:T(8,128)S(1)} %get-tuple-element.28.keep_ref, s32[8,64,128]{2,1,0:T(8,128)S(1)} %copy-done, s32[8,8,128]{2,1,0:T(8,128)S(1)} %get-tuple-element.29.pack_ref, ...), custom_call_target="tpu_custom_call" | custom-call | flops 1000000 | bytes 18000000 | tf_op jit(solution)/shard_map/early/pallas_call | solution.py:647
  18.7 0.0 all-to-all-done.got_ref
  18.7 0.0 collective-permute-done.theirs_e_ref
  18.7 0.0 collective-permute-done.1.theirs_o_ref
  18.8 0.0 copy-done.1
  18.8 3.3 %second.1 = (f32[32,1,1280]{2,1,0:T(1,128)}, f32[8,1024]{1,0:T(8,128)S(1)}, f32[48,128]{1,0:T(8,128)S(1)}, f32[48,128]{1,0:T(8,128)S(1)}, f32[24,128]{1,0:T(8,128)S(1)}, /*index=5*/f32[24,128]{1,0:T(8,128)S(1)}) custom-call(f32[32,8,128]{2,1,0:T(8,128)S(1)} %all-to-all-done.got_ref, f32[32,1024]{1,0:T(8,128)S(1)} %get-tuple-element.28.keep_ref, ...), custom_call_target="tpu_custom_call" | custom-call | flops 1000000 | bytes 10000000 | tf_op jit(solution)/shard_map/second/pallas_call | solution.py:657
  22.1 4.7 %all-to-all-start.1 = ((f32[32,1,1280]{2,1,0:T(1,128)}), f32[32,1,1280]{2,1,0:T(1,128)S(1)}, u32[]{:S(2)}, u32[]{:S(2)}) async-start(f32[32,1,1280]{2,1,0:T(1,128)} %get-tuple-element.43), calls=%async_computation.1 | async-start | bytes 327680 | tf_op jit(solution)/shard_map/all_to_all | solution.py:666
  26.8 0.3 collective-permute-start.2
  27.2 1.5 %collective-permute-start.3 = (f32[48,128]{1,0:T(8,128)S(1)}, f32[48,128]{1,0:T(8,128)S(1)}, u32[]{:S(2)}, u32[]{:S(2)}) collective-permute-start(f32[48,128]{1,0:T(8,128)S(1)} %get-tuple-element.51), channel_id=1, source_target_pairs={{2,4},{3,5},{6,8},{7,9},{10,12},{11,13},{14,16},{15,17},{18,20},{1... | collective-permute-start | bytes 73736 | tf_op jit(solution)/shard_map/ppermute | solution.py:572
  28.7 1.2 %collective-permute-start.4 = (f32[24,128]{1,0:T(8,128)S(1)}, f32[24,128]{1,0:T(8,128)S(1)}, u32[]{:S(2)}, u32[]{:S(2)}) collective-permute-start(f32[24,128]{1,0:T(8,128)S(1)} %get-tuple-element.48.mine_ye_ref), channel_id=1, source_target_pairs={{0,1},{2,3},{4,5},{6,7},{8,9},{10,11},{12,13},{14,15},{16,17},{18,... | collective-permute-start | bytes 36872 | tf_op jit(solution)/shard_map/ppermute | solution.py:572
  29.9 6.7 %fields.1 = (f32[3,8,8,128]{3,2,1,0:T(8,128)S(1)}, f32[8,8,8,128]{3,2,1,0:T(8,128)S(1)}, f32[8,8,8,128]{3,2,1,0:T(8,128)S(1)}) custom-call(f32[32,1024]{1,0:T(8,128)S(1)} %get-tuple-element.28.keep_ref, f32[8,1024]{1,0:T(8,128)S(1)} %get-tuple-element.44.t_ref, s32[8,64,128]{2,1,0:T(8,128)S(1)} %copy-done, f32[9,8,128]{2,1,0:T(8,128)S(1)} %get-tuple-element.30.weight_ref, ...), custom_call_target="tpu_custom_call" | custom-call | flops 1000000 | bytes 36000000 | tf_op jit(solution)/shard_map/fields/pallas_call | solution.py:672
  36.6 0.0 collective-permute-done.4.ye_ref
  36.6 0.0 collective-permute-done.2.xe_ref
  36.6 0.0 collective-permute-done.3.xo_ref
  36.6 0.0 all-to-all-done.1.got_ref
  36.6 1.5 %last.1 = (f32[8,1,1024]{2,1,0:T(1,128)}, f32[64,128]{1,0:T(8,128)}) custom-call(f32[32,1,1280]{2,1,0:T(1,128)S(1)} %all-to-all-done.1.got_ref, f32[128,128]{1,0:T(8,128)S(1)} %copy-done.1, f32[32,1024]{1,0:T(8,128)S(1)} %get-tuple-element.28.keep_ref, f32[8,1024]{1,0:T(8,128)S(1)} %get-tuple-element.44.t_ref, ...), custom_call_target="tpu_custom_call" | custom-call | flops 1000000 | bytes 4000000 | tf_op jit(solution)/shard_map/last/pallas_call | solution.py:678
  (1 shorter events, 0.0 us)
Async XLA Ops:
  0.6 13.9 %copy-start = (s32[8,64,128]{2,1,0:T(8,128)S(1)}, s32[8,64,128]{2,1,0:T(8,128)}, u32[]{:S(2)}) copy-start(s32[8,64,128]{2,1,0:T(8,128)} %dofs_ref.3) | copy-start | bytes 786436
  0.6 18.1 %copy-start.1 = (f32[128,128]{1,0:T(8,128)S(1)}, f32[128,128]{1,0:T(8,128)}, u32[]{:S(2)}) copy-start(f32[128,128]{1,0:T(8,128)} %coarse_ref.3) | copy-start | bytes 196612
  3.0 15.7 %all-to-all-start = ((f32[32,8,128]{2,1,0:T(8,128)}), f32[32,8,128]{2,1,0:T(8,128)S(1)}, u32[]{:S(2)}, u32[]{:S(2)}) async-start(f32[32,8,128]{2,1,0:T(8,128)} %get-tuple-element.27), calls=%async_computation | async-start | bytes 262144 | tf_op jit(solution)/shard_map/all_to_all | solution.py:633
  12.7 6.0 %collective-permute-start = (f32[152,128]{1,0:T(8,128)S(1)}, f32[152,128]{1,0:T(8,128)S(1)}, u32[]{:S(2)}, u32[]{:S(2)}) collective-permute-start(f32[152,128]{1,0:T(8,128)S(1)} %get-tuple-element.34.mine_e_ref), channel_id=1, source_target_pairs={{0,2},{1,3},{4,6},{5,7},{8,10},{9,11},{12,14},{13,15},{16,18},{17,... | collective-permute-start | bytes 233480 | tf_op jit(solution)/shard_map/ppermute | solution.py:572
  13.1 5.7 %collective-permute-start.1 = (f32[152,128]{1,0:T(8,128)S(1)}, f32[152,128]{1,0:T(8,128)S(1)}, u32[]{:S(2)}, u32[]{:S(2)}) collective-permute-start(f32[152,128]{1,0:T(8,128)S(1)} %get-tuple-element.35.mine_o_ref), channel_id=1, source_target_pairs={{2,4},{3,5},{6,8},{7,9},{10,12},{11,13},{14,16},{15,17},{18,20},{1... | collective-permute-start | bytes 233480 | tf_op jit(solution)/shard_map/ppermute | solution.py:572
  22.1 14.5 %all-to-all-start.1 = ((f32[32,1,1280]{2,1,0:T(1,128)}), f32[32,1,1280]{2,1,0:T(1,128)S(1)}, u32[]{:S(2)}, u32[]{:S(2)}) async-start(f32[32,1,1280]{2,1,0:T(1,128)} %get-tuple-element.43), calls=%async_computation.1 | async-start | bytes 327680 | tf_op jit(solution)/shard_map/all_to_all | solution.py:666
  26.8 9.8 %collective-permute-start.2 = (f32[48,128]{1,0:T(8,128)S(1)}, f32[48,128]{1,0:T(8,128)S(1)}, u32[]{:S(2)}, u32[]{:S(2)}) collective-permute-start(f32[48,128]{1,0:T(8,128)S(1)} %get-tuple-element.50), channel_id=1, source_target_pairs={{0,2},{1,3},{4,6},{5,7},{8,10},{9,11},{12,14},{13,15},{16,18},{17,... | collective-permute-start | bytes 73736 | tf_op jit(solution)/shard_map/ppermute | solution.py:572
  27.2 9.5 %collective-permute-start.3 = (f32[48,128]{1,0:T(8,128)S(1)}, f32[48,128]{1,0:T(8,128)S(1)}, u32[]{:S(2)}, u32[]{:S(2)}) collective-permute-start(f32[48,128]{1,0:T(8,128)S(1)} %get-tuple-element.51), channel_id=1, source_target_pairs={{2,4},{3,5},{6,8},{7,9},{10,12},{11,13},{14,16},{15,17},{18,20},{1... | collective-permute-start | bytes 73736 | tf_op jit(solution)/shard_map/ppermute | solution.py:572
  28.7 7.9 %collective-permute-start.4 = (f32[24,128]{1,0:T(8,128)S(1)}, f32[24,128]{1,0:T(8,128)S(1)}, u32[]{:S(2)}, u32[]{:S(2)}) collective-permute-start(f32[24,128]{1,0:T(8,128)S(1)} %get-tuple-element.48.mine_ye_ref), channel_id=1, source_target_pairs={{0,1},{2,3},{4,5},{6,7},{8,9},{10,11},{12,13},{14,15},{16,17},{18,... | collective-permute-start | bytes 36872 | tf_op jit(solution)/shard_map/ppermute | solution.py:572
